TPU v7x, 32 devices: a whole 2x2x4 slice. The times are simulated.
32 devices in a mesh: seq: 8 (over z, x), head: 4 (over y, core).
Axes of the slice: x: 2, y: 2, z: 4, core: 2. Of those that a mesh axis runs over, the one named last changes fastest.
Arguments:
- queries: bfloat16 [2048, 4096], P('seq', 'head'), may hold values from -100 to 100
- keys_values: bfloat16 [2048, 2, 512], P('seq', None, 'head'), may hold values from -4.5 to 4.5
- cache_kv: bfloat16 [2048, 2, 512], P('seq', None, 'head'), may hold values from -4 to 4
- vertical_pages: int32 [4, 4], P('head'), may hold values from 0 to 15, as said below
- slash_shift: int32 [4, 3], P('head'), may hold values from 1 to 8, as said below
- slash_live: int32 [8, 4, 3], P('seq', 'head'), may hold values 0 or 1
- out_proj: bfloat16 [4096, 2048], P('head'), may hold values from -0.09375 to 0.09375
Outputs:
- projected: bfloat16 [2048, 2048], P('seq', 'head')
Inputs may be any that keep to these rules, and one draw needn't show every extreme that they name: `vertical_pages`: each head group lists 4 distinct pages. `slash_shift`: each head group lists 3 distinct distances.
All inputs are finite; a program needn't handle non-finite values. No bound on the sum of `slash_live` on one device may be relied on, other than what follows from the above.
Results may differ from a plain program's by a relative error of at most 0.0057.
Values may be sent and summed in bfloat16 or wider, within the bound.
No kernel may reach another device: no remote copies, remote signals or barrier semaphores. Data moves between devices by JAX's collectives and lax.ppermute only.
A program may use at most 64 MiB of HBM per device.

v0:
```python
import functools
import math

import jax
import jax.numpy as jnp
from jax import lax
from jax.experimental import pallas as pl
from jax.experimental.pallas import tpu as pltpu
from jax.sharding import PartitionSpec as P


PAGE = 128
LANES = 128
FAR = 1e30
TREE_MAX = 16


def swapped(value, axis, mask):
    count = lax.axis_size(axis)
    return lax.ppermute(value, axis, [(source, source ^ mask) for source in range(count)])


def passed_along(value, axis, steps):
    count = lax.axis_size(axis)
    return lax.ppermute(value, axis, [(source, (source + steps) % count) for source in range(count)])


def gathered(first_hops, axis, count):
    blocks = {}
    for mask in range(1, count):
        low = mask & -mask
        source = blocks[mask - low] if mask > low else first_hops[low]
        blocks[mask] = swapped(source, axis, low)
    return [blocks[mask] for mask in range(1, count)]


def rotate(value, amount, shards):
    reduced = amount % shards
    for bit_number in range(max(1, (shards - 1).bit_length())):
        moved = passed_along(value, "seq", 1 << bit_number)
        value = jnp.where(reduced // (1 << bit_number) % 2 == 1, moved, value)
    return value


def decoded(sizes, table, me):
    shards, per_shard = sizes["shards"], sizes["per_shard"]
    slash_count, page_count = sizes["slash_count"], sizes["page_count"]
    slashes, pages = [], []
    for k in range(slash_count):
        distance = table[0, page_count + k]
        older = distance > me
        source = jnp.where(older, shards + me - distance, me - distance)
        slashes.append((source ^ me, older, table[0, page_count + slash_count + k] == 1))
    for i in range(page_count):
        owner = table[0, i] // per_shard
        clash = functools.reduce(
            jnp.logical_or,
            [live & older & (bits == (owner ^ me)) for bits, older, live in slashes],
        )
        pages.append((owner ^ me, table[0, i] - owner * per_shard, jnp.logical_not(clash)))
    return slashes, pages


def open_kernel(sizes, own_in, cache_in, *rest):
    shards, per_shard, piece = sizes["shards"], sizes["per_shard"], sizes["piece"]
    own_near, cache_near, sems = rest[0], rest[1], rest[-1]
    hop_count = shards.bit_length() - 1
    hops, pieces = rest[2 : 2 + hop_count], rest[2 + hop_count : -1]
    copies = [
        pltpu.make_async_copy(own_in, own_near, sems.at[0]),
        pltpu.make_async_copy(cache_in, cache_near, sems.at[1]),
    ]
    for copy in copies:
        copy.start()
    for copy in copies:
        copy.wait()
    me = lax.axis_index("seq")
    for number, hop in enumerate(hops):
        upper = (me >> number) & 1

        @pl.when(upper == 0)
        def _(hop=hop):
            hop[...] = own_near[...]

        @pl.when(upper == 1)
        def _(hop=hop):
            hop[...] = cache_near[...]

    for mask, place in enumerate(pieces):
        for at in range(per_shard):
            first = (at * len(pieces) + mask) * piece
            place[pl.ds(at * piece, piece), :] = cache_near[pl.ds(first, piece), :]


def stage_kernel(query_in, page_in, shift_in, live_in, query_near, table, *rest):
    page_near, shift_near, live_near, sems = rest
    ints = (page_near, shift_near, live_near)
    copies = [
        pltpu.make_async_copy(source, place, sems.at[at])
        for at, (source, place) in enumerate(
            [(page_in, page_near), (shift_in, shift_near), (live_in, live_near)]
            + [(query_in, query_near)]
        )
    ]
    for copy in copies:
        copy.start()
    for copy in copies[:3]:
        copy.wait()
    at = 0
    for part in ints:
        for entry in range(part.shape[1]):
            table[0, at] = part[0, entry]
            at += 1
    copies[3].wait()


def pick_kernel(sizes, table, *rest):
    pieces, slots = rest[:-1], rest[-1]
    piece = sizes["piece"]
    _, pages = decoded(sizes, table, lax.axis_index("seq"))
    for i, (bits, place, _) in enumerate(pages):
        for mask, source in enumerate(pieces):

            @pl.when((bits & (len(pieces) - 1)) == mask)
            def _(source=source):
                first = pl.multiple_of(place * piece, piece)
                slots[pl.ds(i * piece, piece), :] = source[pl.ds(first, piece), :]


def merge_kernel(sizes, table, mine, other, merged):
    piece = sizes["piece"]
    _, pages = decoded(sizes, table, lax.axis_index("seq"))
    for i, (bits, _, _) in enumerate(pages):
        here = pl.ds(i * piece, piece)
        far = bits >= sizes["shards"] // 2

        @pl.when(far)
        def _(here=here):
            merged[here, :] = other[here, :]

        @pl.when(jnp.logical_not(far))
        def _(here=here):
            merged[here, :] = mine[here, :]


def attention_kernel(sizes, table, query_ref, proj_ref, own_ref, *rest):
    shards, heads, head_width = sizes["shards"], sizes["heads"], sizes["head_width"]
    slash_count, page_count = sizes["slash_count"], sizes["page_count"]
    page_rows, members, tree = sizes["page_rows"], sizes["members"], sizes["tree"]
    piece = sizes["piece"]
    block_count = shards if tree else slash_count
    piece_count = shards // 2 if tree else page_count
    blocks = rest[:block_count]
    pieces = rest[block_count : block_count + piece_count]
    rest = rest[block_count + piece_count :]
    send_ref, keep_ref, wide, keys, values, scores, weights, attended, proj, proj_sem = rest
    proj_copy = pltpu.make_async_copy(proj_ref, proj, proj_sem)
    proj_copy.start()
    rows = query_ref.shape[0]
    slashes, pages = decoded(sizes, table, lax.axis_index("seq"))
    wide[pl.ds(0, 2 * rows), :] = own_ref[...].astype(jnp.float32)
    chunks = [(0, rows, None)]
    first = rows
    for k, (bits, _, live) in enumerate(slashes):
        here = pl.ds(2 * first, 2 * rows)
        if tree:
            for mask in range(shards):

                @pl.when(bits == mask)
                def _(mask=mask):
                    wide[here, :] = blocks[mask][...].astype(jnp.float32)
        else:
            wide[here, :] = blocks[k][...].astype(jnp.float32)
        chunks.append((first, rows, live))
        first += rows
    for i, (bits, _, is_open) in enumerate(pages):
        if tree:
            for mask in range(piece_count):
                at = pl.multiple_of(2 * first + ((mask ^ bits) & (piece_count - 1)) * piece, piece)
                wide[pl.ds(at, piece), :] = pieces[mask][pl.ds(i * piece, piece), :].astype(
                    jnp.float32
                )
        else:
            wide[pl.ds(2 * first, 2 * page_rows), :] = pieces[i][...].astype(jnp.float32)
        chunks.append((first, page_rows, is_open))
        first += page_rows
    keys[...] = wide[pl.ds(0, first, stride=2), :].astype(jnp.bfloat16)
    values[:, pl.ds(0, head_width)] = wide[pl.ds(1, first, stride=2), :].astype(jnp.bfloat16)
    values[:, pl.ds(head_width, LANES)] = jnp.ones((first, LANES), jnp.bfloat16)
    scale = head_width**-0.5 * math.log2(math.e)
    causal = lax.broadcasted_iota(jnp.int32, (rows, rows), 0) >= lax.broadcasted_iota(
        jnp.int32, (rows, rows), 1
    )

    def score(head, chunk, highest):
        start, count, flag = chunk
        part = lax.dot_general(
            query_ref[:, pl.ds(head * head_width, head_width)],
            keys[pl.ds(start, count), :],
            (((1,), (1,)), ((), ())),
            preferred_element_type=jnp.float32,
        )
        if flag is None:
            part = jnp.where(causal, part, -FAR)
        scores[head % 2, :, pl.ds(start, count)] = part
        top = functools.reduce(
            jnp.maximum, [part[:, at : at + LANES] for at in range(0, count, LANES)]
        )
        if flag is not None:
            top = jnp.where(flag, top, -FAR)
        return top if highest is None else jnp.maximum(highest, top)

    def weigh(head, chunk, highest):
        start, count, flag = chunk
        level = highest if flag is None else jnp.where(flag, highest, FAR)
        part = jnp.exp2((scores[head % 2, :, pl.ds(start, count)] - level) * scale)
        weights[head % 2, :, pl.ds(start, count)] = part.astype(jnp.bfloat16)

    running = None
    for chunk in chunks:
        running = score(0, chunk, running)
    for head in range(heads):
        highest = jnp.max(running, axis=1, keepdims=True)
        running = None
        for chunk in chunks:
            if head + 1 < heads:
                running = score(head + 1, chunk, running)
            weigh(head, chunk, highest)
        total = jnp.dot(weights[head % 2], values[...], preferred_element_type=jnp.float32)
        attended[:, pl.ds(head * head_width, head_width)] = (
            total[:, :head_width] / total[:, head_width:]
        ).astype(jnp.bfloat16)

    proj_copy.wait()
    mine = lax.axis_index("head")
    block = proj_ref.shape[1] // members
    for mask in range(members):
        column = pl.multiple_of((mine ^ mask) * block, block)
        term = jnp.dot(
            attended[...], proj[:, pl.ds(column, block)], preferred_element_type=jnp.float32
        )
        if mask % 2:
            send_ref[mask // 2] = term.astype(send_ref.dtype)
        else:
            keep_ref[mask // 2] = term


def body(queries, keys_values, cache_kv, vertical_pages, slash_shift, slash_live, out_proj):
    row_count = queries.shape[0]
    head_width = keys_values.shape[2]
    heads = queries.shape[1] // head_width
    shards = lax.axis_size("seq")
    members = lax.axis_size("head")
    slash_count = slash_shift.shape[1]
    page_count = vertical_pages.shape[1]
    per_shard = row_count // PAGE
    out_width = out_proj.shape[1]
    own = keys_values.reshape(2 * row_count, head_width)
    cache = cache_kv.reshape(2 * row_count, head_width)
    tree = is_tree(shards)
    piece = 2 * PAGE // (shards // 2) if tree else 0
    sizes = dict(
        shards=shards, heads=heads, head_width=head_width, slash_count=slash_count,
        page_count=page_count, page_rows=PAGE, per_shard=per_shard, members=members, tree=tree,
        piece=piece,
    )
    scalars = pl.BlockSpec(memory_space=pltpu.SMEM)
    vector = pl.BlockSpec(memory_space=pltpu.VMEM)
    hbm = pl.BlockSpec(memory_space=pltpu.HBM)
    far = functools.partial(pltpu.with_memory_space_constraint, memory_space=pltpu.HBM)
    lists = [vertical_pages, slash_shift, slash_live.reshape(1, slash_count)]
    table_size = sum(part.shape[1] for part in lists)
    queries, table = pl.pallas_call(
        stage_kernel,
        out_shape=[
            jax.ShapeDtypeStruct(queries.shape, queries.dtype),
            jax.ShapeDtypeStruct((1, table_size), jnp.int32),
        ],
        in_specs=[hbm] * 4,
        out_specs=[vector, scalars],
        scratch_shapes=[pltpu.SMEM(part.shape, jnp.int32) for part in lists]
        + [pltpu.SemaphoreType.DMA((4,))],
        compiler_params=pltpu.CompilerParams(vmem_limit_bytes=1 << 20),
        cost_estimate=pl.CostEstimate(flops=0, bytes_accessed=2 << 20, transcendentals=0),
        name="stage",
    )(*map(far, [queries] + lists))
    own_shard = lax.axis_index("seq")
    if tree:
        half = shards // 2
        bits = [1 << number for number in range(shards.bit_length() - 1)]
        block_shape = jax.ShapeDtypeStruct(own.shape, own.dtype)
        piece_shape = jax.ShapeDtypeStruct((per_shard * piece, head_width), own.dtype)
        opened = pl.pallas_call(
            functools.partial(open_kernel, sizes),
            out_shape=[block_shape] * (2 + len(bits)) + [piece_shape] * half,
            in_specs=[hbm] * 2,
            out_specs=[vector] * (2 + len(bits) + half),
            scratch_shapes=[pltpu.SemaphoreType.DMA((2,))],
            compiler_params=pltpu.CompilerParams(vmem_limit_bytes=1 << 20),
            cost_estimate=pl.CostEstimate(flops=0, bytes_accessed=1 << 20, transcendentals=0),
            name="open",
        )(far(own), far(cache))
        own, cache = opened[:2]
        near = opened[2 + len(bits) :]
        pieces = [near[0]] + [swapped(near[mask], "seq", mask) for mask in range(1, half)]
        first_hops = dict(zip(bits, opened[2 : 2 + len(bits)]))
        blocks = [cache] + gathered(first_hops, "seq", shards)
        slot_shape = jax.ShapeDtypeStruct((page_count * piece, head_width), jnp.bfloat16)
        small = dict(
            out_shape=slot_shape,
            out_specs=vector,
            compiler_params=pltpu.CompilerParams(vmem_limit_bytes=2 << 20),
            cost_estimate=pl.CostEstimate(flops=0, bytes_accessed=4 << 20, transcendentals=0),
        )
        mine = pl.pallas_call(
            functools.partial(pick_kernel, sizes),
            in_specs=[scalars] + [vector] * len(pieces),
            name="pick",
            **small,
        )(table, *pieces)
        merged = pl.pallas_call(
            functools.partial(merge_kernel, sizes),
            in_specs=[scalars, vector, vector],
            name="merge",
            **small,
        )(table, mine, swapped(mine, "seq", half))
        pieces = [merged] + gathered(dict.fromkeys(bits, merged), "seq", half)
    else:
        blocks, pieces = [], []
        for k in range(slash_count):
            distance = slash_shift[0, k]
            payload = jnp.where(own_shard < shards - distance, keys_values, cache_kv)
            blocks.append(rotate(payload, distance, shards).reshape(2 * row_count, head_width))
        whole = lax.all_gather(cache_kv, "seq", axis=0, tiled=True)
        for i in range(page_count):
            page = lax.dynamic_slice_in_dim(whole, vertical_pages[0, i] * PAGE, PAGE, 0)
            pieces.append(page.reshape(2 * PAGE, head_width))
    key_count = (1 + slash_count) * row_count + page_count * PAGE
    block = out_width // members
    send, keep = pl.pallas_call(
        functools.partial(attention_kernel, sizes),
        out_shape=[
            jax.ShapeDtypeStruct((members // 2, row_count, block), jnp.bfloat16),
            jax.ShapeDtypeStruct((members // 2, row_count, block), jnp.float32),
        ],
        in_specs=[scalars, vector, hbm] + [vector] * (1 + len(blocks) + len(pieces)),
        out_specs=[vector, vector],
        scratch_shapes=[
            pltpu.VMEM((2 * key_count, head_width), jnp.float32),
            pltpu.VMEM((key_count, head_width), jnp.bfloat16),
            pltpu.VMEM((key_count, head_width + LANES), jnp.bfloat16),
            pltpu.VMEM((2, row_count, key_count), jnp.float32),
            pltpu.VMEM((2, row_count, key_count), jnp.bfloat16),
            pltpu.VMEM((row_count, heads * head_width), jnp.bfloat16),
            pltpu.VMEM(out_proj.shape, out_proj.dtype),
            pltpu.SemaphoreType.DMA,
        ],
        compiler_params=pltpu.CompilerParams(vmem_limit_bytes=32 << 20),
        cost_estimate=pl.CostEstimate(
            flops=4 * heads * row_count * key_count * head_width
            + 2 * row_count * heads * head_width * out_width,
            bytes_accessed=8 << 20,
            transcendentals=heads * row_count * key_count,
        ),
        name="attend",
    )(table, queries, far(out_proj), own, *blocks, *pieces)
    step = 1
    while step < members:
        keep = keep + swapped(send, "head", step).astype(jnp.float32)
        step *= 2
        if step < members:
            send = keep[1::2].astype(jnp.bfloat16)
            keep = keep[0::2]
    return keep[0].astype(jnp.bfloat16)


def is_tree(shards):
    return 4 <= shards <= TREE_MAX and shards & (shards - 1) == 0


def solution(mesh):
    placed = (
        P("seq", "head"),
        P("seq", None, "head"),
        P("seq", None, "head"),
        P("head", None),
        P("head", None),
        P("seq", "head", None),
        P("head", None),
    )


    step = jax.shard_map(
        body, mesh=mesh, in_specs=placed, out_specs=P("seq", "head"), check_vma=False
    )
    if not is_tree(mesh.shape["seq"]):
        return step
    return step
```

profile of v0, /device:TPU:0, one launch (start us, length us, event | category | flops | bytes accessed | tf_op | source)
XLA Modules:
  0.0 57.7 jit_solution(5258324623060165462)
XLA Ops:
  0.0 1.0 %open.1 = (bf16[512,128]{1,0:T(8,128)(2,1)S(1)}, bf16[512,128]{1,0:T(8,128)(2,1)S(1)}, bf16[512,128]{1,0:T(8,128)(2,1)S(1)}, bf16[512,128]{1,0:T(8,128)(2,1)S(1)...) custom-call(bf16[512,128]{1,0:T(8,128)(2,1)} %bitcast.5, ...), custom_call_target="tpu_custom_call" | custom-call | bytes 1048576 | tf_op jit(solution)/shard_map/open/pallas_call | solution.py:293
  1.0 4.1 %collective-permute-start.3 = (bf16[512,128]{1,0:T(8,128)(2,1)S(1)}, bf16[512,128]{1,0:T(8,128)(2,1)S(1)}, u32[]{:S(2)}, u32[]{:S(2)}) collective-permute-start(bf16[512,128]{1,0:T(8,128)(2,1)S(1)} %get-tuple-element.24), channel_id=1, source_target_pairs={{0,16},{4,20},{8,24},{12,28},{16,0},{20,4},{24,8},{28,12},{1,17},{... | collective-permute-start | bytes 393224 | tf_op jit(solution)/shard_map/ppermute | solution.py:20
  5.2 1.6 %collective-permute-start.1 = (bf16[512,128]{1,0:T(8,128)(2,1)S(1)}, bf16[512,128]{1,0:T(8,128)(2,1)S(1)}, u32[]{:S(2)}, u32[]{:S(2)}) collective-permute-start(bf16[512,128]{1,0:T(8,128)(2,1)S(1)} %get-tuple-element.23), channel_id=1, source_target_pairs={{0,8},{4,12},{8,0},{12,4},{16,24},{20,28},{24,16},{28,20},{1,9},{5... | collective-permute-start | bytes 393224 | tf_op jit(solution)/shard_map/ppermute | solution.py:20
  6.7 4.8 %collective-permute-done.3.rest_4_ = bf16[512,128]{1,0:T(8,128)(2,1)S(1)} collective-permute-done((bf16[512,128]{1,0:T(8,128)(2,1)S(1)}, bf16[512,128]{1,0:T(8,128)(2,1)S(1)}, u32[]{:S(2)}, u32[]{:S(2)}) %collective-permute-start.3) | collective-permute-done | bytes 131104 | tf_op jit(solution)/shard_map/ppermute | solution.py:20
  11.6 0.6 %collective-permute-start.5 = (bf16[512,128]{1,0:T(8,128)(2,1)S(1)}, bf16[512,128]{1,0:T(8,128)(2,1)S(1)}, u32[]{:S(2)}, u32[]{:S(2)}) collective-permute-start(bf16[512,128]{1,0:T(8,128)(2,1)S(1)} %collective-permute-done.3.rest_4_), channel_id=1, source_target_pairs={{0,8},{4,12},{8,0},{12,4},{16,24},{20,28},{24,16},{28,20},{1,9},{5... | collective-permute-start | bytes 393224 | tf_op jit(solution)/shard_map/ppermute | solution.py:20
  12.2 1.5 %collective-permute-start.7 = (bf16[128,128]{1,0:T(8,128)(2,1)S(1)}, bf16[128,128]{1,0:T(8,128)(2,1)S(1)}, u32[]{:S(2)}, u32[]{:S(2)}) collective-permute-start(bf16[128,128]{1,0:T(8,128)(2,1)S(1)} %get-tuple-element.26), channel_id=1, source_target_pairs={{0,4},{4,0},{8,12},{12,8},{16,20},{20,16},{24,28},{28,24},{1,5},{5... | collective-permute-start | bytes 98312 | tf_op jit(solution)/shard_map/ppermute | solution.py:20
  13.7 1.5 %collective-permute-start.8 = (bf16[128,128]{1,0:T(8,128)(2,1)S(1)}, bf16[128,128]{1,0:T(8,128)(2,1)S(1)}, u32[]{:S(2)}, u32[]{:S(2)}) collective-permute-start(bf16[128,128]{1,0:T(8,128)(2,1)S(1)} %get-tuple-element.27), channel_id=1, source_target_pairs={{0,8},{4,12},{8,0},{12,4},{16,24},{20,28},{24,16},{28,20},{1,9},{5... | collective-permute-start | bytes 98312 | tf_op jit(solution)/shard_map/ppermute | solution.py:20
  15.1 0.5 collective-permute-start.9
  15.7 1.7 %stage.1 = (bf16[256,1024]{1,0:T(8,128)(2,1)S(1)}, s32[1,10]{1,0:T(1,128)S(1)}) custom-call(bf16[256,1024]{1,0:T(8,128)(2,1)} %query_in.1, s32[1,4]{1,0:T(1,128)} %page_in.1, s32[1,3]{1,0:T(1,128)} %shift_in.1, s32[1,3]{1,0:T(1,128)} %bitcast.7), custom_call_target="tpu_custom_call" | custom-call | bytes 2097152 | tf_op jit(solution)/shard_map/stage/pallas_call | solution.py:273
  17.4 0.0 collective-permute-done.7.rest_1_
  17.4 0.2 collective-permute-done.8.rest_2_
  17.6 2.4 %collective-permute-done.9.rest_3_ = bf16[128,128]{1,0:T(8,128)(2,1)S(1)} collective-permute-done((bf16[128,128]{1,0:T(8,128)(2,1)S(1)}, bf16[128,128]{1,0:T(8,128)(2,1)S(1)}, u32[]{:S(2)}, u32[]{:S(2)}) %collective-permute-start.9) | collective-permute-done | bytes 32800 | tf_op jit(solution)/shard_map/ppermute | solution.py:20
  20.0 0.7 %pick.1.mine = bf16[256,128]{1,0:T(8,128)(2,1)S(1)} custom-call(s32[1,10]{1,0:T(1,128)S(1)} %get-tuple-element.18.table, bf16[128,128]{1,0:T(8,128)(2,1)S(1)} %get-tuple-element.25.rest_0_, bf16[128,128]{1,0:T(8,128)(2,1)S(1)} %collective-permute-done.7.rest_1_, bf16[128,128]{1,0:T(8,128)(2,1)S(1)} %collective-permute-done.8.rest_2_, ...), custom_call_target="tpu_custom_call" | custom-call | bytes 4194304 | tf_op jit(solution)/shard_map/pick/pallas_call | solution.py:315
  20.6 2.0 %collective-permute-start.10 = (bf16[256,128]{1,0:T(8,128)(2,1)S(1)}, bf16[256,128]{1,0:T(8,128)(2,1)S(1)}, u32[]{:S(2)}, u32[]{:S(2)}) collective-permute-start(bf16[256,128]{1,0:T(8,128)(2,1)S(1)} %pick.1.mine), channel_id=1, source_target_pairs={{0,16},{4,20},{8,24},{12,28},{16,0},{20,4},{24,8},{28,12},{1,17},{... | collective-permute-start | bytes 196616 | tf_op jit(solution)/shard_map/ppermute | solution.py:20
  22.6 0.9 %collective-permute-start = (bf16[512,128]{1,0:T(8,128)(2,1)S(1)}, bf16[512,128]{1,0:T(8,128)(2,1)S(1)}, u32[]{:S(2)}, u32[]{:S(2)}) collective-permute-start(bf16[512,128]{1,0:T(8,128)(2,1)S(1)} %get-tuple-element.22), channel_id=1, source_target_pairs={{0,4},{4,0},{8,12},{12,8},{16,20},{20,16},{24,28},{28,24},{1,5},{5... | collective-permute-start | bytes 393224 | tf_op jit(solution)/shard_map/ppermute | solution.py:20
  23.5 3.1 %collective-permute-done.10.other = bf16[256,128]{1,0:T(8,128)(2,1)S(1)} collective-permute-done((bf16[256,128]{1,0:T(8,128)(2,1)S(1)}, bf16[256,128]{1,0:T(8,128)(2,1)S(1)}, u32[]{:S(2)}, u32[]{:S(2)}) %collective-permute-start.10) | collective-permute-done | bytes 65568 | tf_op jit(solution)/shard_map/ppermute | solution.py:20
  26.6 0.6 %merge.1.rest_8_ = bf16[256,128]{1,0:T(8,128)(2,1)S(1)} custom-call(s32[1,10]{1,0:T(1,128)S(1)} %get-tuple-element.18.table, bf16[256,128]{1,0:T(8,128)(2,1)S(1)} %pick.1.mine, bf16[256,128]{1,0:T(8,128)(2,1)S(1)} %collective-permute-done.10.other), custom_call_target="tpu_custom_call" | custom-call | bytes 4194304 | tf_op jit(solution)/shard_map/merge/pallas_call | solution.py:321
  27.3 0.4 collective-permute-start.12
  27.6 0.5 collective-permute-start.4
  28.2 0.0 collective-permute-done.1.rest_2_
  28.2 1.5 %collective-permute-start.2 = (bf16[512,128]{1,0:T(8,128)(2,1)S(1)}, bf16[512,128]{1,0:T(8,128)(2,1)S(1)}, u32[]{:S(2)}, u32[]{:S(2)}) collective-permute-start(bf16[512,128]{1,0:T(8,128)(2,1)S(1)} %collective-permute-done.1.rest_2_), channel_id=1, source_target_pairs={{0,4},{4,0},{8,12},{12,8},{16,20},{20,16},{24,28},{28,24},{1,5},{5... | collective-permute-start | bytes 393224 | tf_op jit(solution)/shard_map/ppermute | solution.py:20
  29.7 0.0 collective-permute-done.5.rest_6_
  29.7 0.5 collective-permute-start.6
  30.2 0.0 collective-permute-done.rest_1_
  30.2 1.5 %collective-permute-start.11 = (bf16[256,128]{1,0:T(8,128)(2,1)S(1)}, bf16[256,128]{1,0:T(8,128)(2,1)S(1)}, u32[]{:S(2)}, u32[]{:S(2)}) collective-permute-start(bf16[256,128]{1,0:T(8,128)(2,1)S(1)} %merge.1.rest_8_), channel_id=1, source_target_pairs={{0,4},{4,0},{8,12},{12,8},{16,20},{20,16},{24,28},{28,24},{1,5},{5... | collective-permute-start | bytes 196616 | tf_op jit(solution)/shard_map/ppermute | solution.py:20
  31.7 0.0 collective-permute-done.12.rest_10_
  31.7 0.5 collective-permute-start.13
  32.2 5.9 %collective-permute-done.11.rest_9_ = bf16[256,128]{1,0:T(8,128)(2,1)S(1)} collective-permute-done((bf16[256,128]{1,0:T(8,128)(2,1)S(1)}, bf16[256,128]{1,0:T(8,128)(2,1)S(1)}, u32[]{:S(2)}, u32[]{:S(2)}) %collective-permute-start.11) | collective-permute-done | bytes 65568 | tf_op jit(solution)/shard_map/ppermute | solution.py:20
  38.1 0.7 %collective-permute-done.13.rest_11_ = bf16[256,128]{1,0:T(8,128)(2,1)S(1)} collective-permute-done((bf16[256,128]{1,0:T(8,128)(2,1)S(1)}, bf16[256,128]{1,0:T(8,128)(2,1)S(1)}, u32[]{:S(2)}, u32[]{:S(2)}) %collective-permute-start.13) | collective-permute-done | bytes 65568 | tf_op jit(solution)/shard_map/ppermute | solution.py:20
  38.8 0.0 collective-permute-done.2.rest_3_
  38.8 0.0 collective-permute-done.4.rest_5_
  38.8 0.0 collective-permute-done.6.rest_7_
  38.8 7.5 %attend.1 = (bf16[2,256,512]{2,1,0:T(8,128)(2,1)S(1)}, f32[2,256,512]{2,1,0:T(8,128)S(1)}) custom-call(s32[1,10]{1,0:T(1,128)S(1)} %get-tuple-element.18.table, bf16[256,1024]{1,0:T(8,128)(2,1)S(1)} %get-tuple-element.19.query_ref, bf16[1024,2048]{1,0:T(8,128)(2,1)} %proj_ref.1, bf16[512,128]{1,0:T(8,128)(2,1)S(1)} %get-tuple-element.20.own_ref, ...), custom_call_target="tpu_custom_call" | custom-call | flops 2684354560 | bytes 8388608 | tf_op jit(solution)/shard_map/attend/pallas_call | solution.py:340
  46.3 0.1 collective-permute-start.14
  46.4 1.9 %collective-permute-done.14 = bf16[2,256,512]{2,1,0:T(8,128)(2,1)S(1)} collective-permute-done((bf16[2,256,512]{2,1,0:T(8,128)(2,1)S(1)}, bf16[2,256,512]{2,1,0:T(8,128)(2,1)S(1)}, u32[]{:S(2)}, u32[]{:S(2)}) %collective-permute-start.14) | collective-permute-done | bytes 524320 | tf_op jit(solution)/shard_map/ppermute | solution.py:20
  48.3 0.2 convert_add_fusion
  48.5 1.6 %collective-permute-start.15 = (bf16[1,256,512]{2,1,0:T(8,128)(2,1)S(1)}, bf16[1,256,512]{2,1,0:T(8,128)(2,1)S(1)}, u32[]{:S(2)}, u32[]{:S(2)}) collective-permute-start(bf16[1,256,512]{2,1,0:T(8,128)(2,1)S(1)} %slice.19), channel_id=1, source_target_pairs={{0,2},{1,3},{2,0},{3,1},{4,6},{5,7},{6,4},{7,5},{8,10},{9,11},{10,... | collective-permute-start | bytes 786440 | tf_op jit(solution)/shard_map/ppermute | solution.py:20
  50.1 6.8 %collective-permute-done.15 = bf16[1,256,512]{2,1,0:T(8,128)(2,1)S(1)} collective-permute-done((bf16[1,256,512]{2,1,0:T(8,128)(2,1)S(1)}, bf16[1,256,512]{2,1,0:T(8,128)(2,1)S(1)}, u32[]{:S(2)}, u32[]{:S(2)}) %collective-permute-start.15) | collective-permute-done | bytes 262176 | tf_op jit(solution)/shard_map/ppermute | solution.py:20
  56.9 0.8 %fusion.1 = bf16[256,512]{1,0:T(8,128)(2,1)} fusion(bf16[1,256,512]{2,1,0:T(8,128)(2,1)S(1)} %collective-permute-done.15, f32[2,256,512]{2,1,0:T(8,128)S(1)} %convert_add_fusion), kind=kLoop, calls=%fused_computation.4 | loop fusion | flops 393216 | bytes 1048576 | tf_op jit(solution)/shard_map/convert_element_type | solution.py:374
  (1 shorter events, 0.0 us)
Async XLA Ops:
  1.0 10.5 %collective-permute-start.3 = (bf16[512,128]{1,0:T(8,128)(2,1)S(1)}, bf16[512,128]{1,0:T(8,128)(2,1)S(1)}, u32[]{:S(2)}, u32[]{:S(2)}) collective-permute-start(bf16[512,128]{1,0:T(8,128)(2,1)S(1)} %get-tuple-element.24), channel_id=1, source_target_pairs={{0,16},{4,20},{8,24},{12,28},{16,0},{20,4},{24,8},{28,12},{1,17},{... | collective-permute-start | bytes 393224 | tf_op jit(solution)/shard_map/ppermute | solution.py:20
  5.2 23.0 %collective-permute-start.1 = (bf16[512,128]{1,0:T(8,128)(2,1)S(1)}, bf16[512,128]{1,0:T(8,128)(2,1)S(1)}, u32[]{:S(2)}, u32[]{:S(2)}) collective-permute-start(bf16[512,128]{1,0:T(8,128)(2,1)S(1)} %get-tuple-element.23), channel_id=1, source_target_pairs={{0,8},{4,12},{8,0},{12,4},{16,24},{20,28},{24,16},{28,20},{1,9},{5... | collective-permute-start | bytes 393224 | tf_op jit(solution)/shard_map/ppermute | solution.py:20
  11.6 18.1 %collective-permute-start.5 = (bf16[512,128]{1,0:T(8,128)(2,1)S(1)}, bf16[512,128]{1,0:T(8,128)(2,1)S(1)}, u32[]{:S(2)}, u32[]{:S(2)}) collective-permute-start(bf16[512,128]{1,0:T(8,128)(2,1)S(1)} %collective-permute-done.3.rest_4_), channel_id=1, source_target_pairs={{0,8},{4,12},{8,0},{12,4},{16,24},{20,28},{24,16},{28,20},{1,9},{5... | collective-permute-start | bytes 393224 | tf_op jit(solution)/shard_map/ppermute | solution.py:20
  12.2 5.2 %collective-permute-start.7 = (bf16[128,128]{1,0:T(8,128)(2,1)S(1)}, bf16[128,128]{1,0:T(8,128)(2,1)S(1)}, u32[]{:S(2)}, u32[]{:S(2)}) collective-permute-start(bf16[128,128]{1,0:T(8,128)(2,1)S(1)} %get-tuple-element.26), channel_id=1, source_target_pairs={{0,4},{4,0},{8,12},{12,8},{16,20},{20,16},{24,28},{28,24},{1,5},{5... | collective-permute-start | bytes 98312 | tf_op jit(solution)/shard_map/ppermute | solution.py:20
  13.7 3.9 %collective-permute-start.8 = (bf16[128,128]{1,0:T(8,128)(2,1)S(1)}, bf16[128,128]{1,0:T(8,128)(2,1)S(1)}, u32[]{:S(2)}, u32[]{:S(2)}) collective-permute-start(bf16[128,128]{1,0:T(8,128)(2,1)S(1)} %get-tuple-element.27), channel_id=1, source_target_pairs={{0,8},{4,12},{8,0},{12,4},{16,24},{20,28},{24,16},{28,20},{1,9},{5... | collective-permute-start | bytes 98312 | tf_op jit(solution)/shard_map/ppermute | solution.py:20
  15.1 4.8 %collective-permute-start.9 = (bf16[128,128]{1,0:T(8,128)(2,1)S(1)}, bf16[128,128]{1,0:T(8,128)(2,1)S(1)}, u32[]{:S(2)}, u32[]{:S(2)}) collective-permute-start(bf16[128,128]{1,0:T(8,128)(2,1)S(1)} %get-tuple-element.28), channel_id=1, source_target_pairs={{0,12},{4,8},{8,4},{12,0},{16,28},{20,24},{24,20},{28,16},{1,13},{... | collective-permute-start | bytes 98312 | tf_op jit(solution)/shard_map/ppermute | solution.py:20
  20.6 6.0 %collective-permute-start.10 = (bf16[256,128]{1,0:T(8,128)(2,1)S(1)}, bf16[256,128]{1,0:T(8,128)(2,1)S(1)}, u32[]{:S(2)}, u32[]{:S(2)}) collective-permute-start(bf16[256,128]{1,0:T(8,128)(2,1)S(1)} %pick.1.mine), channel_id=1, source_target_pairs={{0,16},{4,20},{8,24},{12,28},{16,0},{20,4},{24,8},{28,12},{1,17},{... | collective-permute-start | bytes 196616 | tf_op jit(solution)/shard_map/ppermute | solution.py:20
  22.6 7.6 %collective-permute-start = (bf16[512,128]{1,0:T(8,128)(2,1)S(1)}, bf16[512,128]{1,0:T(8,128)(2,1)S(1)}, u32[]{:S(2)}, u32[]{:S(2)}) collective-permute-start(bf16[512,128]{1,0:T(8,128)(2,1)S(1)} %get-tuple-element.22), channel_id=1, source_target_pairs={{0,4},{4,0},{8,12},{12,8},{16,20},{20,16},{24,28},{28,24},{1,5},{5... | collective-permute-start | bytes 393224 | tf_op jit(solution)/shard_map/ppermute | solution.py:20
  27.3 4.5 %collective-permute-start.12 = (bf16[256,128]{1,0:T(8,128)(2,1)S(1)}, bf16[256,128]{1,0:T(8,128)(2,1)S(1)}, u32[]{:S(2)}, u32[]{:S(2)}) collective-permute-start(bf16[256,128]{1,0:T(8,128)(2,1)S(1)} %merge.1.rest_8_), channel_id=1, source_target_pairs={{0,8},{4,12},{8,0},{12,4},{16,24},{20,28},{24,16},{28,20},{1,9},{5... | collective-permute-start | bytes 196616 | tf_op jit(solution)/shard_map/ppermute | solution.py:20
  27.6 11.2 %collective-permute-start.4 = (bf16[512,128]{1,0:T(8,128)(2,1)S(1)}, bf16[512,128]{1,0:T(8,128)(2,1)S(1)}, u32[]{:S(2)}, u32[]{:S(2)}) collective-permute-start(bf16[512,128]{1,0:T(8,128)(2,1)S(1)} %collective-permute-done.3.rest_4_), channel_id=1, source_target_pairs={{0,4},{4,0},{8,12},{12,8},{16,20},{20,16},{24,28},{28,24},{1,5},{5... | collective-permute-start | bytes 393224 | tf_op jit(solution)/shard_map/ppermute | solution.py:20
  28.2 10.6 %collective-permute-start.2 = (bf16[512,128]{1,0:T(8,128)(2,1)S(1)}, bf16[512,128]{1,0:T(8,128)(2,1)S(1)}, u32[]{:S(2)}, u32[]{:S(2)}) collective-permute-start(bf16[512,128]{1,0:T(8,128)(2,1)S(1)} %collective-permute-done.1.rest_2_), channel_id=1, source_target_pairs={{0,4},{4,0},{8,12},{12,8},{16,20},{20,16},{24,28},{28,24},{1,5},{5... | collective-permute-start | bytes 393224 | tf_op jit(solution)/shard_map/ppermute | solution.py:20
  29.7 9.1 %collective-permute-start.6 = (bf16[512,128]{1,0:T(8,128)(2,1)S(1)}, bf16[512,128]{1,0:T(8,128)(2,1)S(1)}, u32[]{:S(2)}, u32[]{:S(2)}) collective-permute-start(bf16[512,128]{1,0:T(8,128)(2,1)S(1)} %collective-permute-done.5.rest_6_), channel_id=1, source_target_pairs={{0,4},{4,0},{8,12},{12,8},{16,20},{20,16},{24,28},{28,24},{1,5},{5... | collective-permute-start | bytes 393224 | tf_op jit(solution)/shard_map/ppermute | solution.py:20
  30.2 7.9 %collective-permute-start.11 = (bf16[256,128]{1,0:T(8,128)(2,1)S(1)}, bf16[256,128]{1,0:T(8,128)(2,1)S(1)}, u32[]{:S(2)}, u32[]{:S(2)}) collective-permute-start(bf16[256,128]{1,0:T(8,128)(2,1)S(1)} %merge.1.rest_8_), channel_id=1, source_target_pairs={{0,4},{4,0},{8,12},{12,8},{16,20},{20,16},{24,28},{28,24},{1,5},{5... | collective-permute-start | bytes 196616 | tf_op jit(solution)/shard_map/ppermute | solution.py:20
  31.7 7.1 %collective-permute-start.13 = (bf16[256,128]{1,0:T(8,128)(2,1)S(1)}, bf16[256,128]{1,0:T(8,128)(2,1)S(1)}, u32[]{:S(2)}, u32[]{:S(2)}) collective-permute-start(bf16[256,128]{1,0:T(8,128)(2,1)S(1)} %collective-permute-done.12.rest_10_), channel_id=1, source_target_pairs={{0,4},{4,0},{8,12},{12,8},{16,20},{20,16},{24,28},{28,24},{1,5},{5... | collective-permute-start | bytes 196616 | tf_op jit(solution)/shard_map/ppermute | solution.py:20
  46.3 2.0 %collective-permute-start.14 = (bf16[2,256,512]{2,1,0:T(8,128)(2,1)S(1)}, bf16[2,256,512]{2,1,0:T(8,128)(2,1)S(1)}, u32[]{:S(2)}, u32[]{:S(2)}) collective-permute-start(bf16[2,256,512]{2,1,0:T(8,128)(2,1)S(1)} %get-tuple-element.30), channel_id=1, source_target_pairs={{0,1},{1,0},{2,3},{3,2},{4,5},{5,4},{6,7},{7,6},{8,9},{9,8},{10,11... | collective-permute-start | bytes 1572872 | tf_op jit(solution)/shard_map/ppermute | solution.py:20
  48.5 8.4 %collective-permute-start.15 = (bf16[1,256,512]{2,1,0:T(8,128)(2,1)S(1)}, bf16[1,256,512]{2,1,0:T(8,128)(2,1)S(1)}, u32[]{:S(2)}, u32[]{:S(2)}) collective-permute-start(bf16[1,256,512]{2,1,0:T(8,128)(2,1)S(1)} %slice.19), channel_id=1, source_target_pairs={{0,2},{1,3},{2,0},{3,1},{4,6},{5,7},{6,4},{7,5},{8,10},{9,11},{10,... | collective-permute-start | bytes 786440 | tf_op jit(solution)/shard_map/ppermute | solution.py:20
where the time goes:
time: 57.9 us; the launch traced here: 57.7 us
  waiting for transfers between devices  25.9 us (45%)
  starting transfers between devices  19.4 us (34%)
  Pallas kernels  11.4 us (20%)
  other arithmetic  0.95 us (2%)
    ppermute x16, waiting for transfers between devices, swapped(): lax.ppermute(value, axis, [(source, source ^ mask) for source in range(co...  25.9 us
    ppermute x16, starting transfers between devices, swapped(): lax.ppermute(value, axis, [(source, source ^ mask) for source in range(co...  19.4 us
    pallas_call x1, Pallas kernels, body(): pl.pallas_call(functools.partial(attention_kernel, sizes), out_shape=[jax...  7.5 us
    pallas_call x1, Pallas kernels, body(): pl.pallas_call(stage_kernel, out_shape=[jax.ShapeDtypeStruct(queries.shap...  1.67 us
  transfers between devices with their start and end apart: 16, of which 8 were waited for; matrix products, arithmetic and copies ran while one was open for 0% of the time, Pallas kernels for 5%

commit v1 on v0

--- a/solution.py
+++ b/solution.py
@@ -25,12 +25,12 @@
     return lax.ppermute(value, axis, [(source, (source + steps) % count) for source in range(count)])
 
 
-def gathered(first_hops, axis, count):
+def gathered(first_hops, axis, count, high_first):
     blocks = {}
     for mask in range(1, count):
-        low = mask & -mask
-        source = blocks[mask - low] if mask > low else first_hops[low]
-        blocks[mask] = swapped(source, axis, low)
+        last = mask & -mask if high_first else 1 << (mask.bit_length() - 1)
+        source = blocks[mask - last] if mask > last else first_hops[last]
+        blocks[mask] = swapped(source, axis, last)
     return [blocks[mask] for mask in range(1, count)]
 
 
@@ -61,19 +61,43 @@
     return slashes, pages
 
 
-def open_kernel(sizes, own_in, cache_in, *rest):
-    shards, per_shard, piece = sizes["shards"], sizes["per_shard"], sizes["piece"]
-    own_near, cache_near, sems = rest[0], rest[1], rest[-1]
-    hop_count = shards.bit_length() - 1
-    hops, pieces = rest[2 : 2 + hop_count], rest[2 + hop_count : -1]
+def fill_table(table, lists):
+    at = 0
+    for part in lists:
+        for entry in range(part.shape[1]):
+            table[0, at] = part[0, entry]
+            at += 1
+
+
+def table_kernel(page_in, shift_in, live_in, table, *rest):
+    lists, sems = rest[:3], rest[3]
     copies = [
-        pltpu.make_async_copy(own_in, own_near, sems.at[0]),
-        pltpu.make_async_copy(cache_in, cache_near, sems.at[1]),
+        pltpu.make_async_copy(source, place, sems.at[at])
+        for at, (source, place) in enumerate(zip((page_in, shift_in, live_in), lists))
     ]
     for copy in copies:
         copy.start()
     for copy in copies:
         copy.wait()
+    fill_table(table, lists)
+
+
+def open_kernel(sizes, own_in, cache_in, page_in, shift_in, live_in, *rest):
+    shards, per_shard, piece = sizes["shards"], sizes["per_shard"], sizes["piece"]
+    own_near, cache_near, table = rest[:3]
+    lists, sems = rest[-4:-1], rest[-1]
+    hop_count = shards.bit_length() - 1
+    hops, pieces = rest[3 : 3 + hop_count], rest[3 + hop_count : -4]
+    sources = (own_in, cache_in, page_in, shift_in, live_in)
+    copies = [
+        pltpu.make_async_copy(source, place, sems.at[at])
+        for at, (source, place) in enumerate(zip(sources, (own_near, cache_near) + tuple(lists)))
+    ]
+    for copy in copies:
+        copy.start()
+    for copy in copies:
+        copy.wait()
+    fill_table(table, lists)
     me = lax.axis_index("seq")
     for number, hop in enumerate(hops):
         upper = (me >> number) & 1
@@ -92,26 +116,10 @@
             place[pl.ds(at * piece, piece), :] = cache_near[pl.ds(first, piece), :]
 
 
-def stage_kernel(query_in, page_in, shift_in, live_in, query_near, table, *rest):
-    page_near, shift_near, live_near, sems = rest
-    ints = (page_near, shift_near, live_near)
-    copies = [
-        pltpu.make_async_copy(source, place, sems.at[at])
-        for at, (source, place) in enumerate(
-            [(page_in, page_near), (shift_in, shift_near), (live_in, live_near)]
-            + [(query_in, query_near)]
-        )
-    ]
-    for copy in copies:
-        copy.start()
-    for copy in copies[:3]:
-        copy.wait()
-    at = 0
-    for part in ints:
-        for entry in range(part.shape[1]):
-            table[0, at] = part[0, entry]
-            at += 1
-    copies[3].wait()
+def stage_kernel(query_in, query_near, sem):
+    copy = pltpu.make_async_copy(query_in, query_near, sem)
+    copy.start()
+    copy.wait()
 
 
 def pick_kernel(sizes, table, *rest):
@@ -270,20 +278,18 @@
     far = functools.partial(pltpu.with_memory_space_constraint, memory_space=pltpu.HBM)
     lists = [vertical_pages, slash_shift, slash_live.reshape(1, slash_count)]
     table_size = sum(part.shape[1] for part in lists)
-    queries, table = pl.pallas_call(
+    table_shape = jax.ShapeDtypeStruct((1, table_size), jnp.int32)
+    list_scratch = [pltpu.SMEM(part.shape, jnp.int32) for part in lists]
+    queries = pl.pallas_call(
         stage_kernel,
-        out_shape=[
-            jax.ShapeDtypeStruct(queries.shape, queries.dtype),
-            jax.ShapeDtypeStruct((1, table_size), jnp.int32),
-        ],
-        in_specs=[hbm] * 4,
-        out_specs=[vector, scalars],
-        scratch_shapes=[pltpu.SMEM(part.shape, jnp.int32) for part in lists]
-        + [pltpu.SemaphoreType.DMA((4,))],
+        out_shape=jax.ShapeDtypeStruct(queries.shape, queries.dtype),
+        in_specs=[hbm],
+        out_specs=vector,
+        scratch_shapes=[pltpu.SemaphoreType.DMA],
         compiler_params=pltpu.CompilerParams(vmem_limit_bytes=1 << 20),
         cost_estimate=pl.CostEstimate(flops=0, bytes_accessed=2 << 20, transcendentals=0),
         name="stage",
-    )(*map(far, [queries] + lists))
+    )(far(queries))
     own_shard = lax.axis_index("seq")
     if tree:
         half = shards // 2
@@ -292,19 +298,22 @@
         piece_shape = jax.ShapeDtypeStruct((per_shard * piece, head_width), own.dtype)
         opened = pl.pallas_call(
             functools.partial(open_kernel, sizes),
-            out_shape=[block_shape] * (2 + len(bits)) + [piece_shape] * half,
-            in_specs=[hbm] * 2,
-            out_specs=[vector] * (2 + len(bits) + half),
-            scratch_shapes=[pltpu.SemaphoreType.DMA((2,))],
+            out_shape=[block_shape] * 2
+            + [table_shape]
+            + [block_shape] * len(bits)
+            + [piece_shape] * half,
+            in_specs=[hbm] * 5,
+            out_specs=[vector] * 2 + [scalars] + [vector] * (len(bits) + half),
+            scratch_shapes=list_scratch + [pltpu.SemaphoreType.DMA((5,))],
             compiler_params=pltpu.CompilerParams(vmem_limit_bytes=1 << 20),
             cost_estimate=pl.CostEstimate(flops=0, bytes_accessed=1 << 20, transcendentals=0),
             name="open",
-        )(far(own), far(cache))
-        own, cache = opened[:2]
-        near = opened[2 + len(bits) :]
+        )(*map(far, [own, cache] + lists))
+        own, cache, table = opened[:3]
+        near = opened[3 + len(bits) :]
         pieces = [near[0]] + [swapped(near[mask], "seq", mask) for mask in range(1, half)]
-        first_hops = dict(zip(bits, opened[2 : 2 + len(bits)]))
-        blocks = [cache] + gathered(first_hops, "seq", shards)
+        first_hops = dict(zip(bits, opened[3 : 3 + len(bits)]))
+        blocks = [cache] + gathered(first_hops, "seq", shards, True)
         slot_shape = jax.ShapeDtypeStruct((page_count * piece, head_width), jnp.bfloat16)
         small = dict(
             out_shape=slot_shape,
@@ -324,8 +333,16 @@
             name="merge",
             **small,
         )(table, mine, swapped(mine, "seq", half))
-        pieces = [merged] + gathered(dict.fromkeys(bits, merged), "seq", half)
+        pieces = [merged] + gathered(dict.fromkeys(bits, merged), "seq", half, False)
     else:
+        table = pl.pallas_call(
+            table_kernel,
+            out_shape=table_shape,
+            in_specs=[hbm] * 3,
+            out_specs=scalars,
+            scratch_shapes=list_scratch + [pltpu.SemaphoreType.DMA((3,))],
+            name="table",
+        )(*map(far, lists))
         blocks, pieces = [], []
         for k in range(slash_count):
             distance = slash_shift[0, k]

time: 57.9 us -> 57.2 us (0.988)
  waiting for transfers between devices: 25.9 us -> 24.3 us
  starting transfers between devices: 19.4 us -> 20.1 us
    ppermute x16, waiting for transfers between devices: 25.9 us -> 24.3 us  [swapped(): lax.ppermute(value, axis, [(source, source ^ mask) for source in range(co...]
    ppermute x16, starting transfers between devices: 19.4 us -> 20.1 us  [swapped(): lax.ppermute(value, axis, [(source, source ^ mask) for source in range(co...]
    pallas_call x1, Pallas kernels: 1.03 us -> 1.69 us  [body(): pl.pallas_call(functools.partial(open_kernel, sizes), out_shape=[block_sh...]
    pallas_call x1, Pallas kernels: 1.67 us -> 1.05 us  [body(): pl.pallas_call(stage_kernel, out_shape=jax.ShapeDtypeStruct(queries.shape...]
  transfers between devices with their start and end apart: 16 -> 16, of which waited for: 8 -> 11; matrix products, arithmetic and copies ran while one was open for 0% -> 0% of each run, Pallas kernels for 5% -> 4%
where the time goes in v1:
time: 57.2 us; the launch traced here: 57 us
  waiting for transfers between devices  24.3 us (42%)
  starting transfers between devices  20.1 us (35%)
  Pallas kernels  11.6 us (20%)
  other arithmetic  0.95 us (2%)
    ppermute x16, waiting for transfers between devices, swapped(): lax.ppermute(value, axis, [(source, source ^ mask) for source in range(co...  24.3 us
    ppermute x16, starting transfers between devices, swapped(): lax.ppermute(value, axis, [(source, source ^ mask) for source in range(co...  20.1 us
    pallas_call x1, Pallas kernels, body(): pl.pallas_call(functools.partial(attention_kernel, sizes), out_shape=[jax...  7.6 us
    pallas_call x1, Pallas kernels, body(): pl.pallas_call(functools.partial(open_kernel, sizes), out_shape=[block_sh...  1.69 us
  transfers between devices with their start and end apart: 16, of which 11 were waited for; matrix products, arithmetic and copies ran while one was open for 0% of the time, Pallas kernels for 4%

profile of v1, /device:TPU:0, one launch (start us, length us, event | category | flops | bytes accessed | tf_op | source)
XLA Modules:
  0.0 57.0 jit_solution(2989167087155042019)
XLA Ops:
  0.0 1.7 %open.1 = (bf16[512,128]{1,0:T(8,128)(2,1)S(1)}, bf16[512,128]{1,0:T(8,128)(2,1)S(1)}, s32[1,10]{1,0:T(1,128)S(1)}, bf16[512,128]{1,0:T(8,128)(2,1)S(1)}, bf16[5...) custom-call(bf16[512,128]{1,0:T(8,128)(2,1)} %bitcast.5, ...), custom_call_target="tpu_custom_call" | custom-call | bytes 1048576 | tf_op jit(solution)/shard_map/open/pallas_call | solution.py:299
  1.7 4.1 %collective-permute-start.3 = (bf16[512,128]{1,0:T(8,128)(2,1)S(1)}, bf16[512,128]{1,0:T(8,128)(2,1)S(1)}, u32[]{:S(2)}, u32[]{:S(2)}) collective-permute-start(bf16[512,128]{1,0:T(8,128)(2,1)S(1)} %get-tuple-element.22), channel_id=1, source_target_pairs={{0,16},{4,20},{8,24},{12,28},{16,0},{20,4},{24,8},{28,12},{1,17},{... | collective-permute-start | bytes 393224 | tf_op jit(solution)/shard_map/ppermute | solution.py:20
  5.8 1.6 %collective-permute-start.1 = (bf16[512,128]{1,0:T(8,128)(2,1)S(1)}, bf16[512,128]{1,0:T(8,128)(2,1)S(1)}, u32[]{:S(2)}, u32[]{:S(2)}) collective-permute-start(bf16[512,128]{1,0:T(8,128)(2,1)S(1)} %get-tuple-element.21), channel_id=1, source_target_pairs={{0,8},{4,12},{8,0},{12,4},{16,24},{20,28},{24,16},{28,20},{1,9},{5... | collective-permute-start | bytes 393224 | tf_op jit(solution)/shard_map/ppermute | solution.py:20
  7.4 4.8 %collective-permute-done.3.rest_4_ = bf16[512,128]{1,0:T(8,128)(2,1)S(1)} collective-permute-done((bf16[512,128]{1,0:T(8,128)(2,1)S(1)}, bf16[512,128]{1,0:T(8,128)(2,1)S(1)}, u32[]{:S(2)}, u32[]{:S(2)}) %collective-permute-start.3) | collective-permute-done | bytes 131104 | tf_op jit(solution)/shard_map/ppermute | solution.py:20
  12.2 0.6 %collective-permute-start.5 = (bf16[512,128]{1,0:T(8,128)(2,1)S(1)}, bf16[512,128]{1,0:T(8,128)(2,1)S(1)}, u32[]{:S(2)}, u32[]{:S(2)}) collective-permute-start(bf16[512,128]{1,0:T(8,128)(2,1)S(1)} %collective-permute-done.3.rest_4_), channel_id=1, source_target_pairs={{0,8},{4,12},{8,0},{12,4},{16,24},{20,28},{24,16},{28,20},{1,9},{5... | collective-permute-start | bytes 393224 | tf_op jit(solution)/shard_map/ppermute | solution.py:20
  12.9 1.5 %collective-permute-start.7 = (bf16[128,128]{1,0:T(8,128)(2,1)S(1)}, bf16[128,128]{1,0:T(8,128)(2,1)S(1)}, u32[]{:S(2)}, u32[]{:S(2)}) collective-permute-start(bf16[128,128]{1,0:T(8,128)(2,1)S(1)} %get-tuple-element.24), channel_id=1, source_target_pairs={{0,4},{4,0},{8,12},{12,8},{16,20},{20,16},{24,28},{28,24},{1,5},{5... | collective-permute-start | bytes 98312 | tf_op jit(solution)/shard_map/ppermute | solution.py:20
  14.3 1.5 %collective-permute-start.8 = (bf16[128,128]{1,0:T(8,128)(2,1)S(1)}, bf16[128,128]{1,0:T(8,128)(2,1)S(1)}, u32[]{:S(2)}, u32[]{:S(2)}) collective-permute-start(bf16[128,128]{1,0:T(8,128)(2,1)S(1)} %get-tuple-element.25), channel_id=1, source_target_pairs={{0,8},{4,12},{8,0},{12,4},{16,24},{20,28},{24,16},{28,20},{1,9},{5... | collective-permute-start | bytes 98312 | tf_op jit(solution)/shard_map/ppermute | solution.py:20
  15.8 0.5 collective-permute-start.9
  16.3 0.4 collective-permute-done.7.rest_1_
  16.8 1.5 %collective-permute-done.8.rest_2_ = bf16[128,128]{1,0:T(8,128)(2,1)S(1)} collective-permute-done((bf16[128,128]{1,0:T(8,128)(2,1)S(1)}, bf16[128,128]{1,0:T(8,128)(2,1)S(1)}, u32[]{:S(2)}, u32[]{:S(2)}) %collective-permute-start.8) | collective-permute-done | bytes 32800 | tf_op jit(solution)/shard_map/ppermute | solution.py:20
  18.3 2.4 %collective-permute-done.9.rest_3_ = bf16[128,128]{1,0:T(8,128)(2,1)S(1)} collective-permute-done((bf16[128,128]{1,0:T(8,128)(2,1)S(1)}, bf16[128,128]{1,0:T(8,128)(2,1)S(1)}, u32[]{:S(2)}, u32[]{:S(2)}) %collective-permute-start.9) | collective-permute-done | bytes 32800 | tf_op jit(solution)/shard_map/ppermute | solution.py:20
  20.6 0.7 %pick.1.mine = bf16[256,128]{1,0:T(8,128)(2,1)S(1)} custom-call(s32[1,10]{1,0:T(1,128)S(1)} %get-tuple-element.17.table, bf16[128,128]{1,0:T(8,128)(2,1)S(1)} %get-tuple-element.23.rest_0_, bf16[128,128]{1,0:T(8,128)(2,1)S(1)} %collective-permute-done.7.rest_1_, bf16[128,128]{1,0:T(8,128)(2,1)S(1)} %collective-permute-done.8.rest_2_, ...), custom_call_target="tpu_custom_call" | custom-call | bytes 4194304 | tf_op jit(solution)/shard_map/pick/pallas_call | solution.py:324
  21.3 2.0 %collective-permute-start.10 = (bf16[256,128]{1,0:T(8,128)(2,1)S(1)}, bf16[256,128]{1,0:T(8,128)(2,1)S(1)}, u32[]{:S(2)}, u32[]{:S(2)}) collective-permute-start(bf16[256,128]{1,0:T(8,128)(2,1)S(1)} %pick.1.mine), channel_id=1, source_target_pairs={{0,16},{4,20},{8,24},{12,28},{16,0},{20,4},{24,8},{28,12},{1,17},{... | collective-permute-start | bytes 196616 | tf_op jit(solution)/shard_map/ppermute | solution.py:20
  23.3 0.9 %collective-permute-start = (bf16[512,128]{1,0:T(8,128)(2,1)S(1)}, bf16[512,128]{1,0:T(8,128)(2,1)S(1)}, u32[]{:S(2)}, u32[]{:S(2)}) collective-permute-start(bf16[512,128]{1,0:T(8,128)(2,1)S(1)} %get-tuple-element.20), channel_id=1, source_target_pairs={{0,4},{4,0},{8,12},{12,8},{16,20},{20,16},{24,28},{28,24},{1,5},{5... | collective-permute-start | bytes 393224 | tf_op jit(solution)/shard_map/ppermute | solution.py:20
  24.2 3.0 %collective-permute-done.10.other = bf16[256,128]{1,0:T(8,128)(2,1)S(1)} collective-permute-done((bf16[256,128]{1,0:T(8,128)(2,1)S(1)}, bf16[256,128]{1,0:T(8,128)(2,1)S(1)}, u32[]{:S(2)}, u32[]{:S(2)}) %collective-permute-start.10) | collective-permute-done | bytes 65568 | tf_op jit(solution)/shard_map/ppermute | solution.py:20
  27.2 0.6 %merge.1.rest_8_ = bf16[256,128]{1,0:T(8,128)(2,1)S(1)} custom-call(s32[1,10]{1,0:T(1,128)S(1)} %get-tuple-element.17.table, bf16[256,128]{1,0:T(8,128)(2,1)S(1)} %pick.1.mine, bf16[256,128]{1,0:T(8,128)(2,1)S(1)} %collective-permute-done.10.other), custom_call_target="tpu_custom_call" | custom-call | bytes 4194304 | tf_op jit(solution)/shard_map/merge/pallas_call | solution.py:330
  27.8 0.6 collective-permute-start.11
  28.4 1.5 %collective-permute-start.4 = (bf16[512,128]{1,0:T(8,128)(2,1)S(1)}, bf16[512,128]{1,0:T(8,128)(2,1)S(1)}, u32[]{:S(2)}, u32[]{:S(2)}) collective-permute-start(bf16[512,128]{1,0:T(8,128)(2,1)S(1)} %collective-permute-done.3.rest_4_), channel_id=1, source_target_pairs={{0,4},{4,0},{8,12},{12,8},{16,20},{20,16},{24,28},{28,24},{1,5},{5... | collective-permute-start | bytes 393224 | tf_op jit(solution)/shard_map/ppermute | solution.py:20
  29.9 0.0 collective-permute-done.1.rest_2_
  29.9 0.5 collective-permute-start.2
  30.4 0.0 collective-permute-done.5.rest_6_
  30.4 1.5 %collective-permute-start.6 = (bf16[512,128]{1,0:T(8,128)(2,1)S(1)}, bf16[512,128]{1,0:T(8,128)(2,1)S(1)}, u32[]{:S(2)}, u32[]{:S(2)}) collective-permute-start(bf16[512,128]{1,0:T(8,128)(2,1)S(1)} %collective-permute-done.5.rest_6_), channel_id=1, source_target_pairs={{0,4},{4,0},{8,12},{12,8},{16,20},{20,16},{24,28},{28,24},{1,5},{5... | collective-permute-start | bytes 393224 | tf_op jit(solution)/shard_map/ppermute | solution.py:20
  31.9 0.0 collective-permute-done.rest_1_
  31.9 0.4 collective-permute-start.12
  32.4 0.5 collective-permute-done.11.rest_9_
  32.8 1.1 %collective-permute-start.13 = (bf16[256,128]{1,0:T(8,128)(2,1)S(1)}, bf16[256,128]{1,0:T(8,128)(2,1)S(1)}, u32[]{:S(2)}, u32[]{:S(2)}) collective-permute-start(bf16[256,128]{1,0:T(8,128)(2,1)S(1)} %collective-permute-done.11.rest_9_), channel_id=1, source_target_pairs={{0,8},{4,12},{8,0},{12,4},{16,24},{20,28},{24,16},{28,20},{1,9},{5... | collective-permute-start | bytes 196616 | tf_op jit(solution)/shard_map/ppermute | solution.py:20
  34.0 1.0 %stage.1.query_ref = bf16[256,1024]{1,0:T(8,128)(2,1)S(1)} custom-call(bf16[256,1024]{1,0:T(8,128)(2,1)} %query_in.1), custom_call_target="tpu_custom_call" | custom-call | bytes 2097152 | tf_op jit(solution)/shard_map/stage/pallas_call | solution.py:283
  35.0 1.2 %collective-permute-done.12.rest_10_ = bf16[256,128]{1,0:T(8,128)(2,1)S(1)} collective-permute-done((bf16[256,128]{1,0:T(8,128)(2,1)S(1)}, bf16[256,128]{1,0:T(8,128)(2,1)S(1)}, u32[]{:S(2)}, u32[]{:S(2)}) %collective-permute-start.12) | collective-permute-done | bytes 65568 | tf_op jit(solution)/shard_map/ppermute | solution.py:20
  36.2 0.9 %collective-permute-done.13.rest_11_ = bf16[256,128]{1,0:T(8,128)(2,1)S(1)} collective-permute-done((bf16[256,128]{1,0:T(8,128)(2,1)S(1)}, bf16[256,128]{1,0:T(8,128)(2,1)S(1)}, u32[]{:S(2)}, u32[]{:S(2)}) %collective-permute-start.13) | collective-permute-done | bytes 65568 | tf_op jit(solution)/shard_map/ppermute | solution.py:20
  37.1 0.0 collective-permute-done.2.rest_3_
  37.1 0.0 collective-permute-done.4.rest_5_
  37.1 0.9 %collective-permute-done.6.rest_7_ = bf16[512,128]{1,0:T(8,128)(2,1)S(1)} collective-permute-done((bf16[512,128]{1,0:T(8,128)(2,1)S(1)}, bf16[512,128]{1,0:T(8,128)(2,1)S(1)}, u32[]{:S(2)}, u32[]{:S(2)}) %collective-permute-start.6) | collective-permute-done | bytes 131104 | tf_op jit(solution)/shard_map/ppermute | solution.py:20
  38.0 7.6 %attend.1 = (bf16[2,256,512]{2,1,0:T(8,128)(2,1)S(1)}, f32[2,256,512]{2,1,0:T(8,128)S(1)}) custom-call(s32[1,10]{1,0:T(1,128)S(1)} %get-tuple-element.17.table, bf16[256,1024]{1,0:T(8,128)(2,1)S(1)} %stage.1.query_ref, bf16[1024,2048]{1,0:T(8,128)(2,1)} %proj_ref.1, bf16[512,128]{1,0:T(8,128)(2,1)S(1)} %get-tuple-element.18.own_ref, ...), custom_call_target="tpu_custom_call" | custom-call | flops 2684354560 | bytes 8388608 | tf_op jit(solution)/shard_map/attend/pallas_call | solution.py:357
  45.6 0.1 collective-permute-start.14
  45.7 1.9 %collective-permute-done.14 = bf16[2,256,512]{2,1,0:T(8,128)(2,1)S(1)} collective-permute-done((bf16[2,256,512]{2,1,0:T(8,128)(2,1)S(1)}, bf16[2,256,512]{2,1,0:T(8,128)(2,1)S(1)}, u32[]{:S(2)}, u32[]{:S(2)}) %collective-permute-start.14) | collective-permute-done | bytes 524320 | tf_op jit(solution)/shard_map/ppermute | solution.py:20
  47.6 0.2 convert_add_fusion
  47.8 1.6 %collective-permute-start.15 = (bf16[1,256,512]{2,1,0:T(8,128)(2,1)S(1)}, bf16[1,256,512]{2,1,0:T(8,128)(2,1)S(1)}, u32[]{:S(2)}, u32[]{:S(2)}) collective-permute-start(bf16[1,256,512]{2,1,0:T(8,128)(2,1)S(1)} %slice.19), channel_id=1, source_target_pairs={{0,2},{1,3},{2,0},{3,1},{4,6},{5,7},{6,4},{7,5},{8,10},{9,11},{10,... | collective-permute-start | bytes 786440 | tf_op jit(solution)/shard_map/ppermute | solution.py:20
  49.4 6.8 %collective-permute-done.15 = bf16[1,256,512]{2,1,0:T(8,128)(2,1)S(1)} collective-permute-done((bf16[1,256,512]{2,1,0:T(8,128)(2,1)S(1)}, bf16[1,256,512]{2,1,0:T(8,128)(2,1)S(1)}, u32[]{:S(2)}, u32[]{:S(2)}) %collective-permute-start.15) | collective-permute-done | bytes 262176 | tf_op jit(solution)/shard_map/ppermute | solution.py:20
  56.2 0.8 %fusion.1 = bf16[256,512]{1,0:T(8,128)(2,1)} fusion(bf16[1,256,512]{2,1,0:T(8,128)(2,1)S(1)} %collective-permute-done.15, f32[2,256,512]{2,1,0:T(8,128)S(1)} %convert_add_fusion), kind=kLoop, calls=%fused_computation.4 | loop fusion | flops 393216 | bytes 1048576 | tf_op jit(solution)/shard_map/convert_element_type | solution.py:391
  (1 shorter events, 0.0 us)
Async XLA Ops:
  1.7 10.5 %collective-permute-start.3 = (bf16[512,128]{1,0:T(8,128)(2,1)S(1)}, bf16[512,128]{1,0:T(8,128)(2,1)S(1)}, u32[]{:S(2)}, u32[]{:S(2)}) collective-permute-start(bf16[512,128]{1,0:T(8,128)(2,1)S(1)} %get-tuple-element.22), channel_id=1, source_target_pairs={{0,16},{4,20},{8,24},{12,28},{16,0},{20,4},{24,8},{28,12},{1,17},{... | collective-permute-start | bytes 393224 | tf_op jit(solution)/shard_map/ppermute | solution.py:20
  5.8 24.1 %collective-permute-start.1 = (bf16[512,128]{1,0:T(8,128)(2,1)S(1)}, bf16[512,128]{1,0:T(8,128)(2,1)S(1)}, u32[]{:S(2)}, u32[]{:S(2)}) collective-permute-start(bf16[512,128]{1,0:T(8,128)(2,1)S(1)} %get-tuple-element.21), channel_id=1, source_target_pairs={{0,8},{4,12},{8,0},{12,4},{16,24},{20,28},{24,16},{28,20},{1,9},{5... | collective-permute-start | bytes 393224 | tf_op jit(solution)/shard_map/ppermute | solution.py:20
  12.2 18.2 %collective-permute-start.5 = (bf16[512,128]{1,0:T(8,128)(2,1)S(1)}, bf16[512,128]{1,0:T(8,128)(2,1)S(1)}, u32[]{:S(2)}, u32[]{:S(2)}) collective-permute-start(bf16[512,128]{1,0:T(8,128)(2,1)S(1)} %collective-permute-done.3.rest_4_), channel_id=1, source_target_pairs={{0,8},{4,12},{8,0},{12,4},{16,24},{20,28},{24,16},{28,20},{1,9},{5... | collective-permute-start | bytes 393224 | tf_op jit(solution)/shard_map/ppermute | solution.py:20
  12.9 3.9 %collective-permute-start.7 = (bf16[128,128]{1,0:T(8,128)(2,1)S(1)}, bf16[128,128]{1,0:T(8,128)(2,1)S(1)}, u32[]{:S(2)}, u32[]{:S(2)}) collective-permute-start(bf16[128,128]{1,0:T(8,128)(2,1)S(1)} %get-tuple-element.24), channel_id=1, source_target_pairs={{0,4},{4,0},{8,12},{12,8},{16,20},{20,16},{24,28},{28,24},{1,5},{5... | collective-permute-start | bytes 98312 | tf_op jit(solution)/shard_map/ppermute | solution.py:20
  14.3 3.9 %collective-permute-start.8 = (bf16[128,128]{1,0:T(8,128)(2,1)S(1)}, bf16[128,128]{1,0:T(8,128)(2,1)S(1)}, u32[]{:S(2)}, u32[]{:S(2)}) collective-permute-start(bf16[128,128]{1,0:T(8,128)(2,1)S(1)} %get-tuple-element.25), channel_id=1, source_target_pairs={{0,8},{4,12},{8,0},{12,4},{16,24},{20,28},{24,16},{28,20},{1,9},{5... | collective-permute-start | bytes 98312 | tf_op jit(solution)/shard_map/ppermute | solution.py:20
  15.8 4.8 %collective-permute-start.9 = (bf16[128,128]{1,0:T(8,128)(2,1)S(1)}, bf16[128,128]{1,0:T(8,128)(2,1)S(1)}, u32[]{:S(2)}, u32[]{:S(2)}) collective-permute-start(bf16[128,128]{1,0:T(8,128)(2,1)S(1)} %get-tuple-element.26), channel_id=1, source_target_pairs={{0,12},{4,8},{8,4},{12,0},{16,28},{20,24},{24,20},{28,16},{1,13},{... | collective-permute-start | bytes 98312 | tf_op jit(solution)/shard_map/ppermute | solution.py:20
  21.3 5.9 %collective-permute-start.10 = (bf16[256,128]{1,0:T(8,128)(2,1)S(1)}, bf16[256,128]{1,0:T(8,128)(2,1)S(1)}, u32[]{:S(2)}, u32[]{:S(2)}) collective-permute-start(bf16[256,128]{1,0:T(8,128)(2,1)S(1)} %pick.1.mine), channel_id=1, source_target_pairs={{0,16},{4,20},{8,24},{12,28},{16,0},{20,4},{24,8},{28,12},{1,17},{... | collective-permute-start | bytes 196616 | tf_op jit(solution)/shard_map/ppermute | solution.py:20
  23.3 8.7 %collective-permute-start = (bf16[512,128]{1,0:T(8,128)(2,1)S(1)}, bf16[512,128]{1,0:T(8,128)(2,1)S(1)}, u32[]{:S(2)}, u32[]{:S(2)}) collective-permute-start(bf16[512,128]{1,0:T(8,128)(2,1)S(1)} %get-tuple-element.20), channel_id=1, source_target_pairs={{0,4},{4,0},{8,12},{12,8},{16,20},{20,16},{24,28},{28,24},{1,5},{5... | collective-permute-start | bytes 393224 | tf_op jit(solution)/shard_map/ppermute | solution.py:20
  27.8 5.0 %collective-permute-start.11 = (bf16[256,128]{1,0:T(8,128)(2,1)S(1)}, bf16[256,128]{1,0:T(8,128)(2,1)S(1)}, u32[]{:S(2)}, u32[]{:S(2)}) collective-permute-start(bf16[256,128]{1,0:T(8,128)(2,1)S(1)} %merge.1.rest_8_), channel_id=1, source_target_pairs={{0,4},{4,0},{8,12},{12,8},{16,20},{20,16},{24,28},{28,24},{1,5},{5... | collective-permute-start | bytes 196616 | tf_op jit(solution)/shard_map/ppermute | solution.py:20
  28.4 8.8 %collective-permute-start.4 = (bf16[512,128]{1,0:T(8,128)(2,1)S(1)}, bf16[512,128]{1,0:T(8,128)(2,1)S(1)}, u32[]{:S(2)}, u32[]{:S(2)}) collective-permute-start(bf16[512,128]{1,0:T(8,128)(2,1)S(1)} %collective-permute-done.3.rest_4_), channel_id=1, source_target_pairs={{0,4},{4,0},{8,12},{12,8},{16,20},{20,16},{24,28},{28,24},{1,5},{5... | collective-permute-start | bytes 393224 | tf_op jit(solution)/shard_map/ppermute | solution.py:20
  29.9 7.2 %collective-permute-start.2 = (bf16[512,128]{1,0:T(8,128)(2,1)S(1)}, bf16[512,128]{1,0:T(8,128)(2,1)S(1)}, u32[]{:S(2)}, u32[]{:S(2)}) collective-permute-start(bf16[512,128]{1,0:T(8,128)(2,1)S(1)} %collective-permute-done.1.rest_2_), channel_id=1, source_target_pairs={{0,4},{4,0},{8,12},{12,8},{16,20},{20,16},{24,28},{28,24},{1,5},{5... | collective-permute-start | bytes 393224 | tf_op jit(solution)/shard_map/ppermute | solution.py:20
  30.4 7.6 %collective-permute-start.6 = (bf16[512,128]{1,0:T(8,128)(2,1)S(1)}, bf16[512,128]{1,0:T(8,128)(2,1)S(1)}, u32[]{:S(2)}, u32[]{:S(2)}) collective-permute-start(bf16[512,128]{1,0:T(8,128)(2,1)S(1)} %collective-permute-done.5.rest_6_), channel_id=1, source_target_pairs={{0,4},{4,0},{8,12},{12,8},{16,20},{20,16},{24,28},{28,24},{1,5},{5... | collective-permute-start | bytes 393224 | tf_op jit(solution)/shard_map/ppermute | solution.py:20
  31.9 4.3 %collective-permute-start.12 = (bf16[256,128]{1,0:T(8,128)(2,1)S(1)}, bf16[256,128]{1,0:T(8,128)(2,1)S(1)}, u32[]{:S(2)}, u32[]{:S(2)}) collective-permute-start(bf16[256,128]{1,0:T(8,128)(2,1)S(1)} %merge.1.rest_8_), channel_id=1, source_target_pairs={{0,8},{4,12},{8,0},{12,4},{16,24},{20,28},{24,16},{28,20},{1,9},{5... | collective-permute-start | bytes 196616 | tf_op jit(solution)/shard_map/ppermute | solution.py:20
  32.8 4.3 %collective-permute-start.13 = (bf16[256,128]{1,0:T(8,128)(2,1)S(1)}, bf16[256,128]{1,0:T(8,128)(2,1)S(1)}, u32[]{:S(2)}, u32[]{:S(2)}) collective-permute-start(bf16[256,128]{1,0:T(8,128)(2,1)S(1)} %collective-permute-done.11.rest_9_), channel_id=1, source_target_pairs={{0,8},{4,12},{8,0},{12,4},{16,24},{20,28},{24,16},{28,20},{1,9},{5... | collective-permute-start | bytes 196616 | tf_op jit(solution)/shard_map/ppermute | solution.py:20
  45.6 2.0 %collective-permute-start.14 = (bf16[2,256,512]{2,1,0:T(8,128)(2,1)S(1)}, bf16[2,256,512]{2,1,0:T(8,128)(2,1)S(1)}, u32[]{:S(2)}, u32[]{:S(2)}) collective-permute-start(bf16[2,256,512]{2,1,0:T(8,128)(2,1)S(1)} %get-tuple-element.28), channel_id=1, source_target_pairs={{0,1},{1,0},{2,3},{3,2},{4,5},{5,4},{6,7},{7,6},{8,9},{9,8},{10,11... | collective-permute-start | bytes 1572872 | tf_op jit(solution)/shard_map/ppermute | solution.py:20
  47.8 8.4 %collective-permute-start.15 = (bf16[1,256,512]{2,1,0:T(8,128)(2,1)S(1)}, bf16[1,256,512]{2,1,0:T(8,128)(2,1)S(1)}, u32[]{:S(2)}, u32[]{:S(2)}) collective-permute-start(bf16[1,256,512]{2,1,0:T(8,128)(2,1)S(1)} %slice.19), channel_id=1, source_target_pairs={{0,2},{1,3},{2,0},{3,1},{4,6},{5,7},{6,4},{7,5},{8,10},{9,11},{10,... | collective-permute-start | bytes 786440 | tf_op jit(solution)/shard_map/ppermute | solution.py:20

commit v2 on v0

--- a/solution.py
+++ b/solution.py
@@ -25,13 +25,13 @@
     return lax.ppermute(value, axis, [(source, (source + steps) % count) for source in range(count)])
 
 
-def gathered(first_hops, axis, count):
+def gathered(first_hops, axis, rows):
     blocks = {}
-    for mask in range(1, count):
+    for mask in range(1, lax.axis_size(axis)):
         low = mask & -mask
-        source = blocks[mask - low] if mask > low else first_hops[low]
+        source = blocks[mask - low][:rows] if mask > low else first_hops[low]
         blocks[mask] = swapped(source, axis, low)
-    return [blocks[mask] for mask in range(1, count)]
+    return [blocks[mask] for mask in range(1, len(blocks) + 1)]
 
 
 def rotate(value, amount, shards):
@@ -61,11 +61,11 @@
     return slashes, pages
 
 
-def open_kernel(sizes, own_in, cache_in, *rest):
+def open_kernel(sizes, own_in, cache_in, own_near, cache_near, *rest):
     shards, per_shard, piece = sizes["shards"], sizes["per_shard"], sizes["piece"]
-    own_near, cache_near, sems = rest[0], rest[1], rest[-1]
+    sems, half = rest[-1], shards // 2
     hop_count = shards.bit_length() - 1
-    hops, pieces = rest[2 : 2 + hop_count], rest[2 + hop_count : -1]
+    hops, alone = rest[:hop_count], list(rest[hop_count:-1])
     copies = [
         pltpu.make_async_copy(own_in, own_near, sems.at[0]),
         pltpu.make_async_copy(cache_in, cache_near, sems.at[1]),
@@ -75,39 +75,41 @@
     for copy in copies:
         copy.wait()
     me = lax.axis_index("seq")
+    block = pl.ds(0, own_near.shape[0])
     for number, hop in enumerate(hops):
         upper = (me >> number) & 1
 
         @pl.when(upper == 0)
         def _(hop=hop):
-            hop[...] = own_near[...]
+            hop[block, :] = own_near[...]
 
         @pl.when(upper == 1)
         def _(hop=hop):
-            hop[...] = cache_near[...]
-
-    for mask, place in enumerate(pieces):
+            hop[block, :] = cache_near[...]
+
+    for mask in range(half):
+        if mask and mask & (mask - 1) == 0:
+            place, base = hops[mask.bit_length() - 1], own_near.shape[0]
+        else:
+            place, base = alone.pop(0), 0
         for at in range(per_shard):
-            first = (at * len(pieces) + mask) * piece
-            place[pl.ds(at * piece, piece), :] = cache_near[pl.ds(first, piece), :]
+            first = (at * half + mask) * piece
+            place[pl.ds(base + at * piece, piece), :] = cache_near[pl.ds(first, piece), :]
 
 
 def stage_kernel(query_in, page_in, shift_in, live_in, query_near, table, *rest):
-    page_near, shift_near, live_near, sems = rest
-    ints = (page_near, shift_near, live_near)
+    lists, sems = rest[:3], rest[3]
+    sources = (page_in, shift_in, live_in, query_in)
     copies = [
         pltpu.make_async_copy(source, place, sems.at[at])
-        for at, (source, place) in enumerate(
-            [(page_in, page_near), (shift_in, shift_near), (live_in, live_near)]
-            + [(query_in, query_near)]
-        )
+        for at, (source, place) in enumerate(zip(sources, tuple(lists) + (query_near,)))
     ]
     for copy in copies:
         copy.start()
     for copy in copies[:3]:
         copy.wait()
     at = 0
-    for part in ints:
+    for part in lists:
         for entry in range(part.shape[1]):
             table[0, at] = part[0, entry]
             at += 1
@@ -123,7 +125,8 @@
 
             @pl.when((bits & (len(pieces) - 1)) == mask)
             def _(source=source):
-                first = pl.multiple_of(place * piece, piece)
+                base = source.shape[0] - sizes["per_shard"] * piece
+                first = pl.multiple_of(base + place * piece, piece)
                 slots[pl.ds(i * piece, piece), :] = source[pl.ds(first, piece), :]
 
 
@@ -149,7 +152,8 @@
     page_rows, members, tree = sizes["page_rows"], sizes["members"], sizes["tree"]
     piece = sizes["piece"]
     block_count = shards if tree else slash_count
-    piece_count = shards // 2 if tree else page_count
+    piece_count = shards.bit_length() - 1 if tree else page_count
+    half = shards // 2
     blocks = rest[:block_count]
     pieces = rest[block_count : block_count + piece_count]
     rest = rest[block_count + piece_count :]
@@ -168,18 +172,19 @@
 
                 @pl.when(bits == mask)
                 def _(mask=mask):
-                    wide[here, :] = blocks[mask][...].astype(jnp.float32)
+                    wide[here, :] = blocks[mask][pl.ds(0, 2 * rows), :].astype(jnp.float32)
         else:
             wide[here, :] = blocks[k][...].astype(jnp.float32)
         chunks.append((first, rows, live))
         first += rows
     for i, (bits, _, is_open) in enumerate(pages):
         if tree:
-            for mask in range(piece_count):
-                at = pl.multiple_of(2 * first + ((mask ^ bits) & (piece_count - 1)) * piece, piece)
-                wide[pl.ds(at, piece), :] = pieces[mask][pl.ds(i * piece, piece), :].astype(
-                    jnp.float32
-                )
+            for mask in range(half):
+                at = pl.multiple_of(2 * first + ((mask ^ bits) & (half - 1)) * piece, piece)
+                top = 1 << (mask.bit_length() - 1) if mask else 0
+                start = ((mask - top) * page_count + i) * piece
+                source = pieces[mask.bit_length()][pl.ds(start, piece), :]
+                wide[pl.ds(at, piece), :] = source.astype(jnp.float32)
         else:
             wide[pl.ds(2 * first, 2 * page_rows), :] = pieces[i][...].astype(jnp.float32)
         chunks.append((first, page_rows, is_open))
@@ -289,12 +294,18 @@
         half = shards // 2
         bits = [1 << number for number in range(shards.bit_length() - 1)]
         block_shape = jax.ShapeDtypeStruct(own.shape, own.dtype)
-        piece_shape = jax.ShapeDtypeStruct((per_shard * piece, head_width), own.dtype)
+        piece_rows = per_shard * piece
+        alone = [mask for mask in range(1, half) if mask & (mask - 1)]
+        extra = [
+            jax.ShapeDtypeStruct((own.shape[0] + (piece_rows if bit < half else 0), head_width), own.dtype)
+            for bit in bits
+        ]
+        piece_shape = jax.ShapeDtypeStruct((piece_rows, head_width), own.dtype)
         opened = pl.pallas_call(
             functools.partial(open_kernel, sizes),
-            out_shape=[block_shape] * (2 + len(bits)) + [piece_shape] * half,
+            out_shape=[block_shape] * 2 + extra + [piece_shape] * (1 + len(alone)),
             in_specs=[hbm] * 2,
-            out_specs=[vector] * (2 + len(bits) + half),
+            out_specs=[vector] * (2 + len(bits) + 1 + len(alone)),
             scratch_shapes=[pltpu.SemaphoreType.DMA((2,))],
             compiler_params=pltpu.CompilerParams(vmem_limit_bytes=1 << 20),
             cost_estimate=pl.CostEstimate(flops=0, bytes_accessed=1 << 20, transcendentals=0),
@@ -302,9 +313,10 @@
         )(far(own), far(cache))
         own, cache = opened[:2]
         near = opened[2 + len(bits) :]
-        pieces = [near[0]] + [swapped(near[mask], "seq", mask) for mask in range(1, half)]
         first_hops = dict(zip(bits, opened[2 : 2 + len(bits)]))
-        blocks = [cache] + gathered(first_hops, "seq", shards)
+        blocks = [cache] + gathered(first_hops, "seq", own.shape[0])
+        diagonal = {mask: swapped(near[1 + at], "seq", mask) for at, mask in enumerate(alone)}
+        pieces = [near[0]] + [diagonal.get(mask, blocks[mask]) for mask in range(1, half)]
         slot_shape = jax.ShapeDtypeStruct((page_count * piece, head_width), jnp.bfloat16)
         small = dict(
             out_shape=slot_shape,
@@ -324,7 +336,10 @@
             name="merge",
             **small,
         )(table, mine, swapped(mine, "seq", half))
-        pieces = [merged] + gathered(dict.fromkeys(bits, merged), "seq", half)
+        pieces = [merged]
+        for bit in bits[:-1]:
+            sent = jnp.concatenate(pieces, 0) if bit > 1 else merged
+            pieces.append(swapped(sent, "seq", bit))
     else:
         blocks, pieces = [], []
         for k in range(slash_count):

time: 57.9 us -> 51.2 us (0.88)
  waiting for transfers between devices: 25.9 us -> 20.4 us
  starting transfers between devices: 19.4 us -> 18.1 us
    ppermute x16 -> x13, waiting for transfers between devices: 25.9 us -> 20.4 us  [swapped(): lax.ppermute(value, axis, [(source, source ^ mask) for source in range(co...]
    ppermute x16 -> x13, starting transfers between devices: 19.4 us -> 18.1 us  [swapped(): lax.ppermute(value, axis, [(source, source ^ mask) for source in range(co...]
  transfers between devices with their start and end apart: 16 -> 13, of which waited for: 8 -> 9; matrix products, arithmetic and copies ran while one was open for 0% -> 0% of each run, Pallas kernels for 5% -> 6%
where the time goes in v2:
time: 51.2 us; the launch traced here: 51.1 us
  waiting for transfers between devices  20.4 us (40%)
  starting transfers between devices  18.1 us (35%)
  Pallas kernels  11.4 us (22%)
  other arithmetic  0.96 us (2%)
    ppermute x13, waiting for transfers between devices, swapped(): lax.ppermute(value, axis, [(source, source ^ mask) for source in range(co...  20.4 us
    ppermute x13, starting transfers between devices, swapped(): lax.ppermute(value, axis, [(source, source ^ mask) for source in range(co...  18.1 us
    pallas_call x1, Pallas kernels, body(): pl.pallas_call(functools.partial(attention_kernel, sizes), out_shape=[jax...  7.49 us
    pallas_call x1, Pallas kernels, body(): pl.pallas_call(stage_kernel, out_shape=[jax.ShapeDtypeStruct(queries.shap...  1.67 us
    pallas_call x1, Pallas kernels, body(): pl.pallas_call(functools.partial(open_kernel, sizes), out_shape=[block_sh...  1.03 us
  transfers between devices with their start and end apart: 13, of which 9 were waited for; matrix products, arithmetic and copies ran while one was open for 0% of the time, Pallas kernels for 6%

profile of v2, /device:TPU:0, one launch (start us, length us, event | category | flops | bytes accessed | tf_op | source)
XLA Modules:
  0.0 51.1 jit_solution(12461907067549428251)
XLA Ops:
  0.0 1.0 %open.1 = (bf16[512,128]{1,0:T(8,128)(2,1)S(1)}, bf16[512,128]{1,0:T(8,128)(2,1)S(1)}, bf16[640,128]{1,0:T(8,128)(2,1)S(1)}, bf16[640,128]{1,0:T(8,128)(2,1)S(1)...) custom-call(bf16[512,128]{1,0:T(8,128)(2,1)} %bitcast.5, ...), custom_call_target="tpu_custom_call" | custom-call | bytes 1048576 | tf_op jit(solution)/shard_map/open/pallas_call | solution.py:304
  1.0 3.0 %collective-permute-start = (bf16[640,128]{1,0:T(8,128)(2,1)S(1)}, bf16[640,128]{1,0:T(8,128)(2,1)S(1)}, u32[]{:S(2)}, u32[]{:S(2)}) collective-permute-start(bf16[640,128]{1,0:T(8,128)(2,1)S(1)} %get-tuple-element.20), channel_id=1, source_target_pairs={{0,4},{4,0},{8,12},{12,8},{16,20},{20,16},{24,28},{28,24},{1,5},{5... | collective-permute-start | bytes 491528 | tf_op jit(solution)/shard_map/ppermute | solution.py:20
  4.1 1.6 %collective-permute-start.1 = (bf16[640,128]{1,0:T(8,128)(2,1)S(1)}, bf16[640,128]{1,0:T(8,128)(2,1)S(1)}, u32[]{:S(2)}, u32[]{:S(2)}) collective-permute-start(bf16[640,128]{1,0:T(8,128)(2,1)S(1)} %get-tuple-element.21), channel_id=1, source_target_pairs={{0,8},{4,12},{8,0},{12,4},{16,24},{20,28},{24,16},{28,20},{1,9},{5... | collective-permute-start | bytes 491528 | tf_op jit(solution)/shard_map/ppermute | solution.py:20
  5.6 2.6 %collective-permute-start.3 = (bf16[512,128]{1,0:T(8,128)(2,1)S(1)}, bf16[512,128]{1,0:T(8,128)(2,1)S(1)}, u32[]{:S(2)}, u32[]{:S(2)}) collective-permute-start(bf16[512,128]{1,0:T(8,128)(2,1)S(1)} %get-tuple-element.22), channel_id=1, source_target_pairs={{0,16},{4,20},{8,24},{12,28},{16,0},{20,4},{24,8},{28,12},{1,17},{... | collective-permute-start | bytes 393224 | tf_op jit(solution)/shard_map/ppermute | solution.py:20
  8.2 0.4 collective-permute-start.7
  8.7 1.7 %stage.1 = (bf16[256,1024]{1,0:T(8,128)(2,1)S(1)}, s32[1,10]{1,0:T(1,128)S(1)}) custom-call(bf16[256,1024]{1,0:T(8,128)(2,1)} %query_in.1, s32[1,4]{1,0:T(1,128)} %page_in.1, s32[1,3]{1,0:T(1,128)} %shift_in.1, s32[1,3]{1,0:T(1,128)} %bitcast.7), custom_call_target="tpu_custom_call" | custom-call | bytes 2097152 | tf_op jit(solution)/shard_map/stage/pallas_call | solution.py:278
  10.3 2.3 %collective-permute-done.3.rest_4_ = bf16[512,128]{1,0:T(8,128)(2,1)S(1)} collective-permute-done((bf16[512,128]{1,0:T(8,128)(2,1)S(1)}, bf16[512,128]{1,0:T(8,128)(2,1)S(1)}, u32[]{:S(2)}, u32[]{:S(2)}) %collective-permute-start.3) | collective-permute-done | bytes 131104 | tf_op jit(solution)/shard_map/ppermute | solution.py:20
  12.7 2.8 %collective-permute-start.5 = (bf16[512,128]{1,0:T(8,128)(2,1)S(1)}, bf16[512,128]{1,0:T(8,128)(2,1)S(1)}, u32[]{:S(2)}, u32[]{:S(2)}) collective-permute-start(bf16[512,128]{1,0:T(8,128)(2,1)S(1)} %collective-permute-done.3.rest_4_), channel_id=1, source_target_pairs={{0,8},{4,12},{8,0},{12,4},{16,24},{20,28},{24,16},{28,20},{1,9},{5... | collective-permute-start | bytes 393224 | tf_op jit(solution)/shard_map/ppermute | solution.py:20
  15.5 0.0 collective-permute-done.7.rest_3_
  15.5 0.0 collective-permute-done.rest_1_
  15.5 0.0 collective-permute-done.1.rest_2_
  15.5 0.7 %pick.1.mine = bf16[256,128]{1,0:T(8,128)(2,1)S(1)} custom-call(s32[1,10]{1,0:T(1,128)S(1)} %get-tuple-element.16.table, bf16[128,128]{1,0:T(8,128)(2,1)S(1)} %get-tuple-element.23.rest_0_, bf16[640,128]{1,0:T(8,128)(2,1)S(1)} %collective-permute-done.rest_1_, bf16[640,128]{1,0:T(8,128)(2,1)S(1)} %collective-permute-done.1.rest_2_, ...), custom_call_target="tpu_custom_call" | custom-call | bytes 4194304 | tf_op jit(solution)/shard_map/pick/pallas_call | solution.py:327
  16.1 1.8 %collective-permute-start.8 = (bf16[256,128]{1,0:T(8,128)(2,1)S(1)}, bf16[256,128]{1,0:T(8,128)(2,1)S(1)}, u32[]{:S(2)}, u32[]{:S(2)}) collective-permute-start(bf16[256,128]{1,0:T(8,128)(2,1)S(1)} %pick.1.mine), channel_id=1, source_target_pairs={{0,16},{4,20},{8,24},{12,28},{16,0},{20,4},{24,8},{28,12},{1,17},{... | collective-permute-start | bytes 196616 | tf_op jit(solution)/shard_map/ppermute | solution.py:20
  18.0 3.6 %collective-permute-done.8.other = bf16[256,128]{1,0:T(8,128)(2,1)S(1)} collective-permute-done((bf16[256,128]{1,0:T(8,128)(2,1)S(1)}, bf16[256,128]{1,0:T(8,128)(2,1)S(1)}, u32[]{:S(2)}, u32[]{:S(2)}) %collective-permute-start.8) | collective-permute-done | bytes 65568 | tf_op jit(solution)/shard_map/ppermute | solution.py:20
  21.5 0.6 %merge.1.rest_8_ = bf16[256,128]{1,0:T(8,128)(2,1)S(1)} custom-call(s32[1,10]{1,0:T(1,128)S(1)} %get-tuple-element.16.table, bf16[256,128]{1,0:T(8,128)(2,1)S(1)} %pick.1.mine, bf16[256,128]{1,0:T(8,128)(2,1)S(1)} %collective-permute-done.8.other), custom_call_target="tpu_custom_call" | custom-call | bytes 4194304 | tf_op jit(solution)/shard_map/merge/pallas_call | solution.py:333
  22.1 0.9 %collective-permute-start.9 = (bf16[256,128]{1,0:T(8,128)(2,1)S(1)}, bf16[256,128]{1,0:T(8,128)(2,1)S(1)}, u32[]{:S(2)}, u32[]{:S(2)}) collective-permute-start(bf16[256,128]{1,0:T(8,128)(2,1)S(1)} %merge.1.rest_8_), channel_id=1, source_target_pairs={{0,4},{4,0},{8,12},{12,8},{16,20},{20,16},{24,28},{28,24},{1,5},{5... | collective-permute-start | bytes 196616 | tf_op jit(solution)/shard_map/ppermute | solution.py:20
  23.0 1.2 %collective-permute-start.4 = (bf16[512,128]{1,0:T(8,128)(2,1)S(1)}, bf16[512,128]{1,0:T(8,128)(2,1)S(1)}, u32[]{:S(2)}, u32[]{:S(2)}) collective-permute-start(bf16[512,128]{1,0:T(8,128)(2,1)S(1)} %collective-permute-done.3.rest_4_), channel_id=1, source_target_pairs={{0,4},{4,0},{8,12},{12,8},{16,20},{20,16},{24,28},{28,24},{1,5},{5... | collective-permute-start | bytes 393224 | tf_op jit(solution)/shard_map/ppermute | solution.py:20
  24.2 0.9 %collective-permute-start.2 = (bf16[512,128]{1,0:T(8,128)(2,1)S(1)}, bf16[512,128]{1,0:T(8,128)(2,1)S(1)}, u32[]{:S(2)}, u32[]{:S(2)}) collective-permute-start(bf16[512,128]{1,0:T(8,128)(2,1)S(1)} %slice.15), channel_id=1, source_target_pairs={{0,4},{4,0},{8,12},{12,8},{16,20},{20,16},{24,28},{28,24},{1,5},{5... | collective-permute-start | bytes 393224 | tf_op jit(solution)/shard_map/ppermute | solution.py:20
  25.1 0.0 collective-permute-done.5.rest_6_
  25.1 1.2 %collective-permute-start.6 = (bf16[512,128]{1,0:T(8,128)(2,1)S(1)}, bf16[512,128]{1,0:T(8,128)(2,1)S(1)}, u32[]{:S(2)}, u32[]{:S(2)}) collective-permute-start(bf16[512,128]{1,0:T(8,128)(2,1)S(1)} %collective-permute-done.5.rest_6_), channel_id=1, source_target_pairs={{0,4},{4,0},{8,12},{12,8},{16,20},{20,16},{24,28},{28,24},{1,5},{5... | collective-permute-start | bytes 393224 | tf_op jit(solution)/shard_map/ppermute | solution.py:20
  26.3 0.8 %collective-permute-done.9.rest_9_ = bf16[256,128]{1,0:T(8,128)(2,1)S(1)} collective-permute-done((bf16[256,128]{1,0:T(8,128)(2,1)S(1)}, bf16[256,128]{1,0:T(8,128)(2,1)S(1)}, u32[]{:S(2)}, u32[]{:S(2)}) %collective-permute-start.9) | collective-permute-done | bytes 65568 | tf_op jit(solution)/shard_map/ppermute | solution.py:20
  27.2 0.1 collective-permute-start.10
  27.3 1.7 %collective-permute-done.4.rest_5_ = bf16[512,128]{1,0:T(8,128)(2,1)S(1)} collective-permute-done((bf16[512,128]{1,0:T(8,128)(2,1)S(1)}, bf16[512,128]{1,0:T(8,128)(2,1)S(1)}, u32[]{:S(2)}, u32[]{:S(2)}) %collective-permute-start.4) | collective-permute-done | bytes 131104 | tf_op jit(solution)/shard_map/ppermute | solution.py:20
  29.0 1.4 %collective-permute-done.2.rest_3_ = bf16[512,128]{1,0:T(8,128)(2,1)S(1)} collective-permute-done((bf16[512,128]{1,0:T(8,128)(2,1)S(1)}, bf16[512,128]{1,0:T(8,128)(2,1)S(1)}, u32[]{:S(2)}, u32[]{:S(2)}) %collective-permute-start.2) | collective-permute-done | bytes 131104 | tf_op jit(solution)/shard_map/ppermute | solution.py:20
  30.4 1.4 %collective-permute-done.6.rest_7_ = bf16[512,128]{1,0:T(8,128)(2,1)S(1)} collective-permute-done((bf16[512,128]{1,0:T(8,128)(2,1)S(1)}, bf16[512,128]{1,0:T(8,128)(2,1)S(1)}, u32[]{:S(2)}, u32[]{:S(2)}) %collective-permute-start.6) | collective-permute-done | bytes 131104 | tf_op jit(solution)/shard_map/ppermute | solution.py:20
  31.8 0.4 collective-permute-done.10.rest_10_
  32.2 7.5 %attend.1 = (bf16[2,256,512]{2,1,0:T(8,128)(2,1)S(1)}, f32[2,256,512]{2,1,0:T(8,128)S(1)}) custom-call(s32[1,10]{1,0:T(1,128)S(1)} %get-tuple-element.16.table, bf16[256,1024]{1,0:T(8,128)(2,1)S(1)} %get-tuple-element.17.query_ref, bf16[1024,2048]{1,0:T(8,128)(2,1)} %proj_ref.1, bf16[512,128]{1,0:T(8,128)(2,1)S(1)} %get-tuple-element.18.own_ref, ...), custom_call_target="tpu_custom_call" | custom-call | flops 2684354560 | bytes 8388608 | tf_op jit(solution)/shard_map/attend/pallas_call | solution.py:355
  39.7 0.1 collective-permute-start.11
  39.8 1.9 %collective-permute-done.11 = bf16[2,256,512]{2,1,0:T(8,128)(2,1)S(1)} collective-permute-done((bf16[2,256,512]{2,1,0:T(8,128)(2,1)S(1)}, bf16[2,256,512]{2,1,0:T(8,128)(2,1)S(1)}, u32[]{:S(2)}, u32[]{:S(2)}) %collective-permute-start.11) | collective-permute-done | bytes 524320 | tf_op jit(solution)/shard_map/ppermute | solution.py:20
  41.7 0.2 convert_add_fusion
  41.9 1.6 %collective-permute-start.12 = (bf16[1,256,512]{2,1,0:T(8,128)(2,1)S(1)}, bf16[1,256,512]{2,1,0:T(8,128)(2,1)S(1)}, u32[]{:S(2)}, u32[]{:S(2)}) collective-permute-start(bf16[1,256,512]{2,1,0:T(8,128)(2,1)S(1)} %slice.24), channel_id=1, source_target_pairs={{0,2},{1,3},{2,0},{3,1},{4,6},{5,7},{6,4},{7,5},{8,10},{9,11},{10,... | collective-permute-start | bytes 786440 | tf_op jit(solution)/shard_map/ppermute | solution.py:20
  43.5 6.8 %collective-permute-done.12 = bf16[1,256,512]{2,1,0:T(8,128)(2,1)S(1)} collective-permute-done((bf16[1,256,512]{2,1,0:T(8,128)(2,1)S(1)}, bf16[1,256,512]{2,1,0:T(8,128)(2,1)S(1)}, u32[]{:S(2)}, u32[]{:S(2)}) %collective-permute-start.12) | collective-permute-done | bytes 262176 | tf_op jit(solution)/shard_map/ppermute | solution.py:20
  50.3 0.8 %fusion.1 = bf16[256,512]{1,0:T(8,128)(2,1)} fusion(bf16[1,256,512]{2,1,0:T(8,128)(2,1)S(1)} %collective-permute-done.12, f32[2,256,512]{2,1,0:T(8,128)S(1)} %convert_add_fusion), kind=kLoop, calls=%fused_computation.4 | loop fusion | flops 393216 | bytes 1048576 | tf_op jit(solution)/shard_map/convert_element_type | solution.py:389
  (3 shorter events, 0.1 us)
Async XLA Ops:
  1.0 14.4 %collective-permute-start = (bf16[640,128]{1,0:T(8,128)(2,1)S(1)}, bf16[640,128]{1,0:T(8,128)(2,1)S(1)}, u32[]{:S(2)}, u32[]{:S(2)}) collective-permute-start(bf16[640,128]{1,0:T(8,128)(2,1)S(1)} %get-tuple-element.20), channel_id=1, source_target_pairs={{0,4},{4,0},{8,12},{12,8},{16,20},{20,16},{24,28},{28,24},{1,5},{5... | collective-permute-start | bytes 491528 | tf_op jit(solution)/shard_map/ppermute | solution.py:20
  4.1 11.4 %collective-permute-start.1 = (bf16[640,128]{1,0:T(8,128)(2,1)S(1)}, bf16[640,128]{1,0:T(8,128)(2,1)S(1)}, u32[]{:S(2)}, u32[]{:S(2)}) collective-permute-start(bf16[640,128]{1,0:T(8,128)(2,1)S(1)} %get-tuple-element.21), channel_id=1, source_target_pairs={{0,8},{4,12},{8,0},{12,4},{16,24},{20,28},{24,16},{28,20},{1,9},{5... | collective-permute-start | bytes 491528 | tf_op jit(solution)/shard_map/ppermute | solution.py:20
  5.6 7.0 %collective-permute-start.3 = (bf16[512,128]{1,0:T(8,128)(2,1)S(1)}, bf16[512,128]{1,0:T(8,128)(2,1)S(1)}, u32[]{:S(2)}, u32[]{:S(2)}) collective-permute-start(bf16[512,128]{1,0:T(8,128)(2,1)S(1)} %get-tuple-element.22), channel_id=1, source_target_pairs={{0,16},{4,20},{8,24},{12,28},{16,0},{20,4},{24,8},{28,12},{1,17},{... | collective-permute-start | bytes 393224 | tf_op jit(solution)/shard_map/ppermute | solution.py:20
  8.2 7.2 %collective-permute-start.7 = (bf16[128,128]{1,0:T(8,128)(2,1)S(1)}, bf16[128,128]{1,0:T(8,128)(2,1)S(1)}, u32[]{:S(2)}, u32[]{:S(2)}) collective-permute-start(bf16[128,128]{1,0:T(8,128)(2,1)S(1)} %get-tuple-element.24), channel_id=1, source_target_pairs={{0,12},{4,8},{8,4},{12,0},{16,28},{20,24},{24,20},{28,16},{1,13},{... | collective-permute-start | bytes 98312 | tf_op jit(solution)/shard_map/ppermute | solution.py:20
  12.7 12.5 %collective-permute-start.5 = (bf16[512,128]{1,0:T(8,128)(2,1)S(1)}, bf16[512,128]{1,0:T(8,128)(2,1)S(1)}, u32[]{:S(2)}, u32[]{:S(2)}) collective-permute-start(bf16[512,128]{1,0:T(8,128)(2,1)S(1)} %collective-permute-done.3.rest_4_), channel_id=1, source_target_pairs={{0,8},{4,12},{8,0},{12,4},{16,24},{20,28},{24,16},{28,20},{1,9},{5... | collective-permute-start | bytes 393224 | tf_op jit(solution)/shard_map/ppermute | solution.py:20
  16.1 5.4 %collective-permute-start.8 = (bf16[256,128]{1,0:T(8,128)(2,1)S(1)}, bf16[256,128]{1,0:T(8,128)(2,1)S(1)}, u32[]{:S(2)}, u32[]{:S(2)}) collective-permute-start(bf16[256,128]{1,0:T(8,128)(2,1)S(1)} %pick.1.mine), channel_id=1, source_target_pairs={{0,16},{4,20},{8,24},{12,28},{16,0},{20,4},{24,8},{28,12},{1,17},{... | collective-permute-start | bytes 196616 | tf_op jit(solution)/shard_map/ppermute | solution.py:20
  22.1 5.0 %collective-permute-start.9 = (bf16[256,128]{1,0:T(8,128)(2,1)S(1)}, bf16[256,128]{1,0:T(8,128)(2,1)S(1)}, u32[]{:S(2)}, u32[]{:S(2)}) collective-permute-start(bf16[256,128]{1,0:T(8,128)(2,1)S(1)} %merge.1.rest_8_), channel_id=1, source_target_pairs={{0,4},{4,0},{8,12},{12,8},{16,20},{20,16},{24,28},{28,24},{1,5},{5... | collective-permute-start | bytes 196616 | tf_op jit(solution)/shard_map/ppermute | solution.py:20
  23.0 5.9 %collective-permute-start.4 = (bf16[512,128]{1,0:T(8,128)(2,1)S(1)}, bf16[512,128]{1,0:T(8,128)(2,1)S(1)}, u32[]{:S(2)}, u32[]{:S(2)}) collective-permute-start(bf16[512,128]{1,0:T(8,128)(2,1)S(1)} %collective-permute-done.3.rest_4_), channel_id=1, source_target_pairs={{0,4},{4,0},{8,12},{12,8},{16,20},{20,16},{24,28},{28,24},{1,5},{5... | collective-permute-start | bytes 393224 | tf_op jit(solution)/shard_map/ppermute | solution.py:20
  24.2 6.1 %collective-permute-start.2 = (bf16[512,128]{1,0:T(8,128)(2,1)S(1)}, bf16[512,128]{1,0:T(8,128)(2,1)S(1)}, u32[]{:S(2)}, u32[]{:S(2)}) collective-permute-start(bf16[512,128]{1,0:T(8,128)(2,1)S(1)} %slice.15), channel_id=1, source_target_pairs={{0,4},{4,0},{8,12},{12,8},{16,20},{20,16},{24,28},{28,24},{1,5},{5... | collective-permute-start | bytes 393224 | tf_op jit(solution)/shard_map/ppermute | solution.py:20
  25.1 6.6 %collective-permute-start.6 = (bf16[512,128]{1,0:T(8,128)(2,1)S(1)}, bf16[512,128]{1,0:T(8,128)(2,1)S(1)}, u32[]{:S(2)}, u32[]{:S(2)}) collective-permute-start(bf16[512,128]{1,0:T(8,128)(2,1)S(1)} %collective-permute-done.5.rest_6_), channel_id=1, source_target_pairs={{0,4},{4,0},{8,12},{12,8},{16,20},{20,16},{24,28},{28,24},{1,5},{5... | collective-permute-start | bytes 393224 | tf_op jit(solution)/shard_map/ppermute | solution.py:20
  27.2 5.0 %collective-permute-start.10 = (bf16[512,128]{1,0:T(8,128)(2,1)S(1)}, bf16[512,128]{1,0:T(8,128)(2,1)S(1)}, u32[]{:S(2)}, u32[]{:S(2)}) collective-permute-start(bf16[512,128]{1,0:T(8,128)(2,1)S(1)} %pad_maximum_fusion), channel_id=1, source_target_pairs={{0,8},{4,12},{8,0},{12,4},{16,24},{20,28},{24,16},{28,20},{1,9},{5... | collective-permute-start | bytes 393224 | tf_op jit(solution)/shard_map/ppermute | solution.py:20
  39.7 2.0 %collective-permute-start.11 = (bf16[2,256,512]{2,1,0:T(8,128)(2,1)S(1)}, bf16[2,256,512]{2,1,0:T(8,128)(2,1)S(1)}, u32[]{:S(2)}, u32[]{:S(2)}) collective-permute-start(bf16[2,256,512]{2,1,0:T(8,128)(2,1)S(1)} %get-tuple-element.26), channel_id=1, source_target_pairs={{0,1},{1,0},{2,3},{3,2},{4,5},{5,4},{6,7},{7,6},{8,9},{9,8},{10,11... | collective-permute-start | bytes 1572872 | tf_op jit(solution)/shard_map/ppermute | solution.py:20
  41.9 8.4 %collective-permute-start.12 = (bf16[1,256,512]{2,1,0:T(8,128)(2,1)S(1)}, bf16[1,256,512]{2,1,0:T(8,128)(2,1)S(1)}, u32[]{:S(2)}, u32[]{:S(2)}) collective-permute-start(bf16[1,256,512]{2,1,0:T(8,128)(2,1)S(1)} %slice.24), channel_id=1, source_target_pairs={{0,2},{1,3},{2,0},{3,1},{4,6},{5,7},{6,4},{7,5},{8,10},{9,11},{10,... | collective-permute-start | bytes 786440 | tf_op jit(solution)/shard_map/ppermute | solution.py:20

commit v3 on v0

v3 whole, which is shorter than its diff:
```python
import functools
import math

import jax
import jax.numpy as jnp
from jax import lax
from jax.experimental import pallas as pl
from jax.experimental.pallas import tpu as pltpu
from jax.sharding import PartitionSpec as P


PAGE = 128
LANES = 128
FAR = 1e30
STRIP = 16
PARTS = 2
TREE_MAX = 16


def swapped(value, axis, mask):
    count = lax.axis_size(axis)
    return lax.ppermute(value, axis, [(source, source ^ mask) for source in range(count)])


def passed_along(value, axis, steps):
    count = lax.axis_size(axis)
    return lax.ppermute(value, axis, [(source, (source + steps) % count) for source in range(count)])


def gathered(first_hops, axis):
    blocks = {}
    for mask in range(1, lax.axis_size(axis)):
        low = mask & -mask
        source = blocks[mask - low] if mask > low else first_hops[low]
        blocks[mask] = swapped(source, axis, low)
    return [blocks[mask] for mask in range(1, len(blocks) + 1)]


def rotate(value, amount, shards):
    reduced = amount % shards
    for bit_number in range(max(1, (shards - 1).bit_length())):
        moved = passed_along(value, "seq", 1 << bit_number)
        value = jnp.where(reduced // (1 << bit_number) % 2 == 1, moved, value)
    return value


def decoded(sizes, table, me):
    shards, per_shard = sizes["shards"], sizes["per_shard"]
    slash_count, page_count = sizes["slash_count"], sizes["page_count"]
    slashes, pages = [], []
    for k in range(slash_count):
        distance = table[0, page_count + k]
        older = distance > me
        source = jnp.where(older, shards + me - distance, me - distance)
        slashes.append((source ^ me, older, table[0, page_count + slash_count + k] == 1))
    for i in range(page_count):
        owner = table[0, i] // per_shard
        clash = functools.reduce(
            jnp.logical_or,
            [live & older & (bits == (owner ^ me)) for bits, older, live in slashes],
        )
        pages.append((owner ^ me, table[0, i] - owner * per_shard, jnp.logical_not(clash)))
    return slashes, pages


def open_kernel(sizes, own_in, cache_in, own_near, cache_near, *rest):
    shards, per_shard, piece = sizes["shards"], sizes["per_shard"], sizes["piece"]
    sems, half = rest[-1], shards // 2
    hop_count = shards.bit_length() - 1
    hops, pieces = rest[:hop_count], rest[hop_count:-1]
    copies = [
        pltpu.make_async_copy(own_in, own_near, sems.at[0]),
        pltpu.make_async_copy(cache_in, cache_near, sems.at[1]),
    ]
    for copy in copies:
        copy.start()
    for copy in copies:
        copy.wait()
    me = lax.axis_index("seq")
    for number, hop in enumerate(hops):
        upper = (me >> number) & 1

        @pl.when(upper == 0)
        def _(hop=hop):
            hop[...] = own_near[...]

        @pl.when(upper == 1)
        def _(hop=hop):
            hop[...] = cache_near[...]

    for mask, place in enumerate(pieces):
        for at in range(per_shard):
            first = (at * half + mask) * piece
            place[pl.ds(at * piece, piece), :] = cache_near[pl.ds(first, piece), :]


def load_table(sources, table, lists, sems):
    copies = [
        pltpu.make_async_copy(source, place, sems.at[at])
        for at, (source, place) in enumerate(zip(sources, lists))
    ]
    for copy in copies:
        copy.start()
    for copy in copies:
        copy.wait()
    at = 0
    for part in lists:
        for entry in range(part.shape[1]):
            table[0, at] = part[0, entry]
            at += 1


def table_kernel(page_in, shift_in, live_in, table, *rest):
    load_table((page_in, shift_in, live_in), table, rest[:3], rest[3])


def stage_kernel(query_in, query_near, sem):
    copy = pltpu.make_async_copy(query_in, query_near, sem)
    copy.start()
    copy.wait()


def pick_kernel(sizes, page_in, shift_in, live_in, *rest):
    pieces, slots, table = rest[:-6], rest[-6], rest[-5]
    load_table((page_in, shift_in, live_in), table, rest[-4:-1], rest[-1])
    piece = sizes["piece"]
    _, pages = decoded(sizes, table, lax.axis_index("seq"))
    for i, (bits, place, _) in enumerate(pages):
        for mask, source in enumerate(pieces):

            @pl.when((bits & (len(pieces) - 1)) == mask)
            def _(source=source):
                first = pl.multiple_of(place * piece, piece)
                slots[pl.ds(i * piece, piece), :] = source[pl.ds(first, piece), :]


def merge_kernel(sizes, table, mine, other, merged):
    piece = sizes["piece"]
    _, pages = decoded(sizes, table, lax.axis_index("seq"))
    for i, (bits, _, _) in enumerate(pages):
        here = pl.ds(i * piece, piece)
        far = bits >= sizes["shards"] // 2

        @pl.when(far)
        def _(here=here):
            merged[here, :] = other[here, :]

        @pl.when(jnp.logical_not(far))
        def _(here=here):
            merged[here, :] = mine[here, :]


def first_kernel(sizes, table, query_ref, proj_ref, own_ref, *rest):
    shards, head_width = sizes["shards"], sizes["head_width"]
    slash_count, page_count = sizes["slash_count"], sizes["page_count"]
    page_rows, tree = sizes["page_rows"], sizes["tree"]
    piece = sizes["piece"]
    block_count = shards if tree else slash_count
    piece_count = shards // 2 if tree else page_count
    half = shards // 2
    blocks = rest[:block_count]
    pieces = rest[block_count : block_count + piece_count]
    rest = rest[block_count + piece_count :]
    send_ref, keep_ref, keys, values, proj, wide, scores, weights, attended, proj_sem = rest
    proj_copy = pltpu.make_async_copy(proj_ref, proj, proj_sem)
    proj_copy.start()
    rows = own_ref.shape[0] // 2
    slashes, pages = decoded(sizes, table, lax.axis_index("seq"))
    wide[pl.ds(0, 2 * rows), :] = own_ref[...].astype(jnp.float32)
    spans = [(0, rows, None)]
    first = rows
    for k, (bits, _, live) in enumerate(slashes):
        here = pl.ds(2 * first, 2 * rows)
        if tree:
            for mask in range(shards):

                @pl.when(bits == mask)
                def _(mask=mask):
                    wide[here, :] = blocks[mask][...].astype(jnp.float32)
        else:
            wide[here, :] = blocks[k][...].astype(jnp.float32)
        spans.append((first, rows, live))
        first += rows
    for i, (bits, _, is_open) in enumerate(pages):
        if tree:
            for mask in range(half):
                at = pl.multiple_of(2 * first + ((mask ^ bits) & (half - 1)) * piece, piece)
                source = pieces[mask][pl.ds(i * piece, piece), :]
                wide[pl.ds(at, piece), :] = source.astype(jnp.float32)
        else:
            wide[pl.ds(2 * first, 2 * page_rows), :] = pieces[i][...].astype(jnp.float32)
        spans.append((first, page_rows, is_open))
        first += page_rows
    keys[:, pl.ds(0, head_width)] = wide[pl.ds(0, first, stride=2), :].astype(jnp.bfloat16)
    values[:, pl.ds(0, head_width)] = wide[pl.ds(1, first, stride=2), :].astype(jnp.bfloat16)
    values[:, pl.ds(head_width, LANES)] = jnp.ones((first, LANES), jnp.bfloat16)
    for first, count, flag in spans:
        added = 0.0 if flag is None else jnp.where(flag, 0.0, -FAR)
        lanes = lax.broadcasted_iota(jnp.int32, (count, LANES), 1)
        keys[pl.ds(first, count), pl.ds(head_width, LANES)] = jnp.where(
            lanes == 0, added, 0.0
        ).astype(jnp.bfloat16)
    attend_rows(
        sizes, 0, query_ref, keys, values, scores, weights, attended
    )
    proj_copy.wait()
    project(sizes, attended, proj, send_ref, keep_ref)


def second_kernel(sizes, query_ref, keys, values, proj, send_ref, keep_ref, *scratch):
    scores, weights, attended = scratch
    attend_rows(sizes, 1, query_ref, keys, values, scores, weights, attended)
    project(sizes, attended, proj, send_ref, keep_ref)


def project(sizes, attended, proj, send_ref, keep_ref):
    members = sizes["members"]
    mine = lax.axis_index("head")
    block = proj.shape[1] // members
    for mask in range(members):
        column = pl.multiple_of((mine ^ mask) * block, block)
        term = jnp.dot(
            attended[...], proj[:, pl.ds(column, block)], preferred_element_type=jnp.float32
        )
        if mask % 2:
            send_ref[mask // 2] = term.astype(send_ref.dtype)
        else:
            keep_ref[mask // 2] = term


def attend_rows(sizes, part, query_ref, keys, values, scores, weights, attended):
    heads, head_width = sizes["heads"], sizes["head_width"]
    rows, part_rows, total_keys = query_ref.shape[0], attended.shape[0], keys.shape[0]
    group = rows // part_rows
    tile_count = heads // group
    one = (lax.broadcasted_iota(jnp.int32, (rows, LANES), 1) == 0).astype(jnp.bfloat16)
    scale = head_width**-0.5 * math.log2(math.e)
    starts = list(range(0, total_keys, rows))
    strips = list(range(0, rows, STRIP))

    def columns(tile, place):
        return pl.ds((tile * group + place) * head_width, head_width)

    def score(tile, start):
        query = jnp.concatenate(
            [query_ref[pl.ds(part * part_rows, part_rows), columns(tile, j)] for j in range(group)], 0
        )
        here = pl.ds(start, min(rows, total_keys - start))
        scores[tile % 2, :, here] = lax.dot_general(
            jnp.concatenate([query, one], 1),
            keys[here, :],
            (((1,), (1,)), ((), ())),
            preferred_element_type=jnp.float32,
        )

    def weigh(tile, top):
        here = pl.ds(top, STRIP)
        local = part * part_rows + top % part_rows
        diagonal = local // LANES
        row = lax.broadcasted_iota(jnp.int32, (STRIP, LANES), 0) + (local - diagonal * LANES)
        causal = row >= lax.broadcasted_iota(jnp.int32, (STRIP, LANES), 1)
        hidden = range((diagonal + 1) * LANES, rows, LANES)
        tiles = {}
        for at in range(0, total_keys, LANES):
            if at not in hidden:
                tiles[at] = scores[tile % 2, here, pl.ds(at, LANES)]
        tiles[diagonal * LANES] = jnp.where(causal, tiles[diagonal * LANES], -FAR)
        highest = jnp.max(functools.reduce(jnp.maximum, tiles.values()), axis=1, keepdims=True)
        for at, entry in tiles.items():
            weights[tile % 2, here, pl.ds(at, LANES)] = jnp.exp2((entry - highest) * scale).astype(
                jnp.bfloat16
            )
        for at in hidden:
            weights[tile % 2, here, pl.ds(at, LANES)] = jnp.zeros((STRIP, LANES), jnp.bfloat16)

    for start in starts:
        score(0, start)
    for tile in range(tile_count):
        for number, start in enumerate(starts):
            if tile + 1 < tile_count:
                score(tile + 1, start)
            low, high = (len(strips) * (number + more) // len(starts) for more in (0, 1))
            for top in strips[low:high]:
                weigh(tile, top)
        total = jnp.dot(weights[tile % 2], values[...], preferred_element_type=jnp.float32)
        mixed = (total[:, :head_width] / total[:, head_width:]).astype(jnp.bfloat16)
        for j in range(group):
            attended[:, columns(tile, j)] = mixed[j * part_rows : (j + 1) * part_rows]


def body(queries, keys_values, cache_kv, vertical_pages, slash_shift, slash_live, out_proj):
    row_count = queries.shape[0]
    head_width = keys_values.shape[2]
    heads = queries.shape[1] // head_width
    shards = lax.axis_size("seq")
    members = lax.axis_size("head")
    slash_count = slash_shift.shape[1]
    page_count = vertical_pages.shape[1]
    per_shard = row_count // PAGE
    out_width = out_proj.shape[1]
    own = keys_values.reshape(2 * row_count, head_width)
    cache = cache_kv.reshape(2 * row_count, head_width)
    tree = is_tree(shards)
    piece = 2 * PAGE // (shards // 2) if tree else 0
    sizes = dict(
        shards=shards, heads=heads, head_width=head_width, slash_count=slash_count,
        page_count=page_count, page_rows=PAGE, per_shard=per_shard, members=members, tree=tree,
        piece=piece,
    )
    scalars = pl.BlockSpec(memory_space=pltpu.SMEM)
    vector = pl.BlockSpec(memory_space=pltpu.VMEM)
    hbm = pl.BlockSpec(memory_space=pltpu.HBM)
    far = functools.partial(pltpu.with_memory_space_constraint, memory_space=pltpu.HBM)
    lists = [vertical_pages, slash_shift, slash_live.reshape(1, slash_count)]
    table_size = sum(part.shape[1] for part in lists)
    queries = pl.pallas_call(
        stage_kernel,
        out_shape=jax.ShapeDtypeStruct(queries.shape, queries.dtype),
        in_specs=[hbm],
        out_specs=vector,
        scratch_shapes=[pltpu.SemaphoreType.DMA],
        compiler_params=pltpu.CompilerParams(vmem_limit_bytes=1 << 20),
        cost_estimate=pl.CostEstimate(flops=0, bytes_accessed=2 << 20, transcendentals=0),
        name="stage",
    )(far(queries))
    table_shape = jax.ShapeDtypeStruct((1, table_size), jnp.int32)
    list_scratch = [pltpu.SMEM(part.shape, jnp.int32) for part in lists]
    list_scratch.append(pltpu.SemaphoreType.DMA((3,)))
    own_shard = lax.axis_index("seq")
    if tree:
        half = shards // 2
        bits = [1 << number for number in range(shards.bit_length() - 1)]
        block_shape = jax.ShapeDtypeStruct(own.shape, own.dtype)
        piece_rows = per_shard * piece
        piece_shape = jax.ShapeDtypeStruct((piece_rows, head_width), own.dtype)
        opened = pl.pallas_call(
            functools.partial(open_kernel, sizes),
            out_shape=[block_shape] * (2 + len(bits)) + [piece_shape] * half,
            in_specs=[hbm] * 2,
            out_specs=[vector] * (2 + len(bits) + half),
            scratch_shapes=[pltpu.SemaphoreType.DMA((2,))],
            compiler_params=pltpu.CompilerParams(vmem_limit_bytes=1 << 20),
            cost_estimate=pl.CostEstimate(flops=0, bytes_accessed=1 << 20, transcendentals=0),
            name="open",
        )(far(own), far(cache))
        own, cache = opened[:2]
        near = opened[2 + len(bits) :]
        first_hops = dict(zip(bits, opened[2 : 2 + len(bits)]))
        blocks = [cache] + gathered(first_hops, "seq")
        pieces = [near[0]] + [swapped(near[mask], "seq", mask) for mask in range(1, half)]
        slot_shape = jax.ShapeDtypeStruct((page_count * piece, head_width), jnp.bfloat16)
        small = dict(
            compiler_params=pltpu.CompilerParams(vmem_limit_bytes=2 << 20),
            cost_estimate=pl.CostEstimate(flops=0, bytes_accessed=4 << 20, transcendentals=0),
        )
        mine, table = pl.pallas_call(
            functools.partial(pick_kernel, sizes),
            out_shape=[slot_shape, table_shape],
            in_specs=[hbm] * 3 + [vector] * len(pieces),
            out_specs=[vector, scalars],
            scratch_shapes=list_scratch,
            name="pick",
            **small,
        )(*map(far, lists), *pieces)
        merged = pl.pallas_call(
            functools.partial(merge_kernel, sizes),
            out_shape=slot_shape,
            in_specs=[scalars, vector, vector],
            out_specs=vector,
            name="merge",
            **small,
        )(table, mine, swapped(mine, "seq", half))
        pieces = {0: merged}
        for mask in range(1, half):
            top = 1 << (mask.bit_length() - 1)
            pieces[mask] = swapped(pieces[mask - top], "seq", top)
        pieces = list(pieces.values())
    else:
        table = pl.pallas_call(
            table_kernel,
            out_shape=table_shape,
            in_specs=[hbm] * 3,
            out_specs=scalars,
            scratch_shapes=list_scratch,
            name="table",
        )(*map(far, lists))
        blocks, pieces = [], []
        for k in range(slash_count):
            distance = slash_shift[0, k]
            payload = jnp.where(own_shard < shards - distance, keys_values, cache_kv)
            blocks.append(rotate(payload, distance, shards).reshape(2 * row_count, head_width))
        whole = lax.all_gather(cache_kv, "seq", axis=0, tiled=True)
        for i in range(page_count):
            page = lax.dynamic_slice_in_dim(whole, vertical_pages[0, i] * PAGE, PAGE, 0)
            pieces.append(page.reshape(2 * PAGE, head_width))
    key_count = (1 + slash_count) * row_count + page_count * PAGE
    block = out_width // members
    part_rows = row_count // PARTS
    term_shapes = [
        jax.ShapeDtypeStruct((members // 2, part_rows, block), jnp.bfloat16),
        jax.ShapeDtypeStruct((members // 2, part_rows, block), jnp.float32),
    ]
    wide_shape = jax.ShapeDtypeStruct((key_count, head_width + LANES), jnp.bfloat16)
    scratch = [
        pltpu.VMEM((2, row_count, key_count), jnp.float32),
        pltpu.VMEM((2, row_count, key_count), jnp.bfloat16),
        pltpu.VMEM((part_rows, heads * head_width), jnp.bfloat16),
    ]
    settings = dict(
        compiler_params=pltpu.CompilerParams(vmem_limit_bytes=24 << 20),
        cost_estimate=pl.CostEstimate(
            flops=2 * heads * row_count * key_count * head_width
            + row_count * heads * head_width * out_width,
            bytes_accessed=8 << 20,
            transcendentals=heads * row_count * key_count // 2,
        ),
    )
    send, keep, keys, values, proj = pl.pallas_call(
        functools.partial(first_kernel, sizes),
        out_shape=term_shapes
        + [wide_shape] * 2
        + [jax.ShapeDtypeStruct(out_proj.shape, out_proj.dtype)],
        in_specs=[scalars, vector, hbm] + [vector] * (1 + len(blocks) + len(pieces)),
        out_specs=[vector] * 5,
        scratch_shapes=[pltpu.VMEM((2 * key_count, head_width), jnp.float32)]
        + scratch
        + [pltpu.SemaphoreType.DMA],
        name="first",
        **settings,
    )(table, queries, far(out_proj), own, *blocks, *pieces)
    terms = [(send, keep)]
    terms.append(
        pl.pallas_call(
            functools.partial(second_kernel, sizes),
            out_shape=term_shapes,
            in_specs=[vector] * 4,
            out_specs=[vector] * 2,
            scratch_shapes=scratch,
            name="second",
            **settings,
        )(queries, keys, values, proj)
    )
    parts = []
    for send, keep in terms:
        step = 1
        while step < members:
            keep = keep + swapped(send, "head", step).astype(jnp.float32)
            step *= 2
            if step < members:
                send = keep[1::2].astype(jnp.bfloat16)
                keep = keep[0::2]
        parts.append(keep[0].astype(jnp.bfloat16))
    return jnp.concatenate(parts, 0)


def is_tree(shards):
    return 4 <= shards <= TREE_MAX and shards & (shards - 1) == 0


def solution(mesh):
    placed = (
        P("seq", "head"),
        P("seq", None, "head"),
        P("seq", None, "head"),
        P("head", None),
        P("head", None),
        P("seq", "head", None),
        P("head", None),
    )


    step = jax.shard_map(
        body, mesh=mesh, in_specs=placed, out_specs=P("seq", "head"), check_vma=False
    )
    if not is_tree(mesh.shape["seq"]):
        return step
    return step
```

time: 57.9 us -> 57 us (0.984)
  waiting for transfers between devices: 25.9 us -> 22.7 us
  starting transfers between devices: 19.4 us -> 21.1 us
  Pallas kernels: 11.4 us -> 12 us
    ppermute x16 -> x18, waiting for transfers between devices: 25.9 us -> 22.7 us  [swapped(): lax.ppermute(value, axis, [(source, source ^ mask) for source in range(co...]
    ppermute x16 -> x18, starting transfers between devices: 19.4 us -> 21.1 us  [swapped(): lax.ppermute(value, axis, [(source, source ^ mask) for source in range(co...]
    convert_element_type x1 -> x2, other arithmetic: 0.78 us -> 0.05 us  [body(): parts.append(keep[0].astype(jnp.bfloat16))]
    concatenate x0 -> x1, other arithmetic: none -> 0.72 us  [body(): return jnp.concatenate(parts, 0)]
    pallas_call x4 -> x5, Pallas kernels: 10.4 us -> 10.9 us  [the longest x1 4.4 us: body(): pl.pallas_call(functools.partial(first_kernel, sizes), out_shape=term_sha...]
  transfers between devices with their start and end apart: 16 -> 18, of which waited for: 8 -> 12; matrix products, arithmetic and copies ran while one was open for 0% -> 0% of each run, Pallas kernels for 5% -> 5%
where the time goes in v3:
time: 57 us; the launch traced here: 56.8 us
  waiting for transfers between devices  22.7 us (40%)
  starting transfers between devices  21.1 us (37%)
  Pallas kernels  12 us (21%)
  other arithmetic  0.92 us (2%)
    ppermute x18, waiting for transfers between devices, swapped(): lax.ppermute(value, axis, [(source, source ^ mask) for source in range(co...  22.7 us
    ppermute x18, starting transfers between devices, swapped(): lax.ppermute(value, axis, [(source, source ^ mask) for source in range(co...  21.1 us
    pallas_call x1, Pallas kernels, body(): pl.pallas_call(functools.partial(first_kernel, sizes), out_shape=term_sha...  4.4 us
    pallas_call x1, Pallas kernels, body(): pl.pallas_call(functools.partial(second_kernel, sizes), out_shape=term_sh...  3.47 us
    pallas_call x1, Pallas kernels, body(): pl.pallas_call(functools.partial(pick_kernel, sizes), out_shape=[slot_sha...  1.41 us
  transfers between devices with their start and end apart: 18, of which 12 were waited for; matrix products, arithmetic and copies ran while one was open for 0% of the time, Pallas kernels for 5%

profile of v3, /device:TPU:0, one launch (start us, length us, event | category | flops | bytes accessed | tf_op | source)
XLA Modules:
  0.0 56.8 jit_solution(6463135835660744572)
XLA Ops:
  0.0 1.0 %open.1 = (bf16[512,128]{1,0:T(8,128)(2,1)S(1)}, bf16[512,128]{1,0:T(8,128)(2,1)S(1)}, bf16[512,128]{1,0:T(8,128)(2,1)S(1)}, bf16[512,128]{1,0:T(8,128)(2,1)S(1)...) custom-call(bf16[512,128]{1,0:T(8,128)(2,1)} %bitcast.7, ...), custom_call_target="tpu_custom_call" | custom-call | bytes 1048576 | tf_op jit(solution)/shard_map/open/pallas_call | solution.py:336
  1.0 4.1 %collective-permute-start.6 = (bf16[512,128]{1,0:T(8,128)(2,1)S(1)}, bf16[512,128]{1,0:T(8,128)(2,1)S(1)}, u32[]{:S(2)}, u32[]{:S(2)}) collective-permute-start(bf16[512,128]{1,0:T(8,128)(2,1)S(1)} %get-tuple-element.32), channel_id=1, source_target_pairs={{0,16},{4,20},{8,24},{12,28},{16,0},{20,4},{24,8},{28,12},{1,17},{... | collective-permute-start | bytes 393224 | tf_op jit(solution)/shard_map/ppermute | solution.py:22
  5.2 1.6 %collective-permute-start.4 = (bf16[512,128]{1,0:T(8,128)(2,1)S(1)}, bf16[512,128]{1,0:T(8,128)(2,1)S(1)}, u32[]{:S(2)}, u32[]{:S(2)}) collective-permute-start(bf16[512,128]{1,0:T(8,128)(2,1)S(1)} %get-tuple-element.31), channel_id=1, source_target_pairs={{0,8},{4,12},{8,0},{12,4},{16,24},{20,28},{24,16},{28,20},{1,9},{5... | collective-permute-start | bytes 393224 | tf_op jit(solution)/shard_map/ppermute | solution.py:22
  6.7 4.8 %collective-permute-done.6.rest_4_ = bf16[512,128]{1,0:T(8,128)(2,1)S(1)} collective-permute-done((bf16[512,128]{1,0:T(8,128)(2,1)S(1)}, bf16[512,128]{1,0:T(8,128)(2,1)S(1)}, u32[]{:S(2)}, u32[]{:S(2)}) %collective-permute-start.6) | collective-permute-done | bytes 131104 | tf_op jit(solution)/shard_map/ppermute | solution.py:22
  11.6 0.6 %collective-permute-start.8 = (bf16[512,128]{1,0:T(8,128)(2,1)S(1)}, bf16[512,128]{1,0:T(8,128)(2,1)S(1)}, u32[]{:S(2)}, u32[]{:S(2)}) collective-permute-start(bf16[512,128]{1,0:T(8,128)(2,1)S(1)} %collective-permute-done.6.rest_4_), channel_id=1, source_target_pairs={{0,8},{4,12},{8,0},{12,4},{16,24},{20,28},{24,16},{28,20},{1,9},{5... | collective-permute-start | bytes 393224 | tf_op jit(solution)/shard_map/ppermute | solution.py:22
  12.2 1.5 %collective-permute-start = (bf16[128,128]{1,0:T(8,128)(2,1)S(1)}, bf16[128,128]{1,0:T(8,128)(2,1)S(1)}, u32[]{:S(2)}, u32[]{:S(2)}) collective-permute-start(bf16[128,128]{1,0:T(8,128)(2,1)S(1)} %get-tuple-element.24), channel_id=1, source_target_pairs={{0,4},{4,0},{8,12},{12,8},{16,20},{20,16},{24,28},{28,24},{1,5},{5... | collective-permute-start | bytes 98312 | tf_op jit(solution)/shard_map/ppermute | solution.py:22
  13.7 1.5 %collective-permute-start.1 = (bf16[128,128]{1,0:T(8,128)(2,1)S(1)}, bf16[128,128]{1,0:T(8,128)(2,1)S(1)}, u32[]{:S(2)}, u32[]{:S(2)}) collective-permute-start(bf16[128,128]{1,0:T(8,128)(2,1)S(1)} %get-tuple-element.25), channel_id=1, source_target_pairs={{0,8},{4,12},{8,0},{12,4},{16,24},{20,28},{24,16},{28,20},{1,9},{5... | collective-permute-start | bytes 98312 | tf_op jit(solution)/shard_map/ppermute | solution.py:22
  15.1 0.5 collective-permute-start.2
  15.7 0.4 collective-permute-done.rest_1_
  16.1 1.5 %collective-permute-done.1.rest_2_ = bf16[128,128]{1,0:T(8,128)(2,1)S(1)} collective-permute-done((bf16[128,128]{1,0:T(8,128)(2,1)S(1)}, bf16[128,128]{1,0:T(8,128)(2,1)S(1)}, u32[]{:S(2)}, u32[]{:S(2)}) %collective-permute-start.1) | collective-permute-done | bytes 32800 | tf_op jit(solution)/shard_map/ppermute | solution.py:22
  17.6 2.4 %collective-permute-done.2.rest_3_ = bf16[128,128]{1,0:T(8,128)(2,1)S(1)} collective-permute-done((bf16[128,128]{1,0:T(8,128)(2,1)S(1)}, bf16[128,128]{1,0:T(8,128)(2,1)S(1)}, u32[]{:S(2)}, u32[]{:S(2)}) %collective-permute-start.2) | collective-permute-done | bytes 32800 | tf_op jit(solution)/shard_map/ppermute | solution.py:22
  20.0 1.4 %pick.1 = (bf16[256,128]{1,0:T(8,128)(2,1)S(1)}, s32[1,10]{1,0:T(1,128)S(1)}) custom-call(s32[1,4]{1,0:T(1,128)} %page_in.1, s32[1,3]{1,0:T(1,128)} %shift_in.1, s32[1,3]{1,0:T(1,128)} %bitcast.9, bf16[128,128]{1,0:T(8,128)(2,1)S(1)} %get-tuple-element.23.rest_0_, bf16[128,128]{1,0:T(8,128)(2,1)S(1)} %collective-permute-done.rest_1_, ...), custom_call_target="tpu_custom_call" | custom-call | bytes 4194304 | tf_op jit(solution)/shard_map/pick/pallas_call | solution.py:356
  21.4 2.0 %collective-permute-start.10 = (bf16[256,128]{1,0:T(8,128)(2,1)S(1)}, bf16[256,128]{1,0:T(8,128)(2,1)S(1)}, u32[]{:S(2)}, u32[]{:S(2)}) collective-permute-start(bf16[256,128]{1,0:T(8,128)(2,1)S(1)} %get-tuple-element.33.mine), channel_id=1, source_target_pairs={{0,16},{4,20},{8,24},{12,28},{16,0},{20,4},{24,8},{28,12},{1,17},{... | collective-permute-start | bytes 196616 | tf_op jit(solution)/shard_map/ppermute | solution.py:22
  23.4 0.9 %collective-permute-start.3 = (bf16[512,128]{1,0:T(8,128)(2,1)S(1)}, bf16[512,128]{1,0:T(8,128)(2,1)S(1)}, u32[]{:S(2)}, u32[]{:S(2)}) collective-permute-start(bf16[512,128]{1,0:T(8,128)(2,1)S(1)} %get-tuple-element.30), channel_id=1, source_target_pairs={{0,4},{4,0},{8,12},{12,8},{16,20},{20,16},{24,28},{28,24},{1,5},{5... | collective-permute-start | bytes 393224 | tf_op jit(solution)/shard_map/ppermute | solution.py:22
  24.3 3.0 %collective-permute-done.10.other = bf16[256,128]{1,0:T(8,128)(2,1)S(1)} collective-permute-done((bf16[256,128]{1,0:T(8,128)(2,1)S(1)}, bf16[256,128]{1,0:T(8,128)(2,1)S(1)}, u32[]{:S(2)}, u32[]{:S(2)}) %collective-permute-start.10) | collective-permute-done | bytes 65568 | tf_op jit(solution)/shard_map/ppermute | solution.py:22
  27.3 0.6 %merge.1.rest_8_ = bf16[256,128]{1,0:T(8,128)(2,1)S(1)} custom-call(s32[1,10]{1,0:T(1,128)S(1)} %get-tuple-element.27.table, bf16[256,128]{1,0:T(8,128)(2,1)S(1)} %get-tuple-element.33.mine, bf16[256,128]{1,0:T(8,128)(2,1)S(1)} %collective-permute-done.10.other), custom_call_target="tpu_custom_call" | custom-call | bytes 4194304 | tf_op jit(solution)/shard_map/merge/pallas_call | solution.py:365
  27.9 0.6 collective-permute-start.11
  28.5 1.5 %collective-permute-start.7 = (bf16[512,128]{1,0:T(8,128)(2,1)S(1)}, bf16[512,128]{1,0:T(8,128)(2,1)S(1)}, u32[]{:S(2)}, u32[]{:S(2)}) collective-permute-start(bf16[512,128]{1,0:T(8,128)(2,1)S(1)} %collective-permute-done.6.rest_4_), channel_id=1, source_target_pairs={{0,4},{4,0},{8,12},{12,8},{16,20},{20,16},{24,28},{28,24},{1,5},{5... | collective-permute-start | bytes 393224 | tf_op jit(solution)/shard_map/ppermute | solution.py:22
  30.0 0.0 collective-permute-done.4.rest_2_
  30.0 0.5 collective-permute-start.5
  30.5 0.0 collective-permute-done.8.rest_6_
  30.5 1.5 %collective-permute-start.9 = (bf16[512,128]{1,0:T(8,128)(2,1)S(1)}, bf16[512,128]{1,0:T(8,128)(2,1)S(1)}, u32[]{:S(2)}, u32[]{:S(2)}) collective-permute-start(bf16[512,128]{1,0:T(8,128)(2,1)S(1)} %collective-permute-done.8.rest_6_), channel_id=1, source_target_pairs={{0,4},{4,0},{8,12},{12,8},{16,20},{20,16},{24,28},{28,24},{1,5},{5... | collective-permute-start | bytes 393224 | tf_op jit(solution)/shard_map/ppermute | solution.py:22
  32.0 0.0 collective-permute-done.3.rest_1_
  32.0 0.4 collective-permute-start.12
  32.5 0.5 collective-permute-done.11.rest_9_
  32.9 1.1 %collective-permute-start.13 = (bf16[256,128]{1,0:T(8,128)(2,1)S(1)}, bf16[256,128]{1,0:T(8,128)(2,1)S(1)}, u32[]{:S(2)}, u32[]{:S(2)}) collective-permute-start(bf16[256,128]{1,0:T(8,128)(2,1)S(1)} %collective-permute-done.11.rest_9_), channel_id=1, source_target_pairs={{0,8},{4,12},{8,0},{12,4},{16,24},{20,28},{24,16},{28,20},{1,9},{5... | collective-permute-start | bytes 196616 | tf_op jit(solution)/shard_map/ppermute | solution.py:22
  34.1 1.0 %stage.1.query_ref = bf16[256,1024]{1,0:T(8,128)(2,1)S(1)} custom-call(bf16[256,1024]{1,0:T(8,128)(2,1)} %query_in.1), custom_call_target="tpu_custom_call" | custom-call | bytes 2097152 | tf_op jit(solution)/shard_map/stage/pallas_call | solution.py:316
  35.1 1.2 %collective-permute-done.12.rest_10_ = bf16[256,128]{1,0:T(8,128)(2,1)S(1)} collective-permute-done((bf16[256,128]{1,0:T(8,128)(2,1)S(1)}, bf16[256,128]{1,0:T(8,128)(2,1)S(1)}, u32[]{:S(2)}, u32[]{:S(2)}) %collective-permute-start.12) | collective-permute-done | bytes 65568 | tf_op jit(solution)/shard_map/ppermute | solution.py:22
  36.3 0.9 %collective-permute-done.13.rest_11_ = bf16[256,128]{1,0:T(8,128)(2,1)S(1)} collective-permute-done((bf16[256,128]{1,0:T(8,128)(2,1)S(1)}, bf16[256,128]{1,0:T(8,128)(2,1)S(1)}, u32[]{:S(2)}, u32[]{:S(2)}) %collective-permute-start.13) | collective-permute-done | bytes 65568 | tf_op jit(solution)/shard_map/ppermute | solution.py:22
  37.2 0.0 collective-permute-done.5.rest_3_
  37.2 0.0 collective-permute-done.7.rest_5_
  37.2 0.9 %collective-permute-done.9.rest_7_ = bf16[512,128]{1,0:T(8,128)(2,1)S(1)} collective-permute-done((bf16[512,128]{1,0:T(8,128)(2,1)S(1)}, bf16[512,128]{1,0:T(8,128)(2,1)S(1)}, u32[]{:S(2)}, u32[]{:S(2)}) %collective-permute-start.9) | collective-permute-done | bytes 131104 | tf_op jit(solution)/shard_map/ppermute | solution.py:22
  38.1 4.4 %first.1 = (bf16[2,128,512]{2,1,0:T(8,128)(2,1)S(1)}, f32[2,128,512]{2,1,0:T(8,128)S(1)}, bf16[1536,256]{1,0:T(8,128)(2,1)S(1)}, bf16[1536,256]{1,0:T(8,128)(2,1)S(1)}, bf16[1024,2048]{1,0:T(8,128)(2,1)S(1)}) custom-call(s32[1,10]{1,0:T(1,128)S(1)} %get-tuple-element.27.table, bf16[256,1024]{1,0:T(8,128)(2,1)S(1)} %stage.1.query_ref, ...), custom_call_target="tpu_custom_call" | custom-call | flops 1342177280 | bytes 8388608 | tf_op jit(solution)/shard_map/first/pallas_call | solution.py:418
  42.5 3.5 %second.1 = (bf16[2,128,512]{2,1,0:T(8,128)(2,1)S(1)}, f32[2,128,512]{2,1,0:T(8,128)S(1)}) custom-call(bf16[256,1024]{1,0:T(8,128)(2,1)S(1)} %stage.1.query_ref, bf16[1536,256]{1,0:T(8,128)(2,1)S(1)} %get-tuple-element.36.keys, bf16[1536,256]{1,0:T(8,128)(2,1)S(1)} %get-tuple-element.37.values, bf16[1024,2048]{1,0:T(8,128)(2,1)S(1)} %get-tuple-element.38.proj), custom_call_target="tpu_custom_call" | custom-call | flops 1342177280 | bytes 8388608 | tf_op jit(solution)/shard_map/second/pallas_call | solution.py:433
  46.0 0.1 collective-permute-start.16
  46.1 0.5 collective-permute-start.14
  46.5 1.0 %collective-permute-done.16 = bf16[2,128,512]{2,1,0:T(8,128)(2,1)S(1)} collective-permute-done((bf16[2,128,512]{2,1,0:T(8,128)(2,1)S(1)}, bf16[2,128,512]{2,1,0:T(8,128)(2,1)S(1)}, u32[]{:S(2)}, u32[]{:S(2)}) %collective-permute-start.16) | collective-permute-done | bytes 262176 | tf_op jit(solution)/shard_map/ppermute | solution.py:22
  47.6 0.1 convert_add_fusion
  47.7 1.6 %collective-permute-start.17 = (bf16[1,128,512]{2,1,0:T(8,128)(2,1)S(1)}, bf16[1,128,512]{2,1,0:T(8,128)(2,1)S(1)}, u32[]{:S(2)}, u32[]{:S(2)}) collective-permute-start(bf16[1,128,512]{2,1,0:T(8,128)(2,1)S(1)} %slice.38), channel_id=1, source_target_pairs={{0,2},{1,3},{2,0},{3,1},{4,6},{5,7},{6,4},{7,5},{8,10},{9,11},{10,... | collective-permute-start | bytes 393224 | tf_op jit(solution)/shard_map/ppermute | solution.py:22
  49.3 0.0 collective-permute-done.14
  49.3 0.1 convert_add_fusion.1
  49.4 0.6 %collective-permute-start.15 = (bf16[1,128,512]{2,1,0:T(8,128)(2,1)S(1)}, bf16[1,128,512]{2,1,0:T(8,128)(2,1)S(1)}, u32[]{:S(2)}, u32[]{:S(2)}) collective-permute-start(bf16[1,128,512]{2,1,0:T(8,128)(2,1)S(1)} %slice.39), channel_id=1, source_target_pairs={{0,2},{1,3},{2,0},{3,1},{4,6},{5,7},{6,4},{7,5},{8,10},{9,11},{10,... | collective-permute-start | bytes 393224 | tf_op jit(solution)/shard_map/ppermute | solution.py:22
  49.9 4.2 %collective-permute-done.17 = bf16[1,128,512]{2,1,0:T(8,128)(2,1)S(1)} collective-permute-done((bf16[1,128,512]{2,1,0:T(8,128)(2,1)S(1)}, bf16[1,128,512]{2,1,0:T(8,128)(2,1)S(1)}, u32[]{:S(2)}, u32[]{:S(2)}) %collective-permute-start.17) | collective-permute-done | bytes 131104 | tf_op jit(solution)/shard_map/ppermute | solution.py:22
  54.1 1.9 %collective-permute-done.15 = bf16[1,128,512]{2,1,0:T(8,128)(2,1)S(1)} collective-permute-done((bf16[1,128,512]{2,1,0:T(8,128)(2,1)S(1)}, bf16[1,128,512]{2,1,0:T(8,128)(2,1)S(1)}, u32[]{:S(2)}, u32[]{:S(2)}) %collective-permute-start.15) | collective-permute-done | bytes 131104 | tf_op jit(solution)/shard_map/ppermute | solution.py:22
  56.1 0.7 %pad_maximum_fusion = bf16[256,512]{1,0:T(8,128)(2,1)} fusion(bf16[128,512]{1,0:T(8,128)(2,1)S(1)} %fusion.3, bf16[128,512]{1,0:T(8,128)(2,1)S(1)} %fusion.2), kind=kLoop, calls=%fused_computation.8 | loop fusion | flops 524288 | bytes 524288 | tf_op jit(solution)/shard_map/concatenate | solution.py:453
  (4 shorter events, 0.1 us)
Async XLA Ops:
  1.0 10.5 %collective-permute-start.6 = (bf16[512,128]{1,0:T(8,128)(2,1)S(1)}, bf16[512,128]{1,0:T(8,128)(2,1)S(1)}, u32[]{:S(2)}, u32[]{:S(2)}) collective-permute-start(bf16[512,128]{1,0:T(8,128)(2,1)S(1)} %get-tuple-element.32), channel_id=1, source_target_pairs={{0,16},{4,20},{8,24},{12,28},{16,0},{20,4},{24,8},{28,12},{1,17},{... | collective-permute-start | bytes 393224 | tf_op jit(solution)/shard_map/ppermute | solution.py:22
  5.2 24.8 %collective-permute-start.4 = (bf16[512,128]{1,0:T(8,128)(2,1)S(1)}, bf16[512,128]{1,0:T(8,128)(2,1)S(1)}, u32[]{:S(2)}, u32[]{:S(2)}) collective-permute-start(bf16[512,128]{1,0:T(8,128)(2,1)S(1)} %get-tuple-element.31), channel_id=1, source_target_pairs={{0,8},{4,12},{8,0},{12,4},{16,24},{20,28},{24,16},{28,20},{1,9},{5... | collective-permute-start | bytes 393224 | tf_op jit(solution)/shard_map/ppermute | solution.py:22
  11.6 18.9 %collective-permute-start.8 = (bf16[512,128]{1,0:T(8,128)(2,1)S(1)}, bf16[512,128]{1,0:T(8,128)(2,1)S(1)}, u32[]{:S(2)}, u32[]{:S(2)}) collective-permute-start(bf16[512,128]{1,0:T(8,128)(2,1)S(1)} %collective-permute-done.6.rest_4_), channel_id=1, source_target_pairs={{0,8},{4,12},{8,0},{12,4},{16,24},{20,28},{24,16},{28,20},{1,9},{5... | collective-permute-start | bytes 393224 | tf_op jit(solution)/shard_map/ppermute | solution.py:22
  12.2 3.9 %collective-permute-start = (bf16[128,128]{1,0:T(8,128)(2,1)S(1)}, bf16[128,128]{1,0:T(8,128)(2,1)S(1)}, u32[]{:S(2)}, u32[]{:S(2)}) collective-permute-start(bf16[128,128]{1,0:T(8,128)(2,1)S(1)} %get-tuple-element.24), channel_id=1, source_target_pairs={{0,4},{4,0},{8,12},{12,8},{16,20},{20,16},{24,28},{28,24},{1,5},{5... | collective-permute-start | bytes 98312 | tf_op jit(solution)/shard_map/ppermute | solution.py:22
  13.7 3.9 %collective-permute-start.1 = (bf16[128,128]{1,0:T(8,128)(2,1)S(1)}, bf16[128,128]{1,0:T(8,128)(2,1)S(1)}, u32[]{:S(2)}, u32[]{:S(2)}) collective-permute-start(bf16[128,128]{1,0:T(8,128)(2,1)S(1)} %get-tuple-element.25), channel_id=1, source_target_pairs={{0,8},{4,12},{8,0},{12,4},{16,24},{20,28},{24,16},{28,20},{1,9},{5... | collective-permute-start | bytes 98312 | tf_op jit(solution)/shard_map/ppermute | solution.py:22
  15.1 4.8 %collective-permute-start.2 = (bf16[128,128]{1,0:T(8,128)(2,1)S(1)}, bf16[128,128]{1,0:T(8,128)(2,1)S(1)}, u32[]{:S(2)}, u32[]{:S(2)}) collective-permute-start(bf16[128,128]{1,0:T(8,128)(2,1)S(1)} %get-tuple-element.26), channel_id=1, source_target_pairs={{0,12},{4,8},{8,4},{12,0},{16,28},{20,24},{24,20},{28,16},{1,13},{... | collective-permute-start | bytes 98312 | tf_op jit(solution)/shard_map/ppermute | solution.py:22
  21.4 5.9 %collective-permute-start.10 = (bf16[256,128]{1,0:T(8,128)(2,1)S(1)}, bf16[256,128]{1,0:T(8,128)(2,1)S(1)}, u32[]{:S(2)}, u32[]{:S(2)}) collective-permute-start(bf16[256,128]{1,0:T(8,128)(2,1)S(1)} %get-tuple-element.33.mine), channel_id=1, source_target_pairs={{0,16},{4,20},{8,24},{12,28},{16,0},{20,4},{24,8},{28,12},{1,17},{... | collective-permute-start | bytes 196616 | tf_op jit(solution)/shard_map/ppermute | solution.py:22
  23.4 8.7 %collective-permute-start.3 = (bf16[512,128]{1,0:T(8,128)(2,1)S(1)}, bf16[512,128]{1,0:T(8,128)(2,1)S(1)}, u32[]{:S(2)}, u32[]{:S(2)}) collective-permute-start(bf16[512,128]{1,0:T(8,128)(2,1)S(1)} %get-tuple-element.30), channel_id=1, source_target_pairs={{0,4},{4,0},{8,12},{12,8},{16,20},{20,16},{24,28},{28,24},{1,5},{5... | collective-permute-start | bytes 393224 | tf_op jit(solution)/shard_map/ppermute | solution.py:22
  27.9 5.0 %collective-permute-start.11 = (bf16[256,128]{1,0:T(8,128)(2,1)S(1)}, bf16[256,128]{1,0:T(8,128)(2,1)S(1)}, u32[]{:S(2)}, u32[]{:S(2)}) collective-permute-start(bf16[256,128]{1,0:T(8,128)(2,1)S(1)} %merge.1.rest_8_), channel_id=1, source_target_pairs={{0,4},{4,0},{8,12},{12,8},{16,20},{20,16},{24,28},{28,24},{1,5},{5... | collective-permute-start | bytes 196616 | tf_op jit(solution)/shard_map/ppermute | solution.py:22
  28.5 8.8 %collective-permute-start.7 = (bf16[512,128]{1,0:T(8,128)(2,1)S(1)}, bf16[512,128]{1,0:T(8,128)(2,1)S(1)}, u32[]{:S(2)}, u32[]{:S(2)}) collective-permute-start(bf16[512,128]{1,0:T(8,128)(2,1)S(1)} %collective-permute-done.6.rest_4_), channel_id=1, source_target_pairs={{0,4},{4,0},{8,12},{12,8},{16,20},{20,16},{24,28},{28,24},{1,5},{5... | collective-permute-start | bytes 393224 | tf_op jit(solution)/shard_map/ppermute | solution.py:22
  30.0 7.2 %collective-permute-start.5 = (bf16[512,128]{1,0:T(8,128)(2,1)S(1)}, bf16[512,128]{1,0:T(8,128)(2,1)S(1)}, u32[]{:S(2)}, u32[]{:S(2)}) collective-permute-start(bf16[512,128]{1,0:T(8,128)(2,1)S(1)} %collective-permute-done.4.rest_2_), channel_id=1, source_target_pairs={{0,4},{4,0},{8,12},{12,8},{16,20},{20,16},{24,28},{28,24},{1,5},{5... | collective-permute-start | bytes 393224 | tf_op jit(solution)/shard_map/ppermute | solution.py:22
  30.5 7.6 %collective-permute-start.9 = (bf16[512,128]{1,0:T(8,128)(2,1)S(1)}, bf16[512,128]{1,0:T(8,128)(2,1)S(1)}, u32[]{:S(2)}, u32[]{:S(2)}) collective-permute-start(bf16[512,128]{1,0:T(8,128)(2,1)S(1)} %collective-permute-done.8.rest_6_), channel_id=1, source_target_pairs={{0,4},{4,0},{8,12},{12,8},{16,20},{20,16},{24,28},{28,24},{1,5},{5... | collective-permute-start | bytes 393224 | tf_op jit(solution)/shard_map/ppermute | solution.py:22
  32.0 4.3 %collective-permute-start.12 = (bf16[256,128]{1,0:T(8,128)(2,1)S(1)}, bf16[256,128]{1,0:T(8,128)(2,1)S(1)}, u32[]{:S(2)}, u32[]{:S(2)}) collective-permute-start(bf16[256,128]{1,0:T(8,128)(2,1)S(1)} %merge.1.rest_8_), channel_id=1, source_target_pairs={{0,8},{4,12},{8,0},{12,4},{16,24},{20,28},{24,16},{28,20},{1,9},{5... | collective-permute-start | bytes 196616 | tf_op jit(solution)/shard_map/ppermute | solution.py:22
  32.9 4.3 %collective-permute-start.13 = (bf16[256,128]{1,0:T(8,128)(2,1)S(1)}, bf16[256,128]{1,0:T(8,128)(2,1)S(1)}, u32[]{:S(2)}, u32[]{:S(2)}) collective-permute-start(bf16[256,128]{1,0:T(8,128)(2,1)S(1)} %collective-permute-done.11.rest_9_), channel_id=1, source_target_pairs={{0,8},{4,12},{8,0},{12,4},{16,24},{20,28},{24,16},{28,20},{1,9},{5... | collective-permute-start | bytes 196616 | tf_op jit(solution)/shard_map/ppermute | solution.py:22
  46.0 1.6 %collective-permute-start.16 = (bf16[2,128,512]{2,1,0:T(8,128)(2,1)S(1)}, bf16[2,128,512]{2,1,0:T(8,128)(2,1)S(1)}, u32[]{:S(2)}, u32[]{:S(2)}) collective-permute-start(bf16[2,128,512]{2,1,0:T(8,128)(2,1)S(1)} %get-tuple-element.40), channel_id=1, source_target_pairs={{0,1},{1,0},{2,3},{3,2},{4,5},{5,4},{6,7},{7,6},{8,9},{9,8},{10,11... | collective-permute-start | bytes 786440 | tf_op jit(solution)/shard_map/ppermute | solution.py:22
  46.1 3.2 %collective-permute-start.14 = (bf16[2,128,512]{2,1,0:T(8,128)(2,1)S(1)}, bf16[2,128,512]{2,1,0:T(8,128)(2,1)S(1)}, u32[]{:S(2)}, u32[]{:S(2)}) collective-permute-start(bf16[2,128,512]{2,1,0:T(8,128)(2,1)S(1)} %get-tuple-element.35), channel_id=1, source_target_pairs={{0,1},{1,0},{2,3},{3,2},{4,5},{5,4},{6,7},{7,6},{8,9},{9,8},{10,11... | collective-permute-start | bytes 786440 | tf_op jit(solution)/shard_map/ppermute | solution.py:22
  47.7 6.4 %collective-permute-start.17 = (bf16[1,128,512]{2,1,0:T(8,128)(2,1)S(1)}, bf16[1,128,512]{2,1,0:T(8,128)(2,1)S(1)}, u32[]{:S(2)}, u32[]{:S(2)}) collective-permute-start(bf16[1,128,512]{2,1,0:T(8,128)(2,1)S(1)} %slice.38), channel_id=1, source_target_pairs={{0,2},{1,3},{2,0},{3,1},{4,6},{5,7},{6,4},{7,5},{8,10},{9,11},{10,... | collective-permute-start | bytes 393224 | tf_op jit(solution)/shard_map/ppermute | solution.py:22
  49.4 6.7 %collective-permute-start.15 = (bf16[1,128,512]{2,1,0:T(8,128)(2,1)S(1)}, bf16[1,128,512]{2,1,0:T(8,128)(2,1)S(1)}, u32[]{:S(2)}, u32[]{:S(2)}) collective-permute-start(bf16[1,128,512]{2,1,0:T(8,128)(2,1)S(1)} %slice.39), channel_id=1, source_target_pairs={{0,2},{1,3},{2,0},{3,1},{4,6},{5,7},{6,4},{7,5},{8,10},{9,11},{10,... | collective-permute-start | bytes 393224 | tf_op jit(solution)/shard_map/ppermute | solution.py:22

commit v4 on v3

--- a/solution.py
+++ b/solution.py
@@ -370,11 +370,7 @@
             name="merge",
             **small,
         )(table, mine, swapped(mine, "seq", half))
-        pieces = {0: merged}
-        for mask in range(1, half):
-            top = 1 << (mask.bit_length() - 1)
-            pieces[mask] = swapped(pieces[mask - top], "seq", top)
-        pieces = list(pieces.values())
+        pieces = [merged] + [swapped(merged, "seq", mask) for mask in range(1, half)]
     else:
         table = pl.pallas_call(
             table_kernel,

time: 57 us -> 58.6 us (1.028)
  waiting for transfers between devices: 22.7 us -> 23.9 us
    ppermute x18, waiting for transfers between devices: 22.7 us -> 23.9 us  [swapped(): lax.ppermute(value, axis, [(source, source ^ mask) for source in range(co...]
  transfers between devices with their start and end apart: 18 -> 18, of which waited for: 12 -> 10; matrix products, arithmetic and copies ran while one was open for 0% -> 0% of each run, Pallas kernels for 5% -> 5%
where the time goes in v4:
time: 58.6 us; the launch traced here: 58.4 us
  waiting for transfers between devices  23.9 us (41%)
  starting transfers between devices  21.4 us (37%)
  Pallas kernels  12 us (20%)
  other arithmetic  0.92 us (2%)
    ppermute x18, waiting for transfers between devices, swapped(): lax.ppermute(value, axis, [(source, source ^ mask) for source in range(co...  23.9 us
    ppermute x18, starting transfers between devices, swapped(): lax.ppermute(value, axis, [(source, source ^ mask) for source in range(co...  21.4 us
    pallas_call x1, Pallas kernels, body(): pl.pallas_call(functools.partial(first_kernel, sizes), out_shape=term_sha...  4.42 us
    pallas_call x1, Pallas kernels, body(): pl.pallas_call(functools.partial(second_kernel, sizes), out_shape=term_sh...  3.47 us
    pallas_call x1, Pallas kernels, body(): pl.pallas_call(functools.partial(pick_kernel, sizes), out_shape=[slot_sha...  1.41 us
  transfers between devices with their start and end apart: 18, of which 10 were waited for; matrix products, arithmetic and copies ran while one was open for 0% of the time, Pallas kernels for 5%

profile of v4, /device:TPU:0, one launch (start us, length us, event | category | flops | bytes accessed | tf_op | source)
XLA Modules:
  0.0 58.4 jit_solution(5272831452895574086)
XLA Ops:
  0.0 1.0 %open.1 = (bf16[512,128]{1,0:T(8,128)(2,1)S(1)}, bf16[512,128]{1,0:T(8,128)(2,1)S(1)}, bf16[512,128]{1,0:T(8,128)(2,1)S(1)}, bf16[512,128]{1,0:T(8,128)(2,1)S(1)...) custom-call(bf16[512,128]{1,0:T(8,128)(2,1)} %bitcast.7, ...), custom_call_target="tpu_custom_call" | custom-call | bytes 1048576 | tf_op jit(solution)/shard_map/open/pallas_call | solution.py:336
  1.0 4.1 %collective-permute-start.6 = (bf16[512,128]{1,0:T(8,128)(2,1)S(1)}, bf16[512,128]{1,0:T(8,128)(2,1)S(1)}, u32[]{:S(2)}, u32[]{:S(2)}) collective-permute-start(bf16[512,128]{1,0:T(8,128)(2,1)S(1)} %get-tuple-element.32), channel_id=1, source_target_pairs={{0,16},{4,20},{8,24},{12,28},{16,0},{20,4},{24,8},{28,12},{1,17},{... | collective-permute-start | bytes 393224 | tf_op jit(solution)/shard_map/ppermute | solution.py:22
  5.2 1.6 %collective-permute-start.4 = (bf16[512,128]{1,0:T(8,128)(2,1)S(1)}, bf16[512,128]{1,0:T(8,128)(2,1)S(1)}, u32[]{:S(2)}, u32[]{:S(2)}) collective-permute-start(bf16[512,128]{1,0:T(8,128)(2,1)S(1)} %get-tuple-element.31), channel_id=1, source_target_pairs={{0,8},{4,12},{8,0},{12,4},{16,24},{20,28},{24,16},{28,20},{1,9},{5... | collective-permute-start | bytes 393224 | tf_op jit(solution)/shard_map/ppermute | solution.py:22
  6.7 4.8 %collective-permute-done.6.rest_4_ = bf16[512,128]{1,0:T(8,128)(2,1)S(1)} collective-permute-done((bf16[512,128]{1,0:T(8,128)(2,1)S(1)}, bf16[512,128]{1,0:T(8,128)(2,1)S(1)}, u32[]{:S(2)}, u32[]{:S(2)}) %collective-permute-start.6) | collective-permute-done | bytes 131104 | tf_op jit(solution)/shard_map/ppermute | solution.py:22
  11.6 0.6 %collective-permute-start.8 = (bf16[512,128]{1,0:T(8,128)(2,1)S(1)}, bf16[512,128]{1,0:T(8,128)(2,1)S(1)}, u32[]{:S(2)}, u32[]{:S(2)}) collective-permute-start(bf16[512,128]{1,0:T(8,128)(2,1)S(1)} %collective-permute-done.6.rest_4_), channel_id=1, source_target_pairs={{0,8},{4,12},{8,0},{12,4},{16,24},{20,28},{24,16},{28,20},{1,9},{5... | collective-permute-start | bytes 393224 | tf_op jit(solution)/shard_map/ppermute | solution.py:22
  12.2 1.5 %collective-permute-start = (bf16[128,128]{1,0:T(8,128)(2,1)S(1)}, bf16[128,128]{1,0:T(8,128)(2,1)S(1)}, u32[]{:S(2)}, u32[]{:S(2)}) collective-permute-start(bf16[128,128]{1,0:T(8,128)(2,1)S(1)} %get-tuple-element.24), channel_id=1, source_target_pairs={{0,4},{4,0},{8,12},{12,8},{16,20},{20,16},{24,28},{28,24},{1,5},{5... | collective-permute-start | bytes 98312 | tf_op jit(solution)/shard_map/ppermute | solution.py:22
  13.7 1.5 %collective-permute-start.1 = (bf16[128,128]{1,0:T(8,128)(2,1)S(1)}, bf16[128,128]{1,0:T(8,128)(2,1)S(1)}, u32[]{:S(2)}, u32[]{:S(2)}) collective-permute-start(bf16[128,128]{1,0:T(8,128)(2,1)S(1)} %get-tuple-element.25), channel_id=1, source_target_pairs={{0,8},{4,12},{8,0},{12,4},{16,24},{20,28},{24,16},{28,20},{1,9},{5... | collective-permute-start | bytes 98312 | tf_op jit(solution)/shard_map/ppermute | solution.py:22
  15.1 0.5 collective-permute-start.2
  15.7 0.4 collective-permute-done.rest_1_
  16.1 1.5 %collective-permute-done.1.rest_2_ = bf16[128,128]{1,0:T(8,128)(2,1)S(1)} collective-permute-done((bf16[128,128]{1,0:T(8,128)(2,1)S(1)}, bf16[128,128]{1,0:T(8,128)(2,1)S(1)}, u32[]{:S(2)}, u32[]{:S(2)}) %collective-permute-start.1) | collective-permute-done | bytes 32800 | tf_op jit(solution)/shard_map/ppermute | solution.py:22
  17.6 2.4 %collective-permute-done.2.rest_3_ = bf16[128,128]{1,0:T(8,128)(2,1)S(1)} collective-permute-done((bf16[128,128]{1,0:T(8,128)(2,1)S(1)}, bf16[128,128]{1,0:T(8,128)(2,1)S(1)}, u32[]{:S(2)}, u32[]{:S(2)}) %collective-permute-start.2) | collective-permute-done | bytes 32800 | tf_op jit(solution)/shard_map/ppermute | solution.py:22
  20.0 1.4 %pick.1 = (bf16[256,128]{1,0:T(8,128)(2,1)S(1)}, s32[1,10]{1,0:T(1,128)S(1)}) custom-call(s32[1,4]{1,0:T(1,128)} %page_in.1, s32[1,3]{1,0:T(1,128)} %shift_in.1, s32[1,3]{1,0:T(1,128)} %bitcast.9, bf16[128,128]{1,0:T(8,128)(2,1)S(1)} %get-tuple-element.23.rest_0_, bf16[128,128]{1,0:T(8,128)(2,1)S(1)} %collective-permute-done.rest_1_, ...), custom_call_target="tpu_custom_call" | custom-call | bytes 4194304 | tf_op jit(solution)/shard_map/pick/pallas_call | solution.py:356
  21.4 2.0 %collective-permute-start.10 = (bf16[256,128]{1,0:T(8,128)(2,1)S(1)}, bf16[256,128]{1,0:T(8,128)(2,1)S(1)}, u32[]{:S(2)}, u32[]{:S(2)}) collective-permute-start(bf16[256,128]{1,0:T(8,128)(2,1)S(1)} %get-tuple-element.33.mine), channel_id=1, source_target_pairs={{0,16},{4,20},{8,24},{12,28},{16,0},{20,4},{24,8},{28,12},{1,17},{... | collective-permute-start | bytes 196616 | tf_op jit(solution)/shard_map/ppermute | solution.py:22
  23.4 0.9 %collective-permute-start.3 = (bf16[512,128]{1,0:T(8,128)(2,1)S(1)}, bf16[512,128]{1,0:T(8,128)(2,1)S(1)}, u32[]{:S(2)}, u32[]{:S(2)}) collective-permute-start(bf16[512,128]{1,0:T(8,128)(2,1)S(1)} %get-tuple-element.30), channel_id=1, source_target_pairs={{0,4},{4,0},{8,12},{12,8},{16,20},{20,16},{24,28},{28,24},{1,5},{5... | collective-permute-start | bytes 393224 | tf_op jit(solution)/shard_map/ppermute | solution.py:22
  24.3 3.1 %collective-permute-done.10.other = bf16[256,128]{1,0:T(8,128)(2,1)S(1)} collective-permute-done((bf16[256,128]{1,0:T(8,128)(2,1)S(1)}, bf16[256,128]{1,0:T(8,128)(2,1)S(1)}, u32[]{:S(2)}, u32[]{:S(2)}) %collective-permute-start.10) | collective-permute-done | bytes 65568 | tf_op jit(solution)/shard_map/ppermute | solution.py:22
  27.4 0.6 %merge.1.rest_8_ = bf16[256,128]{1,0:T(8,128)(2,1)S(1)} custom-call(s32[1,10]{1,0:T(1,128)S(1)} %get-tuple-element.27.table, bf16[256,128]{1,0:T(8,128)(2,1)S(1)} %get-tuple-element.33.mine, bf16[256,128]{1,0:T(8,128)(2,1)S(1)} %collective-permute-done.10.other), custom_call_target="tpu_custom_call" | custom-call | bytes 4194304 | tf_op jit(solution)/shard_map/merge/pallas_call | solution.py:365
  28.0 0.4 collective-permute-start.13
  28.4 1.5 %collective-permute-start.7 = (bf16[512,128]{1,0:T(8,128)(2,1)S(1)}, bf16[512,128]{1,0:T(8,128)(2,1)S(1)}, u32[]{:S(2)}, u32[]{:S(2)}) collective-permute-start(bf16[512,128]{1,0:T(8,128)(2,1)S(1)} %collective-permute-done.6.rest_4_), channel_id=1, source_target_pairs={{0,4},{4,0},{8,12},{12,8},{16,20},{20,16},{24,28},{28,24},{1,5},{5... | collective-permute-start | bytes 393224 | tf_op jit(solution)/shard_map/ppermute | solution.py:22
  29.9 0.0 collective-permute-done.4.rest_2_
  29.9 0.5 collective-permute-start.5
  30.4 0.0 collective-permute-done.8.rest_6_
  30.4 1.5 %collective-permute-start.9 = (bf16[512,128]{1,0:T(8,128)(2,1)S(1)}, bf16[512,128]{1,0:T(8,128)(2,1)S(1)}, u32[]{:S(2)}, u32[]{:S(2)}) collective-permute-start(bf16[512,128]{1,0:T(8,128)(2,1)S(1)} %collective-permute-done.8.rest_6_), channel_id=1, source_target_pairs={{0,4},{4,0},{8,12},{12,8},{16,20},{20,16},{24,28},{28,24},{1,5},{5... | collective-permute-start | bytes 393224 | tf_op jit(solution)/shard_map/ppermute | solution.py:22
  31.9 0.0 collective-permute-done.3.rest_1_
  31.9 1.7 %collective-permute-start.12 = (bf16[256,128]{1,0:T(8,128)(2,1)S(1)}, bf16[256,128]{1,0:T(8,128)(2,1)S(1)}, u32[]{:S(2)}, u32[]{:S(2)}) collective-permute-start(bf16[256,128]{1,0:T(8,128)(2,1)S(1)} %merge.1.rest_8_), channel_id=1, source_target_pairs={{0,8},{4,12},{8,0},{12,4},{16,24},{20,28},{24,16},{28,20},{1,9},{5... | collective-permute-start | bytes 196616 | tf_op jit(solution)/shard_map/ppermute | solution.py:22
  33.6 0.0 collective-permute-done.13.rest_11_
  33.6 0.4 collective-permute-start.11
  34.0 1.0 %stage.1.query_ref = bf16[256,1024]{1,0:T(8,128)(2,1)S(1)} custom-call(bf16[256,1024]{1,0:T(8,128)(2,1)} %query_in.1), custom_call_target="tpu_custom_call" | custom-call | bytes 2097152 | tf_op jit(solution)/shard_map/stage/pallas_call | solution.py:316
  35.0 1.1 %collective-permute-done.12.rest_10_ = bf16[256,128]{1,0:T(8,128)(2,1)S(1)} collective-permute-done((bf16[256,128]{1,0:T(8,128)(2,1)S(1)}, bf16[256,128]{1,0:T(8,128)(2,1)S(1)}, u32[]{:S(2)}, u32[]{:S(2)}) %collective-permute-start.12) | collective-permute-done | bytes 65568 | tf_op jit(solution)/shard_map/ppermute | solution.py:22
  36.2 3.4 %collective-permute-done.11.rest_9_ = bf16[256,128]{1,0:T(8,128)(2,1)S(1)} collective-permute-done((bf16[256,128]{1,0:T(8,128)(2,1)S(1)}, bf16[256,128]{1,0:T(8,128)(2,1)S(1)}, u32[]{:S(2)}, u32[]{:S(2)}) %collective-permute-start.11) | collective-permute-done | bytes 65568 | tf_op jit(solution)/shard_map/ppermute | solution.py:22
  39.6 0.0 collective-permute-done.5.rest_3_
  39.6 0.0 collective-permute-done.7.rest_5_
  39.6 0.0 collective-permute-done.9.rest_7_
  39.6 4.4 %first.1 = (bf16[2,128,512]{2,1,0:T(8,128)(2,1)S(1)}, f32[2,128,512]{2,1,0:T(8,128)S(1)}, bf16[1536,256]{1,0:T(8,128)(2,1)S(1)}, bf16[1536,256]{1,0:T(8,128)(2,1)S(1)}, bf16[1024,2048]{1,0:T(8,128)(2,1)S(1)}) custom-call(s32[1,10]{1,0:T(1,128)S(1)} %get-tuple-element.27.table, bf16[256,1024]{1,0:T(8,128)(2,1)S(1)} %stage.1.query_ref, ...), custom_call_target="tpu_custom_call" | custom-call | flops 1342177280 | bytes 8388608 | tf_op jit(solution)/shard_map/first/pallas_call | solution.py:414
  44.0 3.5 %second.1 = (bf16[2,128,512]{2,1,0:T(8,128)(2,1)S(1)}, f32[2,128,512]{2,1,0:T(8,128)S(1)}) custom-call(bf16[256,1024]{1,0:T(8,128)(2,1)S(1)} %stage.1.query_ref, bf16[1536,256]{1,0:T(8,128)(2,1)S(1)} %get-tuple-element.36.keys, bf16[1536,256]{1,0:T(8,128)(2,1)S(1)} %get-tuple-element.37.values, bf16[1024,2048]{1,0:T(8,128)(2,1)S(1)} %get-tuple-element.38.proj), custom_call_target="tpu_custom_call" | custom-call | flops 1342177280 | bytes 8388608 | tf_op jit(solution)/shard_map/second/pallas_call | solution.py:429
  47.5 0.1 collective-permute-start.16
  47.6 0.5 collective-permute-start.14
  48.1 1.0 %collective-permute-done.16 = bf16[2,128,512]{2,1,0:T(8,128)(2,1)S(1)} collective-permute-done((bf16[2,128,512]{2,1,0:T(8,128)(2,1)S(1)}, bf16[2,128,512]{2,1,0:T(8,128)(2,1)S(1)}, u32[]{:S(2)}, u32[]{:S(2)}) %collective-permute-start.16) | collective-permute-done | bytes 262176 | tf_op jit(solution)/shard_map/ppermute | solution.py:22
  49.1 0.1 convert_add_fusion
  49.2 1.6 %collective-permute-start.17 = (bf16[1,128,512]{2,1,0:T(8,128)(2,1)S(1)}, bf16[1,128,512]{2,1,0:T(8,128)(2,1)S(1)}, u32[]{:S(2)}, u32[]{:S(2)}) collective-permute-start(bf16[1,128,512]{2,1,0:T(8,128)(2,1)S(1)} %slice.38), channel_id=1, source_target_pairs={{0,2},{1,3},{2,0},{3,1},{4,6},{5,7},{6,4},{7,5},{8,10},{9,11},{10,... | collective-permute-start | bytes 393224 | tf_op jit(solution)/shard_map/ppermute | solution.py:22
  50.8 0.0 collective-permute-done.14
  50.8 0.1 convert_add_fusion.1
  50.9 0.6 collective-permute-start.15
  51.5 4.2 %collective-permute-done.17 = bf16[1,128,512]{2,1,0:T(8,128)(2,1)S(1)} collective-permute-done((bf16[1,128,512]{2,1,0:T(8,128)(2,1)S(1)}, bf16[1,128,512]{2,1,0:T(8,128)(2,1)S(1)}, u32[]{:S(2)}, u32[]{:S(2)}) %collective-permute-start.17) | collective-permute-done | bytes 131104 | tf_op jit(solution)/shard_map/ppermute | solution.py:22
  55.7 1.9 %collective-permute-done.15 = bf16[1,128,512]{2,1,0:T(8,128)(2,1)S(1)} collective-permute-done((bf16[1,128,512]{2,1,0:T(8,128)(2,1)S(1)}, bf16[1,128,512]{2,1,0:T(8,128)(2,1)S(1)}, u32[]{:S(2)}, u32[]{:S(2)}) %collective-permute-start.15) | collective-permute-done | bytes 131104 | tf_op jit(solution)/shard_map/ppermute | solution.py:22
  57.6 0.7 %pad_maximum_fusion = bf16[256,512]{1,0:T(8,128)(2,1)} fusion(bf16[128,512]{1,0:T(8,128)(2,1)S(1)} %fusion.3, bf16[128,512]{1,0:T(8,128)(2,1)S(1)} %fusion.2), kind=kLoop, calls=%fused_computation.8 | loop fusion | flops 524288 | bytes 524288 | tf_op jit(solution)/shard_map/concatenate | solution.py:449
  (4 shorter events, 0.1 us)
Async XLA Ops:
  1.0 10.5 %collective-permute-start.6 = (bf16[512,128]{1,0:T(8,128)(2,1)S(1)}, bf16[512,128]{1,0:T(8,128)(2,1)S(1)}, u32[]{:S(2)}, u32[]{:S(2)}) collective-permute-start(bf16[512,128]{1,0:T(8,128)(2,1)S(1)} %get-tuple-element.32), channel_id=1, source_target_pairs={{0,16},{4,20},{8,24},{12,28},{16,0},{20,4},{24,8},{28,12},{1,17},{... | collective-permute-start | bytes 393224 | tf_op jit(solution)/shard_map/ppermute | solution.py:22
  5.2 24.7 %collective-permute-start.4 = (bf16[512,128]{1,0:T(8,128)(2,1)S(1)}, bf16[512,128]{1,0:T(8,128)(2,1)S(1)}, u32[]{:S(2)}, u32[]{:S(2)}) collective-permute-start(bf16[512,128]{1,0:T(8,128)(2,1)S(1)} %get-tuple-element.31), channel_id=1, source_target_pairs={{0,8},{4,12},{8,0},{12,4},{16,24},{20,28},{24,16},{28,20},{1,9},{5... | collective-permute-start | bytes 393224 | tf_op jit(solution)/shard_map/ppermute | solution.py:22
  11.6 18.8 %collective-permute-start.8 = (bf16[512,128]{1,0:T(8,128)(2,1)S(1)}, bf16[512,128]{1,0:T(8,128)(2,1)S(1)}, u32[]{:S(2)}, u32[]{:S(2)}) collective-permute-start(bf16[512,128]{1,0:T(8,128)(2,1)S(1)} %collective-permute-done.6.rest_4_), channel_id=1, source_target_pairs={{0,8},{4,12},{8,0},{12,4},{16,24},{20,28},{24,16},{28,20},{1,9},{5... | collective-permute-start | bytes 393224 | tf_op jit(solution)/shard_map/ppermute | solution.py:22
  12.2 3.9 %collective-permute-start = (bf16[128,128]{1,0:T(8,128)(2,1)S(1)}, bf16[128,128]{1,0:T(8,128)(2,1)S(1)}, u32[]{:S(2)}, u32[]{:S(2)}) collective-permute-start(bf16[128,128]{1,0:T(8,128)(2,1)S(1)} %get-tuple-element.24), channel_id=1, source_target_pairs={{0,4},{4,0},{8,12},{12,8},{16,20},{20,16},{24,28},{28,24},{1,5},{5... | collective-permute-start | bytes 98312 | tf_op jit(solution)/shard_map/ppermute | solution.py:22
  13.7 3.9 %collective-permute-start.1 = (bf16[128,128]{1,0:T(8,128)(2,1)S(1)}, bf16[128,128]{1,0:T(8,128)(2,1)S(1)}, u32[]{:S(2)}, u32[]{:S(2)}) collective-permute-start(bf16[128,128]{1,0:T(8,128)(2,1)S(1)} %get-tuple-element.25), channel_id=1, source_target_pairs={{0,8},{4,12},{8,0},{12,4},{16,24},{20,28},{24,16},{28,20},{1,9},{5... | collective-permute-start | bytes 98312 | tf_op jit(solution)/shard_map/ppermute | solution.py:22
  15.1 4.8 %collective-permute-start.2 = (bf16[128,128]{1,0:T(8,128)(2,1)S(1)}, bf16[128,128]{1,0:T(8,128)(2,1)S(1)}, u32[]{:S(2)}, u32[]{:S(2)}) collective-permute-start(bf16[128,128]{1,0:T(8,128)(2,1)S(1)} %get-tuple-element.26), channel_id=1, source_target_pairs={{0,12},{4,8},{8,4},{12,0},{16,28},{20,24},{24,20},{28,16},{1,13},{... | collective-permute-start | bytes 98312 | tf_op jit(solution)/shard_map/ppermute | solution.py:22
  21.4 6.0 %collective-permute-start.10 = (bf16[256,128]{1,0:T(8,128)(2,1)S(1)}, bf16[256,128]{1,0:T(8,128)(2,1)S(1)}, u32[]{:S(2)}, u32[]{:S(2)}) collective-permute-start(bf16[256,128]{1,0:T(8,128)(2,1)S(1)} %get-tuple-element.33.mine), channel_id=1, source_target_pairs={{0,16},{4,20},{8,24},{12,28},{16,0},{20,4},{24,8},{28,12},{1,17},{... | collective-permute-start | bytes 196616 | tf_op jit(solution)/shard_map/ppermute | solution.py:22
  23.4 8.5 %collective-permute-start.3 = (bf16[512,128]{1,0:T(8,128)(2,1)S(1)}, bf16[512,128]{1,0:T(8,128)(2,1)S(1)}, u32[]{:S(2)}, u32[]{:S(2)}) collective-permute-start(bf16[512,128]{1,0:T(8,128)(2,1)S(1)} %get-tuple-element.30), channel_id=1, source_target_pairs={{0,4},{4,0},{8,12},{12,8},{16,20},{20,16},{24,28},{28,24},{1,5},{5... | collective-permute-start | bytes 393224 | tf_op jit(solution)/shard_map/ppermute | solution.py:22
  28.0 5.6 %collective-permute-start.13 = (bf16[256,128]{1,0:T(8,128)(2,1)S(1)}, bf16[256,128]{1,0:T(8,128)(2,1)S(1)}, u32[]{:S(2)}, u32[]{:S(2)}) collective-permute-start(bf16[256,128]{1,0:T(8,128)(2,1)S(1)} %merge.1.rest_8_), channel_id=1, source_target_pairs={{0,12},{4,8},{8,4},{12,0},{16,28},{20,24},{24,20},{28,16},{1,13},{... | collective-permute-start | bytes 196616 | tf_op jit(solution)/shard_map/ppermute | solution.py:22
  28.4 11.2 %collective-permute-start.7 = (bf16[512,128]{1,0:T(8,128)(2,1)S(1)}, bf16[512,128]{1,0:T(8,128)(2,1)S(1)}, u32[]{:S(2)}, u32[]{:S(2)}) collective-permute-start(bf16[512,128]{1,0:T(8,128)(2,1)S(1)} %collective-permute-done.6.rest_4_), channel_id=1, source_target_pairs={{0,4},{4,0},{8,12},{12,8},{16,20},{20,16},{24,28},{28,24},{1,5},{5... | collective-permute-start | bytes 393224 | tf_op jit(solution)/shard_map/ppermute | solution.py:22
  29.9 9.7 %collective-permute-start.5 = (bf16[512,128]{1,0:T(8,128)(2,1)S(1)}, bf16[512,128]{1,0:T(8,128)(2,1)S(1)}, u32[]{:S(2)}, u32[]{:S(2)}) collective-permute-start(bf16[512,128]{1,0:T(8,128)(2,1)S(1)} %collective-permute-done.4.rest_2_), channel_id=1, source_target_pairs={{0,4},{4,0},{8,12},{12,8},{16,20},{20,16},{24,28},{28,24},{1,5},{5... | collective-permute-start | bytes 393224 | tf_op jit(solution)/shard_map/ppermute | solution.py:22
  30.4 9.2 %collective-permute-start.9 = (bf16[512,128]{1,0:T(8,128)(2,1)S(1)}, bf16[512,128]{1,0:T(8,128)(2,1)S(1)}, u32[]{:S(2)}, u32[]{:S(2)}) collective-permute-start(bf16[512,128]{1,0:T(8,128)(2,1)S(1)} %collective-permute-done.8.rest_6_), channel_id=1, source_target_pairs={{0,4},{4,0},{8,12},{12,8},{16,20},{20,16},{24,28},{28,24},{1,5},{5... | collective-permute-start | bytes 393224 | tf_op jit(solution)/shard_map/ppermute | solution.py:22
  31.9 4.3 %collective-permute-start.12 = (bf16[256,128]{1,0:T(8,128)(2,1)S(1)}, bf16[256,128]{1,0:T(8,128)(2,1)S(1)}, u32[]{:S(2)}, u32[]{:S(2)}) collective-permute-start(bf16[256,128]{1,0:T(8,128)(2,1)S(1)} %merge.1.rest_8_), channel_id=1, source_target_pairs={{0,8},{4,12},{8,0},{12,4},{16,24},{20,28},{24,16},{28,20},{1,9},{5... | collective-permute-start | bytes 196616 | tf_op jit(solution)/shard_map/ppermute | solution.py:22
  33.6 6.0 %collective-permute-start.11 = (bf16[256,128]{1,0:T(8,128)(2,1)S(1)}, bf16[256,128]{1,0:T(8,128)(2,1)S(1)}, u32[]{:S(2)}, u32[]{:S(2)}) collective-permute-start(bf16[256,128]{1,0:T(8,128)(2,1)S(1)} %merge.1.rest_8_), channel_id=1, source_target_pairs={{0,4},{4,0},{8,12},{12,8},{16,20},{20,16},{24,28},{28,24},{1,5},{5... | collective-permute-start | bytes 196616 | tf_op jit(solution)/shard_map/ppermute | solution.py:22
  47.5 1.6 %collective-permute-start.16 = (bf16[2,128,512]{2,1,0:T(8,128)(2,1)S(1)}, bf16[2,128,512]{2,1,0:T(8,128)(2,1)S(1)}, u32[]{:S(2)}, u32[]{:S(2)}) collective-permute-start(bf16[2,128,512]{2,1,0:T(8,128)(2,1)S(1)} %get-tuple-element.40), channel_id=1, source_target_pairs={{0,1},{1,0},{2,3},{3,2},{4,5},{5,4},{6,7},{7,6},{8,9},{9,8},{10,11... | collective-permute-start | bytes 786440 | tf_op jit(solution)/shard_map/ppermute | solution.py:22
  47.6 3.2 %collective-permute-start.14 = (bf16[2,128,512]{2,1,0:T(8,128)(2,1)S(1)}, bf16[2,128,512]{2,1,0:T(8,128)(2,1)S(1)}, u32[]{:S(2)}, u32[]{:S(2)}) collective-permute-start(bf16[2,128,512]{2,1,0:T(8,128)(2,1)S(1)} %get-tuple-element.35), channel_id=1, source_target_pairs={{0,1},{1,0},{2,3},{3,2},{4,5},{5,4},{6,7},{7,6},{8,9},{9,8},{10,11... | collective-permute-start | bytes 786440 | tf_op jit(solution)/shard_map/ppermute | solution.py:22
  49.2 6.4 %collective-permute-start.17 = (bf16[1,128,512]{2,1,0:T(8,128)(2,1)S(1)}, bf16[1,128,512]{2,1,0:T(8,128)(2,1)S(1)}, u32[]{:S(2)}, u32[]{:S(2)}) collective-permute-start(bf16[1,128,512]{2,1,0:T(8,128)(2,1)S(1)} %slice.38), channel_id=1, source_target_pairs={{0,2},{1,3},{2,0},{3,1},{4,6},{5,7},{6,4},{7,5},{8,10},{9,11},{10,... | collective-permute-start | bytes 393224 | tf_op jit(solution)/shard_map/ppermute | solution.py:22
  50.9 6.7 %collective-permute-start.15 = (bf16[1,128,512]{2,1,0:T(8,128)(2,1)S(1)}, bf16[1,128,512]{2,1,0:T(8,128)(2,1)S(1)}, u32[]{:S(2)}, u32[]{:S(2)}) collective-permute-start(bf16[1,128,512]{2,1,0:T(8,128)(2,1)S(1)} %slice.39), channel_id=1, source_target_pairs={{0,2},{1,3},{2,0},{3,1},{4,6},{5,7},{6,4},{7,5},{8,10},{9,11},{10,... | collective-permute-start | bytes 393224 | tf_op jit(solution)/shard_map/ppermute | solution.py:22

commit v5 on v4

--- a/solution.py
+++ b/solution.py
@@ -120,9 +120,8 @@
     copy.wait()
 
 
-def pick_kernel(sizes, page_in, shift_in, live_in, *rest):
-    pieces, slots, table = rest[:-6], rest[-6], rest[-5]
-    load_table((page_in, shift_in, live_in), table, rest[-4:-1], rest[-1])
+def pick_kernel(sizes, table, *rest):
+    pieces, slots = rest[:-1], rest[-1]
     piece = sizes["piece"]
     _, pages = decoded(sizes, table, lax.axis_index("seq"))
     for i, (bits, place, _) in enumerate(pages):
@@ -326,6 +325,16 @@
     table_shape = jax.ShapeDtypeStruct((1, table_size), jnp.int32)
     list_scratch = [pltpu.SMEM(part.shape, jnp.int32) for part in lists]
     list_scratch.append(pltpu.SemaphoreType.DMA((3,)))
+    table = pl.pallas_call(
+        table_kernel,
+        out_shape=table_shape,
+        in_specs=[hbm] * 3,
+        out_specs=scalars,
+        scratch_shapes=list_scratch,
+        compiler_params=pltpu.CompilerParams(vmem_limit_bytes=1 << 20),
+        cost_estimate=pl.CostEstimate(flops=0, bytes_accessed=1 << 20, transcendentals=0),
+        name="table",
+    )(*map(far, lists))
     own_shard = lax.axis_index("seq")
     if tree:
         half = shards // 2
@@ -353,15 +362,14 @@
             compiler_params=pltpu.CompilerParams(vmem_limit_bytes=2 << 20),
             cost_estimate=pl.CostEstimate(flops=0, bytes_accessed=4 << 20, transcendentals=0),
         )
-        mine, table = pl.pallas_call(
+        mine = pl.pallas_call(
             functools.partial(pick_kernel, sizes),
-            out_shape=[slot_shape, table_shape],
-            in_specs=[hbm] * 3 + [vector] * len(pieces),
-            out_specs=[vector, scalars],
-            scratch_shapes=list_scratch,
+            out_shape=slot_shape,
+            in_specs=[scalars] + [vector] * len(pieces),
+            out_specs=vector,
             name="pick",
             **small,
-        )(*map(far, lists), *pieces)
+        )(table, *pieces)
         merged = pl.pallas_call(
             functools.partial(merge_kernel, sizes),
             out_shape=slot_shape,
@@ -372,14 +380,6 @@
         )(table, mine, swapped(mine, "seq", half))
         pieces = [merged] + [swapped(merged, "seq", mask) for mask in range(1, half)]
     else:
-        table = pl.pallas_call(
-            table_kernel,
-            out_shape=table_shape,
-            in_specs=[hbm] * 3,
-            out_specs=scalars,
-            scratch_shapes=list_scratch,
-            name="table",
-        )(*map(far, lists))
         blocks, pieces = [], []
         for k in range(slash_count):
             distance = slash_shift[0, k]

time: 58.6 us -> 57.8 us (0.986)
  waiting for transfers between devices: 23.9 us -> 22.6 us
    ppermute x18, waiting for transfers between devices: 23.9 us -> 22.6 us  [swapped(): lax.ppermute(value, axis, [(source, source ^ mask) for source in range(co...]
    pallas_call x1 -> x2, Pallas kernels: 1.41 us -> 1.96 us  [the longest x1 1.3 us: body(): pl.pallas_call(table_kernel, out_shape=table_shape, in_specs=[hbm] * 3, o...]
  transfers between devices with their start and end apart: 18 -> 18, of which waited for: 10 -> 9; matrix products, arithmetic and copies ran while one was open for 0% -> 0% of each run, Pallas kernels for 5% -> 6%
where the time goes in v5:
time: 57.8 us; the launch traced here: 57.6 us
  waiting for transfers between devices  22.6 us (39%)
  starting transfers between devices  21.4 us (37%)
  Pallas kernels  12.5 us (22%)
  other arithmetic  0.92 us (2%)
    ppermute x18, waiting for transfers between devices, swapped(): lax.ppermute(value, axis, [(source, source ^ mask) for source in range(co...  22.6 us
    ppermute x18, starting transfers between devices, swapped(): lax.ppermute(value, axis, [(source, source ^ mask) for source in range(co...  21.4 us
    pallas_call x1, Pallas kernels, body(): pl.pallas_call(functools.partial(first_kernel, sizes), out_shape=term_sha...  4.42 us
    pallas_call x1, Pallas kernels, body(): pl.pallas_call(functools.partial(second_kernel, sizes), out_shape=term_sh...  3.47 us
    pallas_call x1, Pallas kernels, body(): pl.pallas_call(table_kernel, out_shape=table_shape, in_specs=[hbm] * 3, o...  1.3 us
  transfers between devices with their start and end apart: 18, of which 9 were waited for; matrix products, arithmetic and copies ran while one was open for 0% of the time, Pallas kernels for 6%

profile of v5, /device:TPU:0, one launch (start us, length us, event | category | flops | bytes accessed | tf_op | source)
XLA Modules:
  0.0 57.6 jit_solution(991242073213526054)
XLA Ops:
  0.0 1.0 %open.1 = (bf16[512,128]{1,0:T(8,128)(2,1)S(1)}, bf16[512,128]{1,0:T(8,128)(2,1)S(1)}, bf16[512,128]{1,0:T(8,128)(2,1)S(1)}, bf16[512,128]{1,0:T(8,128)(2,1)S(1)...) custom-call(bf16[512,128]{1,0:T(8,128)(2,1)} %bitcast.7, ...), custom_call_target="tpu_custom_call" | custom-call | bytes 1048576 | tf_op jit(solution)/shard_map/open/pallas_call | solution.py:345
  1.0 4.1 %collective-permute-start.3 = (bf16[512,128]{1,0:T(8,128)(2,1)S(1)}, bf16[512,128]{1,0:T(8,128)(2,1)S(1)}, u32[]{:S(2)}, u32[]{:S(2)}) collective-permute-start(bf16[512,128]{1,0:T(8,128)(2,1)S(1)} %get-tuple-element.25), channel_id=1, source_target_pairs={{0,16},{4,20},{8,24},{12,28},{16,0},{20,4},{24,8},{28,12},{1,17},{... | collective-permute-start | bytes 393224 | tf_op jit(solution)/shard_map/ppermute | solution.py:22
  5.2 1.6 %collective-permute-start.1 = (bf16[512,128]{1,0:T(8,128)(2,1)S(1)}, bf16[512,128]{1,0:T(8,128)(2,1)S(1)}, u32[]{:S(2)}, u32[]{:S(2)}) collective-permute-start(bf16[512,128]{1,0:T(8,128)(2,1)S(1)} %get-tuple-element.24), channel_id=1, source_target_pairs={{0,8},{4,12},{8,0},{12,4},{16,24},{20,28},{24,16},{28,20},{1,9},{5... | collective-permute-start | bytes 393224 | tf_op jit(solution)/shard_map/ppermute | solution.py:22
  6.7 4.8 %collective-permute-done.3.rest_4_ = bf16[512,128]{1,0:T(8,128)(2,1)S(1)} collective-permute-done((bf16[512,128]{1,0:T(8,128)(2,1)S(1)}, bf16[512,128]{1,0:T(8,128)(2,1)S(1)}, u32[]{:S(2)}, u32[]{:S(2)}) %collective-permute-start.3) | collective-permute-done | bytes 131104 | tf_op jit(solution)/shard_map/ppermute | solution.py:22
  11.6 0.6 %collective-permute-start.5 = (bf16[512,128]{1,0:T(8,128)(2,1)S(1)}, bf16[512,128]{1,0:T(8,128)(2,1)S(1)}, u32[]{:S(2)}, u32[]{:S(2)}) collective-permute-start(bf16[512,128]{1,0:T(8,128)(2,1)S(1)} %collective-permute-done.3.rest_4_), channel_id=1, source_target_pairs={{0,8},{4,12},{8,0},{12,4},{16,24},{20,28},{24,16},{28,20},{1,9},{5... | collective-permute-start | bytes 393224 | tf_op jit(solution)/shard_map/ppermute | solution.py:22
  12.2 1.5 %collective-permute-start.7 = (bf16[128,128]{1,0:T(8,128)(2,1)S(1)}, bf16[128,128]{1,0:T(8,128)(2,1)S(1)}, u32[]{:S(2)}, u32[]{:S(2)}) collective-permute-start(bf16[128,128]{1,0:T(8,128)(2,1)S(1)} %get-tuple-element.27), channel_id=1, source_target_pairs={{0,4},{4,0},{8,12},{12,8},{16,20},{20,16},{24,28},{28,24},{1,5},{5... | collective-permute-start | bytes 98312 | tf_op jit(solution)/shard_map/ppermute | solution.py:22
  13.7 1.5 %collective-permute-start.8 = (bf16[128,128]{1,0:T(8,128)(2,1)S(1)}, bf16[128,128]{1,0:T(8,128)(2,1)S(1)}, u32[]{:S(2)}, u32[]{:S(2)}) collective-permute-start(bf16[128,128]{1,0:T(8,128)(2,1)S(1)} %get-tuple-element.28), channel_id=1, source_target_pairs={{0,8},{4,12},{8,0},{12,4},{16,24},{20,28},{24,16},{28,20},{1,9},{5... | collective-permute-start | bytes 98312 | tf_op jit(solution)/shard_map/ppermute | solution.py:22
  15.1 0.5 collective-permute-start.9
  15.7 1.3 %table.1 = s32[1,10]{1,0:T(1,128)S(1)} custom-call(s32[1,4]{1,0:T(1,128)} %page_in.1, s32[1,3]{1,0:T(1,128)} %shift_in.1, s32[1,3]{1,0:T(1,128)} %bitcast.9), custom_call_target="tpu_custom_call" | custom-call | bytes 1048576 | tf_op jit(solution)/shard_map/table/pallas_call | solution.py:328
  17.0 0.0 collective-permute-done.7.rest_1_
  17.0 0.6 %collective-permute-done.8.rest_2_ = bf16[128,128]{1,0:T(8,128)(2,1)S(1)} collective-permute-done((bf16[128,128]{1,0:T(8,128)(2,1)S(1)}, bf16[128,128]{1,0:T(8,128)(2,1)S(1)}, u32[]{:S(2)}, u32[]{:S(2)}) %collective-permute-start.8) | collective-permute-done | bytes 32800 | tf_op jit(solution)/shard_map/ppermute | solution.py:22
  17.6 2.4 %collective-permute-done.9.rest_3_ = bf16[128,128]{1,0:T(8,128)(2,1)S(1)} collective-permute-done((bf16[128,128]{1,0:T(8,128)(2,1)S(1)}, bf16[128,128]{1,0:T(8,128)(2,1)S(1)}, u32[]{:S(2)}, u32[]{:S(2)}) %collective-permute-start.9) | collective-permute-done | bytes 32800 | tf_op jit(solution)/shard_map/ppermute | solution.py:22
  20.0 0.7 %pick.1.mine = bf16[256,128]{1,0:T(8,128)(2,1)S(1)} custom-call(s32[1,10]{1,0:T(1,128)S(1)} %table.1, bf16[128,128]{1,0:T(8,128)(2,1)S(1)} %get-tuple-element.26.rest_0_, bf16[128,128]{1,0:T(8,128)(2,1)S(1)} %collective-permute-done.7.rest_1_, bf16[128,128]{1,0:T(8,128)(2,1)S(1)} %collective-permute-done.8.rest_2_, ...), custom_call_target="tpu_custom_call" | custom-call | bytes 4194304 | tf_op jit(solution)/shard_map/pick/pallas_call | solution.py:365
  20.6 2.0 %collective-permute-start.10 = (bf16[256,128]{1,0:T(8,128)(2,1)S(1)}, bf16[256,128]{1,0:T(8,128)(2,1)S(1)}, u32[]{:S(2)}, u32[]{:S(2)}) collective-permute-start(bf16[256,128]{1,0:T(8,128)(2,1)S(1)} %pick.1.mine), channel_id=1, source_target_pairs={{0,16},{4,20},{8,24},{12,28},{16,0},{20,4},{24,8},{28,12},{1,17},{... | collective-permute-start | bytes 196616 | tf_op jit(solution)/shard_map/ppermute | solution.py:22
  22.6 0.9 %collective-permute-start = (bf16[512,128]{1,0:T(8,128)(2,1)S(1)}, bf16[512,128]{1,0:T(8,128)(2,1)S(1)}, u32[]{:S(2)}, u32[]{:S(2)}) collective-permute-start(bf16[512,128]{1,0:T(8,128)(2,1)S(1)} %get-tuple-element.23), channel_id=1, source_target_pairs={{0,4},{4,0},{8,12},{12,8},{16,20},{20,16},{24,28},{28,24},{1,5},{5... | collective-permute-start | bytes 393224 | tf_op jit(solution)/shard_map/ppermute | solution.py:22
  23.5 3.1 %collective-permute-done.10.other = bf16[256,128]{1,0:T(8,128)(2,1)S(1)} collective-permute-done((bf16[256,128]{1,0:T(8,128)(2,1)S(1)}, bf16[256,128]{1,0:T(8,128)(2,1)S(1)}, u32[]{:S(2)}, u32[]{:S(2)}) %collective-permute-start.10) | collective-permute-done | bytes 65568 | tf_op jit(solution)/shard_map/ppermute | solution.py:22
  26.6 0.6 %merge.1.rest_8_ = bf16[256,128]{1,0:T(8,128)(2,1)S(1)} custom-call(s32[1,10]{1,0:T(1,128)S(1)} %table.1, bf16[256,128]{1,0:T(8,128)(2,1)S(1)} %pick.1.mine, bf16[256,128]{1,0:T(8,128)(2,1)S(1)} %collective-permute-done.10.other), custom_call_target="tpu_custom_call" | custom-call | bytes 4194304 | tf_op jit(solution)/shard_map/merge/pallas_call | solution.py:373
  27.2 0.4 collective-permute-start.13
  27.6 1.5 %collective-permute-start.4 = (bf16[512,128]{1,0:T(8,128)(2,1)S(1)}, bf16[512,128]{1,0:T(8,128)(2,1)S(1)}, u32[]{:S(2)}, u32[]{:S(2)}) collective-permute-start(bf16[512,128]{1,0:T(8,128)(2,1)S(1)} %collective-permute-done.3.rest_4_), channel_id=1, source_target_pairs={{0,4},{4,0},{8,12},{12,8},{16,20},{20,16},{24,28},{28,24},{1,5},{5... | collective-permute-start | bytes 393224 | tf_op jit(solution)/shard_map/ppermute | solution.py:22
  29.1 0.0 collective-permute-done.1.rest_2_
  29.1 0.5 collective-permute-start.2
  29.6 0.0 collective-permute-done.5.rest_6_
  29.6 1.5 %collective-permute-start.6 = (bf16[512,128]{1,0:T(8,128)(2,1)S(1)}, bf16[512,128]{1,0:T(8,128)(2,1)S(1)}, u32[]{:S(2)}, u32[]{:S(2)}) collective-permute-start(bf16[512,128]{1,0:T(8,128)(2,1)S(1)} %collective-permute-done.5.rest_6_), channel_id=1, source_target_pairs={{0,4},{4,0},{8,12},{12,8},{16,20},{20,16},{24,28},{28,24},{1,5},{5... | collective-permute-start | bytes 393224 | tf_op jit(solution)/shard_map/ppermute | solution.py:22
  31.1 0.0 collective-permute-done.rest_1_
  31.1 1.7 %collective-permute-start.12 = (bf16[256,128]{1,0:T(8,128)(2,1)S(1)}, bf16[256,128]{1,0:T(8,128)(2,1)S(1)}, u32[]{:S(2)}, u32[]{:S(2)}) collective-permute-start(bf16[256,128]{1,0:T(8,128)(2,1)S(1)} %merge.1.rest_8_), channel_id=1, source_target_pairs={{0,8},{4,12},{8,0},{12,4},{16,24},{20,28},{24,16},{28,20},{1,9},{5... | collective-permute-start | bytes 196616 | tf_op jit(solution)/shard_map/ppermute | solution.py:22
  32.8 0.0 collective-permute-done.13.rest_11_
  32.8 0.4 collective-permute-start.11
  33.2 1.0 %stage.1.query_ref = bf16[256,1024]{1,0:T(8,128)(2,1)S(1)} custom-call(bf16[256,1024]{1,0:T(8,128)(2,1)} %query_in.1), custom_call_target="tpu_custom_call" | custom-call | bytes 2097152 | tf_op jit(solution)/shard_map/stage/pallas_call | solution.py:315
  34.3 1.1 %collective-permute-done.12.rest_10_ = bf16[256,128]{1,0:T(8,128)(2,1)S(1)} collective-permute-done((bf16[256,128]{1,0:T(8,128)(2,1)S(1)}, bf16[256,128]{1,0:T(8,128)(2,1)S(1)}, u32[]{:S(2)}, u32[]{:S(2)}) %collective-permute-start.12) | collective-permute-done | bytes 65568 | tf_op jit(solution)/shard_map/ppermute | solution.py:22
  35.4 3.4 %collective-permute-done.11.rest_9_ = bf16[256,128]{1,0:T(8,128)(2,1)S(1)} collective-permute-done((bf16[256,128]{1,0:T(8,128)(2,1)S(1)}, bf16[256,128]{1,0:T(8,128)(2,1)S(1)}, u32[]{:S(2)}, u32[]{:S(2)}) %collective-permute-start.11) | collective-permute-done | bytes 65568 | tf_op jit(solution)/shard_map/ppermute | solution.py:22
  38.8 0.0 collective-permute-done.2.rest_3_
  38.8 0.0 collective-permute-done.4.rest_5_
  38.8 0.0 collective-permute-done.6.rest_7_
  38.8 4.4 %first.1 = (bf16[2,128,512]{2,1,0:T(8,128)(2,1)S(1)}, f32[2,128,512]{2,1,0:T(8,128)S(1)}, bf16[1536,256]{1,0:T(8,128)(2,1)S(1)}, bf16[1536,256]{1,0:T(8,128)(2,1)S(1)}, bf16[1024,2048]{1,0:T(8,128)(2,1)S(1)}) custom-call(s32[1,10]{1,0:T(1,128)S(1)} %table.1, bf16[256,1024]{1,0:T(8,128)(2,1)S(1)} %stage.1.query_ref, bf16[1024,2048]{1,0:T(8,128)(2,1)} %proj_ref.1, ...), custom_call_target="tpu_custom_call" | custom-call | flops 1342177280 | bytes 8388608 | tf_op jit(solution)/shard_map/first/pallas_call | solution.py:414
  43.2 3.5 %second.1 = (bf16[2,128,512]{2,1,0:T(8,128)(2,1)S(1)}, f32[2,128,512]{2,1,0:T(8,128)S(1)}) custom-call(bf16[256,1024]{1,0:T(8,128)(2,1)S(1)} %stage.1.query_ref, bf16[1536,256]{1,0:T(8,128)(2,1)S(1)} %get-tuple-element.32.keys, bf16[1536,256]{1,0:T(8,128)(2,1)S(1)} %get-tuple-element.33.values, bf16[1024,2048]{1,0:T(8,128)(2,1)S(1)} %get-tuple-element.34.proj), custom_call_target="tpu_custom_call" | custom-call | flops 1342177280 | bytes 8388608 | tf_op jit(solution)/shard_map/second/pallas_call | solution.py:429
  46.7 0.1 collective-permute-start.16
  46.8 0.5 collective-permute-start.14
  47.3 1.0 %collective-permute-done.16 = bf16[2,128,512]{2,1,0:T(8,128)(2,1)S(1)} collective-permute-done((bf16[2,128,512]{2,1,0:T(8,128)(2,1)S(1)}, bf16[2,128,512]{2,1,0:T(8,128)(2,1)S(1)}, u32[]{:S(2)}, u32[]{:S(2)}) %collective-permute-start.16) | collective-permute-done | bytes 262176 | tf_op jit(solution)/shard_map/ppermute | solution.py:22
  48.3 0.1 convert_add_fusion
  48.4 1.6 %collective-permute-start.17 = (bf16[1,128,512]{2,1,0:T(8,128)(2,1)S(1)}, bf16[1,128,512]{2,1,0:T(8,128)(2,1)S(1)}, u32[]{:S(2)}, u32[]{:S(2)}) collective-permute-start(bf16[1,128,512]{2,1,0:T(8,128)(2,1)S(1)} %slice.38), channel_id=1, source_target_pairs={{0,2},{1,3},{2,0},{3,1},{4,6},{5,7},{6,4},{7,5},{8,10},{9,11},{10,... | collective-permute-start | bytes 393224 | tf_op jit(solution)/shard_map/ppermute | solution.py:22
  50.0 0.0 collective-permute-done.14
  50.0 0.1 convert_add_fusion.1
  50.1 0.6 collective-permute-start.15
  50.7 4.2 %collective-permute-done.17 = bf16[1,128,512]{2,1,0:T(8,128)(2,1)S(1)} collective-permute-done((bf16[1,128,512]{2,1,0:T(8,128)(2,1)S(1)}, bf16[1,128,512]{2,1,0:T(8,128)(2,1)S(1)}, u32[]{:S(2)}, u32[]{:S(2)}) %collective-permute-start.17) | collective-permute-done | bytes 131104 | tf_op jit(solution)/shard_map/ppermute | solution.py:22
  54.9 1.9 %collective-permute-done.15 = bf16[1,128,512]{2,1,0:T(8,128)(2,1)S(1)} collective-permute-done((bf16[1,128,512]{2,1,0:T(8,128)(2,1)S(1)}, bf16[1,128,512]{2,1,0:T(8,128)(2,1)S(1)}, u32[]{:S(2)}, u32[]{:S(2)}) %collective-permute-start.15) | collective-permute-done | bytes 131104 | tf_op jit(solution)/shard_map/ppermute | solution.py:22
  56.9 0.7 %pad_maximum_fusion = bf16[256,512]{1,0:T(8,128)(2,1)} fusion(bf16[128,512]{1,0:T(8,128)(2,1)S(1)} %fusion.3, bf16[128,512]{1,0:T(8,128)(2,1)S(1)} %fusion.2), kind=kLoop, calls=%fused_computation.8 | loop fusion | flops 524288 | bytes 524288 | tf_op jit(solution)/shard_map/concatenate | solution.py:449
  (4 shorter events, 0.1 us)
Async XLA Ops:
  1.0 10.5 %collective-permute-start.3 = (bf16[512,128]{1,0:T(8,128)(2,1)S(1)}, bf16[512,128]{1,0:T(8,128)(2,1)S(1)}, u32[]{:S(2)}, u32[]{:S(2)}) collective-permute-start(bf16[512,128]{1,0:T(8,128)(2,1)S(1)} %get-tuple-element.25), channel_id=1, source_target_pairs={{0,16},{4,20},{8,24},{12,28},{16,0},{20,4},{24,8},{28,12},{1,17},{... | collective-permute-start | bytes 393224 | tf_op jit(solution)/shard_map/ppermute | solution.py:22
  5.2 23.9 %collective-permute-start.1 = (bf16[512,128]{1,0:T(8,128)(2,1)S(1)}, bf16[512,128]{1,0:T(8,128)(2,1)S(1)}, u32[]{:S(2)}, u32[]{:S(2)}) collective-permute-start(bf16[512,128]{1,0:T(8,128)(2,1)S(1)} %get-tuple-element.24), channel_id=1, source_target_pairs={{0,8},{4,12},{8,0},{12,4},{16,24},{20,28},{24,16},{28,20},{1,9},{5... | collective-permute-start | bytes 393224 | tf_op jit(solution)/shard_map/ppermute | solution.py:22
  11.6 18.1 %collective-permute-start.5 = (bf16[512,128]{1,0:T(8,128)(2,1)S(1)}, bf16[512,128]{1,0:T(8,128)(2,1)S(1)}, u32[]{:S(2)}, u32[]{:S(2)}) collective-permute-start(bf16[512,128]{1,0:T(8,128)(2,1)S(1)} %collective-permute-done.3.rest_4_), channel_id=1, source_target_pairs={{0,8},{4,12},{8,0},{12,4},{16,24},{20,28},{24,16},{28,20},{1,9},{5... | collective-permute-start | bytes 393224 | tf_op jit(solution)/shard_map/ppermute | solution.py:22
  12.2 4.8 %collective-permute-start.7 = (bf16[128,128]{1,0:T(8,128)(2,1)S(1)}, bf16[128,128]{1,0:T(8,128)(2,1)S(1)}, u32[]{:S(2)}, u32[]{:S(2)}) collective-permute-start(bf16[128,128]{1,0:T(8,128)(2,1)S(1)} %get-tuple-element.27), channel_id=1, source_target_pairs={{0,4},{4,0},{8,12},{12,8},{16,20},{20,16},{24,28},{28,24},{1,5},{5... | collective-permute-start | bytes 98312 | tf_op jit(solution)/shard_map/ppermute | solution.py:22
  13.7 3.9 %collective-permute-start.8 = (bf16[128,128]{1,0:T(8,128)(2,1)S(1)}, bf16[128,128]{1,0:T(8,128)(2,1)S(1)}, u32[]{:S(2)}, u32[]{:S(2)}) collective-permute-start(bf16[128,128]{1,0:T(8,128)(2,1)S(1)} %get-tuple-element.28), channel_id=1, source_target_pairs={{0,8},{4,12},{8,0},{12,4},{16,24},{20,28},{24,16},{28,20},{1,9},{5... | collective-permute-start | bytes 98312 | tf_op jit(solution)/shard_map/ppermute | solution.py:22
  15.1 4.8 %collective-permute-start.9 = (bf16[128,128]{1,0:T(8,128)(2,1)S(1)}, bf16[128,128]{1,0:T(8,128)(2,1)S(1)}, u32[]{:S(2)}, u32[]{:S(2)}) collective-permute-start(bf16[128,128]{1,0:T(8,128)(2,1)S(1)} %get-tuple-element.29), channel_id=1, source_target_pairs={{0,12},{4,8},{8,4},{12,0},{16,28},{20,24},{24,20},{28,16},{1,13},{... | collective-permute-start | bytes 98312 | tf_op jit(solution)/shard_map/ppermute | solution.py:22
  20.6 6.0 %collective-permute-start.10 = (bf16[256,128]{1,0:T(8,128)(2,1)S(1)}, bf16[256,128]{1,0:T(8,128)(2,1)S(1)}, u32[]{:S(2)}, u32[]{:S(2)}) collective-permute-start(bf16[256,128]{1,0:T(8,128)(2,1)S(1)} %pick.1.mine), channel_id=1, source_target_pairs={{0,16},{4,20},{8,24},{12,28},{16,0},{20,4},{24,8},{28,12},{1,17},{... | collective-permute-start | bytes 196616 | tf_op jit(solution)/shard_map/ppermute | solution.py:22
  22.6 8.5 %collective-permute-start = (bf16[512,128]{1,0:T(8,128)(2,1)S(1)}, bf16[512,128]{1,0:T(8,128)(2,1)S(1)}, u32[]{:S(2)}, u32[]{:S(2)}) collective-permute-start(bf16[512,128]{1,0:T(8,128)(2,1)S(1)} %get-tuple-element.23), channel_id=1, source_target_pairs={{0,4},{4,0},{8,12},{12,8},{16,20},{20,16},{24,28},{28,24},{1,5},{5... | collective-permute-start | bytes 393224 | tf_op jit(solution)/shard_map/ppermute | solution.py:22
  27.2 5.6 %collective-permute-start.13 = (bf16[256,128]{1,0:T(8,128)(2,1)S(1)}, bf16[256,128]{1,0:T(8,128)(2,1)S(1)}, u32[]{:S(2)}, u32[]{:S(2)}) collective-permute-start(bf16[256,128]{1,0:T(8,128)(2,1)S(1)} %merge.1.rest_8_), channel_id=1, source_target_pairs={{0,12},{4,8},{8,4},{12,0},{16,28},{20,24},{24,20},{28,16},{1,13},{... | collective-permute-start | bytes 196616 | tf_op jit(solution)/shard_map/ppermute | solution.py:22
  27.6 11.2 %collective-permute-start.4 = (bf16[512,128]{1,0:T(8,128)(2,1)S(1)}, bf16[512,128]{1,0:T(8,128)(2,1)S(1)}, u32[]{:S(2)}, u32[]{:S(2)}) collective-permute-start(bf16[512,128]{1,0:T(8,128)(2,1)S(1)} %collective-permute-done.3.rest_4_), channel_id=1, source_target_pairs={{0,4},{4,0},{8,12},{12,8},{16,20},{20,16},{24,28},{28,24},{1,5},{5... | collective-permute-start | bytes 393224 | tf_op jit(solution)/shard_map/ppermute | solution.py:22
  29.1 9.7 %collective-permute-start.2 = (bf16[512,128]{1,0:T(8,128)(2,1)S(1)}, bf16[512,128]{1,0:T(8,128)(2,1)S(1)}, u32[]{:S(2)}, u32[]{:S(2)}) collective-permute-start(bf16[512,128]{1,0:T(8,128)(2,1)S(1)} %collective-permute-done.1.rest_2_), channel_id=1, source_target_pairs={{0,4},{4,0},{8,12},{12,8},{16,20},{20,16},{24,28},{28,24},{1,5},{5... | collective-permute-start | bytes 393224 | tf_op jit(solution)/shard_map/ppermute | solution.py:22
  29.6 9.2 %collective-permute-start.6 = (bf16[512,128]{1,0:T(8,128)(2,1)S(1)}, bf16[512,128]{1,0:T(8,128)(2,1)S(1)}, u32[]{:S(2)}, u32[]{:S(2)}) collective-permute-start(bf16[512,128]{1,0:T(8,128)(2,1)S(1)} %collective-permute-done.5.rest_6_), channel_id=1, source_target_pairs={{0,4},{4,0},{8,12},{12,8},{16,20},{20,16},{24,28},{28,24},{1,5},{5... | collective-permute-start | bytes 393224 | tf_op jit(solution)/shard_map/ppermute | solution.py:22
  31.1 4.3 %collective-permute-start.12 = (bf16[256,128]{1,0:T(8,128)(2,1)S(1)}, bf16[256,128]{1,0:T(8,128)(2,1)S(1)}, u32[]{:S(2)}, u32[]{:S(2)}) collective-permute-start(bf16[256,128]{1,0:T(8,128)(2,1)S(1)} %merge.1.rest_8_), channel_id=1, source_target_pairs={{0,8},{4,12},{8,0},{12,4},{16,24},{20,28},{24,16},{28,20},{1,9},{5... | collective-permute-start | bytes 196616 | tf_op jit(solution)/shard_map/ppermute | solution.py:22
  32.8 6.0 %collective-permute-start.11 = (bf16[256,128]{1,0:T(8,128)(2,1)S(1)}, bf16[256,128]{1,0:T(8,128)(2,1)S(1)}, u32[]{:S(2)}, u32[]{:S(2)}) collective-permute-start(bf16[256,128]{1,0:T(8,128)(2,1)S(1)} %merge.1.rest_8_), channel_id=1, source_target_pairs={{0,4},{4,0},{8,12},{12,8},{16,20},{20,16},{24,28},{28,24},{1,5},{5... | collective-permute-start | bytes 196616 | tf_op jit(solution)/shard_map/ppermute | solution.py:22
  46.7 1.6 %collective-permute-start.16 = (bf16[2,128,512]{2,1,0:T(8,128)(2,1)S(1)}, bf16[2,128,512]{2,1,0:T(8,128)(2,1)S(1)}, u32[]{:S(2)}, u32[]{:S(2)}) collective-permute-start(bf16[2,128,512]{2,1,0:T(8,128)(2,1)S(1)} %get-tuple-element.36), channel_id=1, source_target_pairs={{0,1},{1,0},{2,3},{3,2},{4,5},{5,4},{6,7},{7,6},{8,9},{9,8},{10,11... | collective-permute-start | bytes 786440 | tf_op jit(solution)/shard_map/ppermute | solution.py:22
  46.8 3.2 %collective-permute-start.14 = (bf16[2,128,512]{2,1,0:T(8,128)(2,1)S(1)}, bf16[2,128,512]{2,1,0:T(8,128)(2,1)S(1)}, u32[]{:S(2)}, u32[]{:S(2)}) collective-permute-start(bf16[2,128,512]{2,1,0:T(8,128)(2,1)S(1)} %get-tuple-element.31), channel_id=1, source_target_pairs={{0,1},{1,0},{2,3},{3,2},{4,5},{5,4},{6,7},{7,6},{8,9},{9,8},{10,11... | collective-permute-start | bytes 786440 | tf_op jit(solution)/shard_map/ppermute | solution.py:22
  48.4 6.4 %collective-permute-start.17 = (bf16[1,128,512]{2,1,0:T(8,128)(2,1)S(1)}, bf16[1,128,512]{2,1,0:T(8,128)(2,1)S(1)}, u32[]{:S(2)}, u32[]{:S(2)}) collective-permute-start(bf16[1,128,512]{2,1,0:T(8,128)(2,1)S(1)} %slice.38), channel_id=1, source_target_pairs={{0,2},{1,3},{2,0},{3,1},{4,6},{5,7},{6,4},{7,5},{8,10},{9,11},{10,... | collective-permute-start | bytes 393224 | tf_op jit(solution)/shard_map/ppermute | solution.py:22
  50.1 6.7 %collective-permute-start.15 = (bf16[1,128,512]{2,1,0:T(8,128)(2,1)S(1)}, bf16[1,128,512]{2,1,0:T(8,128)(2,1)S(1)}, u32[]{:S(2)}, u32[]{:S(2)}) collective-permute-start(bf16[1,128,512]{2,1,0:T(8,128)(2,1)S(1)} %slice.39), channel_id=1, source_target_pairs={{0,2},{1,3},{2,0},{3,1},{4,6},{5,7},{6,4},{7,5},{8,10},{9,11},{10,... | collective-permute-start | bytes 393224 | tf_op jit(solution)/shard_map/ppermute | solution.py:22
